TPU v7x, 32 devices: a whole 2x2x4 slice. The times are simulated.
32 devices in a mesh: gx: 4 (over z), gy: 4 (over y, x), gz: 2 (over core).
Axes of the slice: x: 2, y: 2, z: 4, core: 2. Of those that a mesh axis runs over, the one named last changes fastest.
Arguments:
- features: bfloat16 [4, 4, 2, 2048, 128], P('gx', 'gy', 'gz'), may hold values from -6 to 6
- positions: float32 [4, 4, 2, 3, 2048], P('gx', 'gy', 'gz'), may hold values from 0 to 1
- counts: int32 [4, 4, 2], P('gx', 'gy', 'gz'), may hold values from 1024 to 2048, as said below
- kvec: int32 [3, 1024], replicated, may hold values from -8 to 8, as said below
- sigma: float32 [128], replicated, may hold values from 0.0005 to 0.01
- w_mix: float32 [128, 128], replicated, may hold values from -0.5 to 0.5
- neighbours: int32 [4, 4, 2, 32, 2048], P('gx', 'gy', 'gz'), may hold values from 0 to 3583
- edge_weight: bfloat16 [4, 4, 2, 32, 2048], P('gx', 'gy', 'gz'), may hold values from 0.19921875 to 1
- send_list: int32 [4, 4, 2, 6, 256], P('gx', 'gy', 'gz'), may hold values from 0 to 2047
- w_message: bfloat16 [128, 128], replicated, may hold values from -0.5 to 0.5
Outputs:
- updated: bfloat16 [4, 4, 2, 2048, 128], P('gx', 'gy', 'gz')
- long_range: float32 [4, 4, 2, 2048, 128], P('gx', 'gy', 'gz')
Inputs may be any that keep to these rules, and one draw needn't show every extreme that they name: `kvec`: no k-vector is zero; some component reaches each end of the range. `counts`: some domain is full and some holds 1024 atoms.
All inputs are finite; a program needn't handle non-finite values.
Results may differ from a plain program's by a relative error of at most 0.0053.
Values may be sent and summed in bfloat16 or wider, within the bound.
No kernel may reach another device: no remote copies, remote signals or barrier semaphores. Data moves between devices by JAX's collectives and lax.ppermute only.
A program may use at most 64 MiB of HBM per device.

v0:
```python
import math

import jax
import jax.numpy as jnp
from jax import lax
from jax.sharding import PartitionSpec as P


def passed_along(value, axis, steps):
    count = lax.axis_size(axis)
    pairs = [(source, (source + steps) % count) for source in range(count)]
    return lax.ppermute(value, axis, pairs)


def phase_tables(frac_x, frac_y, frac_z, kvec_f):
    theta = (
        2.0
        * math.pi
        * (
            frac_x[:, None] * kvec_f[0][None, :]
            + frac_y[:, None] * kvec_f[1][None, :]
            + frac_z[:, None] * kvec_f[2][None, :]
        )
    )
    return (jnp.cos(theta).astype(jnp.bfloat16), jnp.sin(theta).astype(jnp.bfloat16))


def filter_rows(factor_rows, ksq_rows, sigma, w_mix):
    mixed = jnp.dot(factor_rows, w_mix, precision=lax.Precision.HIGHEST)
    return (mixed * jnp.exp(-sigma[None, :] * ksq_rows[:, None])).astype(jnp.bfloat16)


def pass_x(block, offset):
    return passed_along(block, "gx", offset)


def pass_y(block, offset):
    return passed_along(block, "gy", offset)


def pass_z(block, offset):
    return passed_along(block, "gz", offset)


def shards(
    features, positions, counts, kvec, sigma, w_mix, neighbours, edge_weight, send_list, w_message
):
    atoms = features.shape[3]
    width = features.shape[4]
    kcount = kvec.shape[1]
    slots = neighbours.shape[3]
    feats = features.reshape(atoms, width)
    alive = (jnp.arange(atoms, dtype=jnp.int32) < counts.reshape(())).astype(jnp.float32)
    own = jnp.where(alive[:, None] > 0.5, feats, jnp.zeros_like(feats))
    size_x = lax.axis_size("gx")
    size_y = lax.axis_size("gy")
    size_z = lax.axis_size("gz")
    devices = size_x * size_y * size_z
    index_x = lax.axis_index("gx")
    index_y = lax.axis_index("gy")
    index_z = lax.axis_index("gz")
    place = positions.reshape(3, atoms)
    frac_x = (index_x.astype(jnp.float32) + place[0]) / size_x
    frac_y = (index_y.astype(jnp.float32) + place[1]) / size_y
    frac_z = (index_z.astype(jnp.float32) + place[2]) / size_z
    kvec_f = kvec.astype(jnp.float32)
    kblock = min(256, kcount)
    send_flat = send_list.reshape(-1)
    atom_iota = jnp.arange(atoms, dtype=jnp.int32)
    selector = (send_flat[:, None] == atom_iota[None, :]).astype(jnp.bfloat16)
    outgoing = (
        jnp.dot(selector, own, preferred_element_type=jnp.float32)
        .astype(jnp.bfloat16)
        .reshape(6, -1, width)
    )
    incoming = [
        pass_x(outgoing[0], 1),
        pass_x(outgoing[1], -1),
        pass_y(outgoing[2], 1),
        pass_y(outgoing[3], -1),
        pass_z(outgoing[4], 1),
        pass_z(outgoing[5], -1),
    ]
    phase_blocks = []
    cos_parts = []
    sin_parts = []
    dims = (((0,), (0,)), ((), ()))
    for start in range(0, kcount, kblock):
        cosine, sine = phase_tables(frac_x, frac_y, frac_z, kvec_f[:, start : start + kblock])
        phase_blocks.append((cosine, sine))
        cos_parts.append(lax.dot_general(cosine, own, dims, preferred_element_type=jnp.float32))
        sin_parts.append(lax.dot_general(sine, own, dims, preferred_element_type=jnp.float32))
    sum_cos = jnp.concatenate(cos_parts, axis=0)
    sum_sin = jnp.concatenate(sin_parts, axis=0)
    scale = 1.0 / math.sqrt(atoms * devices)
    ksq = jnp.sum(kvec_f * kvec_f, axis=0)
    total_cos, total_sin = lax.psum((sum_cos, sum_sin), ("gx", "gy", "gz"))
    g_cos = filter_rows(total_cos * scale, ksq, sigma, w_mix)
    g_sin = filter_rows(total_sin * scale, ksq, sigma, w_mix)
    table = jnp.concatenate([own] + [piece for piece in incoming], axis=0)
    table_rows = table.shape[0]
    table_iota = jnp.arange(table_rows, dtype=jnp.int32)
    picks_all = neighbours.reshape(slots, atoms)
    weights_all = edge_weight.reshape(slots, atoms).astype(jnp.float32)
    ablock = min(512, atoms)

    def message_block(start):
        picks = lax.dynamic_slice_in_dim(picks_all, start, ablock, 1)
        weights = lax.dynamic_slice_in_dim(weights_all, start, ablock, 1)
        matched = picks[:, :, None] == table_iota[None, None, :]
        adjacency = jnp.sum(jnp.where(matched, weights[:, :, None], 0.0), axis=0)
        upper = adjacency.astype(jnp.bfloat16)
        lower = (adjacency - upper.astype(jnp.float32)).astype(jnp.bfloat16)
        summed = jnp.dot(upper, table, preferred_element_type=jnp.float32) + jnp.dot(
            lower, table, preferred_element_type=jnp.float32
        )
        return (summed / math.sqrt(slots)).astype(jnp.bfloat16)

    starts = jnp.arange(atoms // ablock, dtype=jnp.int32) * ablock
    message = lax.map(message_block, starts).reshape(atoms, width)
    hidden = jnp.dot(message, w_message, preferred_element_type=jnp.float32)
    upd = ((own.astype(jnp.float32) + jax.nn.silu(hidden)) * alive[:, None]).astype(jnp.bfloat16)
    back = jnp.zeros((atoms, width), jnp.float32)
    for number, start in enumerate(range(0, kcount, kblock)):
        cosine, sine = phase_blocks[number]
        back = back + jnp.dot(
            cosine, g_cos[start : start + kblock], preferred_element_type=jnp.float32
        )
        back = back + jnp.dot(
            sine, g_sin[start : start + kblock], preferred_element_type=jnp.float32
        )
    long_term = back * (2.0 / math.sqrt(kcount)) * alive[:, None]
    return (upd.reshape(1, 1, 1, atoms, width), long_term.reshape(1, 1, 1, atoms, width))


def solution(mesh):
    placed = (
        P("gx", "gy", "gz", None, None),
        P("gx", "gy", "gz", None, None),
        P("gx", "gy", "gz"),
        P(),
        P(),
        P(),
        P("gx", "gy", "gz", None, None),
        P("gx", "gy", "gz", None, None),
        P("gx", "gy", "gz", None, None),
        P(),
    )
    return jax.shard_map(
        shards,
        mesh=mesh,
        in_specs=placed,
        out_specs=(P("gx", "gy", "gz", None, None), P("gx", "gy", "gz", None, None)),
        check_vma=False,
    )
```

profile of v0, /device:TPU:0, one launch (start us, length us, event | category | flops | bytes accessed | tf_op | source)
XLA Modules:
  0.0 426.0 jit_solution(15445030284885510722)
XLA Ops:
  7.9 0.7 reduce
  8.6 3.5 fusion.25
  12.2 3.1 collective-permute-start
  15.3 2.1 collective-permute-start.1
  17.4 1.6 collective-permute-start.2
  19.0 1.5 collective-permute-start.3
  20.6 8.1 %fusion.30 = f32[256,128]{1,0:T(8,128)S(1)} fusion(f32[256]{0:T(256)S(1)} %bitcast.111, f32[256]{0:T(256)S(1)} %bitcast.115, f32[256]{0:T(256)S(1)} %bitcast.119, f32[2048]{0:T(1024)S(1)} %bitcast.79, f32[2048]{0:T(1024)S(1)} %bitcast.95, f32[2048]{0:T(1024)S(1)} %bitcast.63, bf16[1,1,1,2048,128]{4,3,2,1,0:T(8,128)(2,1)S(1)} %copy-done.2, ...), kind=kOutput, calls=%fused_computation.47 | convolution fusion | flops 138149888 | bytes 685056 | tf_op jit(solution)/shard_map/dot_general | solution.py:91
  28.7 8.6 %fusion.34 = f32[256,128]{1,0:T(8,128)S(1)} fusion(f32[256]{0:T(256)S(1)} %bitcast.112, f32[256]{0:T(256)S(1)} %bitcast.116, f32[256]{0:T(256)S(1)} %bitcast.120, f32[2048]{0:T(1024)S(1)} %bitcast.80, f32[2048]{0:T(1024)S(1)} %bitcast.96, f32[2048]{0:T(1024)S(1)} %bitcast.64, bf16[1,1,1,2048,128]{4,3,2,1,0:T(8,128)(2,1)S(1)} %copy-done.2, ...), kind=kOutput, calls=%fused_computation.51 | convolution fusion | flops 138149888 | bytes 685056 | tf_op jit(solution)/shard_map/dot_general | solution.py:92
  37.2 8.2 %fusion.29 = f32[256,128]{1,0:T(8,128)S(1)} fusion(f32[256]{0:T(256)S(1)} %bitcast.123, f32[256]{0:T(256)S(1)} %bitcast.127, f32[256]{0:T(256)S(1)} %bitcast.131, f32[2048]{0:T(1024)S(1)} %bitcast.81, f32[2048]{0:T(1024)S(1)} %bitcast.97, f32[2048]{0:T(1024)S(1)} %bitcast.65, bf16[1,1,1,2048,128]{4,3,2,1,0:T(8,128)(2,1)S(1)} %copy-done.2, ...), kind=kOutput, calls=%fused_computation.46 | convolution fusion | flops 138149888 | bytes 685056 | tf_op jit(solution)/shard_map/dot_general | solution.py:91
  45.5 8.2 %fusion.33 = f32[256,128]{1,0:T(8,128)S(1)} fusion(f32[256]{0:T(256)S(1)} %bitcast.124, f32[256]{0:T(256)S(1)} %bitcast.128, f32[256]{0:T(256)S(1)} %bitcast.132, f32[2048]{0:T(1024)S(1)} %bitcast.82, f32[2048]{0:T(1024)S(1)} %bitcast.98, f32[2048]{0:T(1024)S(1)} %bitcast.66, bf16[1,1,1,2048,128]{4,3,2,1,0:T(8,128)(2,1)S(1)} %copy-done.2, ...), kind=kOutput, calls=%fused_computation.50 | convolution fusion | flops 138149888 | bytes 685056 | tf_op jit(solution)/shard_map/dot_general | solution.py:92
  53.6 8.3 %fusion.28 = f32[256,128]{1,0:T(8,128)S(1)} fusion(f32[256]{0:T(256)S(1)} %bitcast.139, f32[256]{0:T(256)S(1)} %bitcast.143, f32[256]{0:T(256)S(1)} %bitcast.135, f32[2048]{0:T(1024)S(1)} %bitcast.83, f32[2048]{0:T(1024)S(1)} %bitcast.99, f32[2048]{0:T(1024)S(1)} %bitcast.67, bf16[1,1,1,2048,128]{4,3,2,1,0:T(8,128)(2,1)S(1)} %copy-done.2, ...), kind=kOutput, calls=%fused_computation.45 | convolution fusion | flops 138149888 | bytes 685056 | tf_op jit(solution)/shard_map/dot_general | solution.py:91
  61.9 8.6 %fusion.32 = f32[256,128]{1,0:T(8,128)S(1)} fusion(f32[256]{0:T(256)S(1)} %bitcast.140, f32[256]{0:T(256)S(1)} %bitcast.144, f32[256]{0:T(256)S(1)} %bitcast.136, f32[2048]{0:T(1024)S(1)} %bitcast.84, f32[2048]{0:T(1024)S(1)} %bitcast.100, f32[2048]{0:T(1024)S(1)} %bitcast.68, bf16[1,1,1,2048,128]{4,3,2,1,0:T(8,128)(2,1)S(1)} %copy-done.2, ...), kind=kOutput, calls=%fused_computation.49 | convolution fusion | flops 138149888 | bytes 685056 | tf_op jit(solution)/shard_map/dot_general | solution.py:92
  70.5 8.1 %fusion.36 = f32[256,128]{1,0:T(8,128)S(1)} fusion(f32[256]{0:T(256)S(1)} %bitcast.147, f32[2048]{0:T(1024)S(1)} %bitcast.85, f32[256]{0:T(256)S(1)} %bitcast.151, f32[2048]{0:T(1024)S(1)} %bitcast.101, f32[256]{0:T(256)S(1)} %bitcast.155, f32[2048]{0:T(1024)S(1)} %bitcast.69, bf16[1,1,1,2048,128]{4,3,2,1,0:T(8,128)(2,1)S(1)} %copy-done.2, ...), kind=kOutput, calls=%fused_computation.53 | convolution fusion | flops 138149888 | bytes 685056 | tf_op jit(solution)/shard_map/dot_general | solution.py:91
  78.6 8.3 %fusion.31 = f32[256,128]{1,0:T(8,128)S(1)} fusion(f32[256]{0:T(256)S(1)} %bitcast.148, f32[2048]{0:T(1024)S(1)} %bitcast.86, f32[256]{0:T(256)S(1)} %bitcast.152, f32[2048]{0:T(1024)S(1)} %bitcast.102, f32[256]{0:T(256)S(1)} %bitcast.156, f32[2048]{0:T(1024)S(1)} %bitcast.70, bf16[1,1,1,2048,128]{4,3,2,1,0:T(8,128)(2,1)S(1)} %copy-done.2, ...), kind=kOutput, calls=%fused_computation.48 | convolution fusion | flops 138149888 | bytes 685056 | tf_op jit(solution)/shard_map/dot_general | solution.py:92
  87.0 1.1 pad_maximum_fusion
  89.2 0.8 collective-permute-done.5
  90.0 261.4 %while.11 = (s32[]{:T(128)}, bf16[4,512,128]{2,1,0:T(8,128)(2,1)S(1)}, s32[4]{0:T(128)S(1)}, s32[32,2048]{1,0:T(8,128)}, f32[32,2048]{1,0:T(8,128)S(1)}, /*index...) while((s32[]{:T(128)}, bf16[4,512,128]{2,1,0:T(8,128)(2,1)S(1)}, ...), condition=%wide.region_2.3_spmd.clone, body=%wide.region_0.0_spmd.clone.sunk | while | flops 1123221504 | bytes 54263996 | solution.py:120
  90.0 0.6 dynamic_slice.20
  92.7 1.0 constant_dynamic-slice_fusion.5
  93.7 53.3 %select_reduce_fusion.2 = f32[512,3584]{1,0:T(8,128)} fusion(f32[32,512]{1,0:T(8,128)S(1)} %constant_dynamic-slice_fusion.4, s32[32,512]{1,0:T(8,128)S(1)} %constant_dynamic-slice_fusion.5), kind=kLoop, calls=%fused_computation.2.clone.1 | loop fusion | flops 174325760 | bytes 7471104 | tf_op jit(solution)/shard_map/while/body/eval_jaxpr/reduce_sum | solution.py:111
  146.9 6.5 %fusion.86 = f32[512,128]{1,0:T(8,128)S(1)} fusion(bf16[3584,128]{1,0:T(8,128)(2,1)S(1)} %get-tuple-element.151, f32[512,3584]{1,0:T(8,128)} %select_reduce_fusion.2), kind=kOutput, calls=%fused_computation.4.clone.1 | convolution fusion | flops 477102080 | bytes 8519680 | tf_op jit(solution)/shard_map/while/body/eval_jaxpr/dot_general | solution.py:114
  153.4 0.8 copy-done.1
  154.2 1.2 fusion.87
  158.1 1.0 constant_dynamic-slice_fusion.5
  159.0 53.3 %select_reduce_fusion.2 = f32[512,3584]{1,0:T(8,128)} fusion(f32[32,512]{1,0:T(8,128)S(1)} %constant_dynamic-slice_fusion.4, s32[32,512]{1,0:T(8,128)S(1)} %constant_dynamic-slice_fusion.5), kind=kLoop, calls=%fused_computation.2.clone.1 | loop fusion | flops 174325760 | bytes 7471104 | tf_op jit(solution)/shard_map/while/body/eval_jaxpr/reduce_sum | solution.py:111
  212.3 6.5 %fusion.86 = f32[512,128]{1,0:T(8,128)S(1)} fusion(bf16[3584,128]{1,0:T(8,128)(2,1)S(1)} %get-tuple-element.151, f32[512,3584]{1,0:T(8,128)} %select_reduce_fusion.2), kind=kOutput, calls=%fused_computation.4.clone.1 | convolution fusion | flops 477102080 | bytes 8519680 | tf_op jit(solution)/shard_map/while/body/eval_jaxpr/dot_general | solution.py:114
  218.8 0.8 copy-done.1
  219.6 1.2 fusion.87
  223.4 1.0 constant_dynamic-slice_fusion.5
  224.4 53.3 %select_reduce_fusion.2 = f32[512,3584]{1,0:T(8,128)} fusion(f32[32,512]{1,0:T(8,128)S(1)} %constant_dynamic-slice_fusion.4, s32[32,512]{1,0:T(8,128)S(1)} %constant_dynamic-slice_fusion.5), kind=kLoop, calls=%fused_computation.2.clone.1 | loop fusion | flops 174325760 | bytes 7471104 | tf_op jit(solution)/shard_map/while/body/eval_jaxpr/reduce_sum | solution.py:111
  277.7 6.4 %fusion.86 = f32[512,128]{1,0:T(8,128)S(1)} fusion(bf16[3584,128]{1,0:T(8,128)(2,1)S(1)} %get-tuple-element.151, f32[512,3584]{1,0:T(8,128)} %select_reduce_fusion.2), kind=kOutput, calls=%fused_computation.4.clone.1 | convolution fusion | flops 477102080 | bytes 8519680 | tf_op jit(solution)/shard_map/while/body/eval_jaxpr/dot_general | solution.py:114
  284.1 0.8 copy-done.1
  284.9 1.2 fusion.87
  288.8 0.9 constant_dynamic-slice_fusion.5
  289.7 53.3 %select_reduce_fusion.2 = f32[512,3584]{1,0:T(8,128)} fusion(f32[32,512]{1,0:T(8,128)S(1)} %constant_dynamic-slice_fusion.4, s32[32,512]{1,0:T(8,128)S(1)} %constant_dynamic-slice_fusion.5), kind=kLoop, calls=%fused_computation.2.clone.1 | loop fusion | flops 174325760 | bytes 7471104 | tf_op jit(solution)/shard_map/while/body/eval_jaxpr/reduce_sum | solution.py:111
  343.0 6.4 %fusion.86 = f32[512,128]{1,0:T(8,128)S(1)} fusion(bf16[3584,128]{1,0:T(8,128)(2,1)S(1)} %get-tuple-element.151, f32[512,3584]{1,0:T(8,128)} %select_reduce_fusion.2), kind=kOutput, calls=%fused_computation.4.clone.1 | convolution fusion | flops 477102080 | bytes 8519680 | tf_op jit(solution)/shard_map/while/body/eval_jaxpr/dot_general | solution.py:114
  349.4 0.8 copy-done.1
  350.3 1.2 fusion.87
  351.5 1.7 fusion.39
  353.2 1.6 fusion.26
  354.8 7.5 %fusion.35 = f32[2048,128]{1,0:T(8,128)S(1)} fusion(f32[256]{0:T(256)S(1)} %bitcast.149, f32[2048]{0:T(1024)S(1)} %bitcast.87, f32[256]{0:T(256)S(1)} %bitcast.153, f32[2048]{0:T(1024)S(1)} %bitcast.103, f32[256]{0:T(256)S(1)} %bitcast.157, f32[2048]{0:T(1024)S(1)} %bitcast.71, bf16[1024,128]{1,0:T(8,128)(2,1)S(1)} %fusion.26), kind=kOutput, calls=%fused_computation.52 | convolution fusion | flops 137887744 | bytes 1141760 | tf_op jit(solution)/shard_map/dot_general | solution.py:126
  362.9 8.0 %convolution_add_fusion.6 = f32[2048,128]{1,0:T(8,128)S(1)} fusion(f32[2048,128]{1,0:T(8,128)S(1)} %fusion.35, f32[256]{0:T(256)S(1)} %bitcast.150, f32[2048]{0:T(1024)S(1)} %bitcast.88, f32[256]{0:T(256)S(1)} %bitcast.154, f32[2048]{0:T(1024)S(1)} %bitcast.104, f32[256]{0:T(256)S(1)} %bitcast.158, f32[2048]{0:T(1024)S(1)} %bitcast.72, ...), kind=kOutput, calls=%fused_computation.26 | convolution fusion | flops 138149888 | bytes 2190336 | tf_op jit(solution)/shard_map/dot_general | solution.py:129
  371.0 7.7 %convolution_add_fusion.5 = f32[2048,128]{1,0:T(8,128)S(1)} fusion(f32[2048,128]{1,0:T(8,128)S(1)} %convolution_add_fusion.6, f32[256]{0:T(256)S(1)} %bitcast.141, f32[256]{0:T(256)S(1)} %bitcast.145, f32[256]{0:T(256)S(1)} %bitcast.137, f32[2048]{0:T(1024)S(1)} %bitcast.89, f32[2048]{0:T(1024)S(1)} %bitcast.105, f32[2048]{0:T(1024)S(1)} %bitcast.73, ...), kind=kOutput, calls=%fused_computation.25 | convolution fusion | flops 138149888 | bytes 2190336 | tf_op jit(solution)/shard_map/dot_general | solution.py:126
  378.7 7.6 %convolution_add_fusion.4 = f32[2048,128]{1,0:T(8,128)S(1)} fusion(f32[2048,128]{1,0:T(8,128)S(1)} %convolution_add_fusion.5, f32[256]{0:T(256)S(1)} %bitcast.142, f32[256]{0:T(256)S(1)} %bitcast.146, f32[256]{0:T(256)S(1)} %bitcast.138, f32[2048]{0:T(1024)S(1)} %bitcast.90, f32[2048]{0:T(1024)S(1)} %bitcast.106, f32[2048]{0:T(1024)S(1)} %bitcast.74, ...), kind=kOutput, calls=%fused_computation.24 | convolution fusion | flops 138149888 | bytes 2190336 | tf_op jit(solution)/shard_map/dot_general | solution.py:129
  386.3 7.8 %convolution_add_fusion.3 = f32[2048,128]{1,0:T(8,128)S(1)} fusion(f32[2048,128]{1,0:T(8,128)S(1)} %convolution_add_fusion.4, f32[256]{0:T(256)S(1)} %bitcast.125, f32[256]{0:T(256)S(1)} %bitcast.129, f32[256]{0:T(256)S(1)} %bitcast.133, f32[2048]{0:T(1024)S(1)} %bitcast.91, f32[2048]{0:T(1024)S(1)} %bitcast.107, f32[2048]{0:T(1024)S(1)} %bitcast.75, ...), kind=kOutput, calls=%fused_computation.23 | convolution fusion | flops 138149888 | bytes 2190336 | tf_op jit(solution)/shard_map/dot_general | solution.py:126
  394.1 7.9 %convolution_add_fusion.2 = f32[2048,128]{1,0:T(8,128)S(1)} fusion(f32[2048,128]{1,0:T(8,128)S(1)} %convolution_add_fusion.3, f32[256]{0:T(256)S(1)} %bitcast.126, f32[256]{0:T(256)S(1)} %bitcast.130, f32[256]{0:T(256)S(1)} %bitcast.134, f32[2048]{0:T(1024)S(1)} %bitcast.92, f32[2048]{0:T(1024)S(1)} %bitcast.108, f32[2048]{0:T(1024)S(1)} %bitcast.76, ...), kind=kOutput, calls=%fused_computation.22 | convolution fusion | flops 138149888 | bytes 2190336 | tf_op jit(solution)/shard_map/dot_general | solution.py:129
  402.0 7.6 %convolution_add_fusion.1 = f32[2048,128]{1,0:T(8,128)S(1)} fusion(f32[2048,128]{1,0:T(8,128)S(1)} %convolution_add_fusion.2, f32[256]{0:T(256)S(1)} %bitcast.113, f32[256]{0:T(256)S(1)} %bitcast.117, f32[256]{0:T(256)S(1)} %bitcast.121, f32[2048]{0:T(1024)S(1)} %bitcast.93, f32[2048]{0:T(1024)S(1)} %bitcast.109, f32[2048]{0:T(1024)S(1)} %bitcast.77, ...), kind=kOutput, calls=%fused_computation.21 | convolution fusion | flops 138149888 | bytes 2190336 | tf_op jit(solution)/shard_map/dot_general | solution.py:126
  409.6 9.2 %fusion.24 = f32[1,1,1,2048,128]{4,3,2,1,0:T(8,128)} fusion(f32[2048,128]{1,0:T(8,128)S(1)} %convolution_add_fusion.1, f32[256]{0:T(256)S(1)} %bitcast.114, f32[256]{0:T(256)S(1)} %bitcast.118, f32[256]{0:T(256)S(1)} %bitcast.122, f32[2048]{0:T(1024)S(1)} %bitcast.94, f32[2048]{0:T(1024)S(1)} %bitcast.110, f32[2048]{0:T(1024)S(1)} %bitcast.78, ...), kind=kOutput, calls=%fused_computation.20 | convolution fusion | flops 138412032 | bytes 2198528 | tf_op jit(solution)/shard_map/dot_general | solution.py:129
  (58 shorter events, 3.9 us)
Async XLA Ops:
  7.2 346.0 %copy-start = (f32[128,128]{1,0:T(8,128)S(1)}, f32[128,128]{1,0:T(8,128)}, u32[]{:S(2)}) copy-start(f32[128,128]{1,0:T(8,128)} %param.17) | copy-start | bytes 196612
  7.2 346.0 %all-reduce.3.cloned.1.call-start = ((), (), s32[]{:S(2)}) async-start(), calls=%async_computation | async-start | bytes 2097152 | tf_op jit(solution)/shard_map/psum | solution.py:97
  8.6 11.9 %copy-start.5 = (s32[3,1024]{1,0:T(4,128)S(1)}, s32[3,1024]{1,0:T(4,128)}, u32[]{:S(2)}) copy-start(s32[3,1024]{1,0:T(4,128)} %param.15) | copy-start | bytes 36868
  8.6 11.9 %copy-start.6 = (f32[1,1,1,3,2048]{4,2,3,1,0:T(1,128)S(1)}, f32[1,1,1,3,2048]{4,2,3,1,0:T(1,128)}, u32[]{:S(2)}) copy-start(f32[1,1,1,3,2048]{4,2,3,1,0:T(1,128)} %param.13) | copy-start | bytes 73732
  8.6 11.9 %copy-start.2 = (bf16[1,1,1,2048,128]{4,3,2,1,0:T(8,128)(2,1)S(1)}, bf16[1,1,1,2048,128]{4,3,2,1,0:T(8,128)(2,1)}, u32[]{:S(2)}) copy-start(bf16[1,1,1,2048,128]{4,3,2,1,0:T(8,128)(2,1)} %param.12) | copy-start | bytes 1572868
  12.2 76.3 %collective-permute-start = (bf16[256,128]{1,0:T(8,128)(2,1)S(1)}, bf16[256,128]{1,0:T(8,128)(2,1)S(1)}, u32[]{:S(2)}, u32[]{:S(2)}) collective-permute-start(bf16[256,128]{1,0:T(8,128)(2,1)S(1)} %get-tuple-element.73), channel_id=1, source_target_pairs={{0,8},{8,16},{16,24},{24,0},{1,9},{9,17},{17,25},{25,1},{2,10},{10... | collective-permute-start | bytes 196616 | tf_op jit(solution)/shard_map/ppermute | solution.py:12
  15.3 73.9 %collective-permute-start.1 = (bf16[256,128]{1,0:T(8,128)(2,1)S(1)}, bf16[256,128]{1,0:T(8,128)(2,1)S(1)}, u32[]{:S(2)}, u32[]{:S(2)}) collective-permute-start(bf16[256,128]{1,0:T(8,128)(2,1)S(1)} %get-tuple-element.72), channel_id=1, source_target_pairs={{0,24},{8,0},{16,8},{24,16},{1,25},{9,1},{17,9},{25,17},{2,26},{10... | collective-permute-start | bytes 196616 | tf_op jit(solution)/shard_map/ppermute | solution.py:12
  17.4 71.8 %collective-permute-start.2 = (bf16[256,128]{1,0:T(8,128)(2,1)S(1)}, bf16[256,128]{1,0:T(8,128)(2,1)S(1)}, u32[]{:S(2)}, u32[]{:S(2)}) collective-permute-start(bf16[256,128]{1,0:T(8,128)(2,1)S(1)} %get-tuple-element.71), channel_id=1, source_target_pairs={{0,2},{2,4},{4,6},{6,0},{1,3},{3,5},{5,7},{7,1},{8,10},{10,12},{12... | collective-permute-start | bytes 196616 | tf_op jit(solution)/shard_map/ppermute | solution.py:12
  19.0 70.2 %collective-permute-start.3 = (bf16[256,128]{1,0:T(8,128)(2,1)S(1)}, bf16[256,128]{1,0:T(8,128)(2,1)S(1)}, u32[]{:S(2)}, u32[]{:S(2)}) collective-permute-start(bf16[256,128]{1,0:T(8,128)(2,1)S(1)} %get-tuple-element.70), channel_id=1, source_target_pairs={{0,6},{2,0},{4,2},{6,4},{1,7},{3,1},{5,3},{7,5},{8,14},{10,8},{12,... | collective-permute-start | bytes 196616 | tf_op jit(solution)/shard_map/ppermute | solution.py:12
  20.5 68.7 %collective-permute-start.4 = (bf16[256,128]{1,0:T(8,128)(2,1)S(1)}, bf16[256,128]{1,0:T(8,128)(2,1)S(1)}, u32[]{:S(2)}, u32[]{:S(2)}) collective-permute-start(bf16[256,128]{1,0:T(8,128)(2,1)S(1)} %get-tuple-element.69), channel_id=1, source_target_pairs={{0,1},{1,0},{2,3},{3,2},{4,5},{5,4},{6,7},{7,6},{8,9},{9,8},{10,11... | collective-permute-start | bytes 196616 | tf_op jit(solution)/shard_map/ppermute | solution.py:12
  86.9 1.5 copy-start.4
  86.9 1.5 copy-start.8
  88.5 1.5 collective-permute-start.5
  90.0 261.5 %copy-start.7 = (bf16[128,128]{1,0:T(8,128)(2,1)S(1)}, bf16[128,128]{1,0:T(8,128)(2,1)}, u32[]{:S(2)}) copy-start(bf16[128,128]{1,0:T(8,128)(2,1)} %param.21) | copy-start | bytes 98308
  146.9 7.3 %copy-start.1 = (f32[512,3584]{1,0:T(8,128)S(1)}, f32[512,3584]{1,0:T(8,128)}, u32[]{:S(2)}) copy-start(f32[512,3584]{1,0:T(8,128)} %select_reduce_fusion.2) | copy-start | bytes 22020100 | tf_op jit(solution)/shard_map/while
  212.3 7.3 %copy-start.1 = (f32[512,3584]{1,0:T(8,128)S(1)}, f32[512,3584]{1,0:T(8,128)}, u32[]{:S(2)}) copy-start(f32[512,3584]{1,0:T(8,128)} %select_reduce_fusion.2) | copy-start | bytes 22020100 | tf_op jit(solution)/shard_map/while
  277.7 7.3 %copy-start.1 = (f32[512,3584]{1,0:T(8,128)S(1)}, f32[512,3584]{1,0:T(8,128)}, u32[]{:S(2)}) copy-start(f32[512,3584]{1,0:T(8,128)} %select_reduce_fusion.2) | copy-start | bytes 22020100 | tf_op jit(solution)/shard_map/while
  343.0 7.3 %copy-start.1 = (f32[512,3584]{1,0:T(8,128)S(1)}, f32[512,3584]{1,0:T(8,128)}, u32[]{:S(2)}) copy-start(f32[512,3584]{1,0:T(8,128)} %select_reduce_fusion.2) | copy-start | bytes 22020100 | tf_op jit(solution)/shard_map/while
  354.8 7.5 %copy-start.3 = (f32[1024,128]{1,0:T(8,128)S(1)}, f32[1024,128]{1,0:T(8,128)}, u32[]{:S(2)}) copy-start(f32[1024,128]{1,0:T(8,128)} %get-tuple-element.67) | copy-start | bytes 1572868
Sparse Core Ops, SparseCore 0:
  88.2 128.9 all-reduce.2
where the time goes:
time: 429 us; the launch traced here: 426 us
  other arithmetic  215 us (50%)
  matrix products  168 us (39%)
  between operations  15.5 us (4%)
  local copies, waits for them, and re-layouts  9.96 us (2%)
  starting transfers between devices  8.89 us (2%)
  loops' own time  7.91 us (2%)
    reduce_sum x4, other arithmetic, message_block(): adjacency = jnp.sum(jnp.where(matched, weights[:, :, None], 0.0), axis=0)  213 us
    dot_general x4, matrix products, shards(): lax.dot_general(sine, own, dims, preferred_element_type=jnp.float32)  33.6 us
    dot_general x4, matrix products, shards(): jnp.dot(sine, g_sin[start:start + kblock], preferred_element_type=jnp.flo...  32.7 us
    dot_general x4, matrix products, shards(): lax.dot_general(cosine, own, dims, preferred_element_type=jnp.float32)  32.7 us
    dot_general x4, matrix products, shards(): jnp.dot(cosine, g_cos[start:start + kblock], preferred_element_type=jnp.f...  30.6 us
    dot_general x4, matrix products, message_block(): jnp.dot(lower, table, preferred_element_type=jnp.float32)  25.8 us
    ppermute x6, starting transfers between devices, passed_along(): return lax.ppermute(value, axis, pairs)  8.85 us
  transfers between devices with their start and end apart: 7, of which 1 were waited for; matrix products, arithmetic and copies ran while one was open for 75% of the time, Pallas kernels for 0%

commit v1 on v0

v1 whole, which is shorter than its diff:
```python
import functools
import math

import jax
import jax.numpy as jnp
import numpy as np
from jax import lax
from jax.experimental import pallas as pl
from jax.experimental.pallas import tpu as pltpu
from jax.sharding import PartitionSpec as P

F32 = jnp.float32
BF16 = jnp.bfloat16
VMEM_LIMIT = 48 << 20


def half_turn_series():
    angle = np.cos((np.arange(400) + 0.5) * np.pi / 800)
    r = 0.5 * angle
    u = r * r
    root = math.sqrt(2.0)
    even = np.polynomial.chebyshev.Chebyshev.fit(u, root * np.cos(np.pi * r), 5, domain=[0, 0.25])
    odd = np.polynomial.chebyshev.Chebyshev.fit(u, root * np.sin(np.pi * r) / r, 4, domain=[0, 0.25])
    take = lambda fit: [float(v) for v in fit.convert(kind=np.polynomial.Polynomial).coef]
    return take(even), take(odd)


EVEN, ODD = half_turn_series()


def horner(coefs, u):
    total = coefs[-1] * u + coefs[-2]
    for coef in coefs[-3::-1]:
        total = total * u + coef
    return total


def phase_kernel(
    place_ref, count_ref, sizes, pos_ref, feat_ref, kvec_ref, table_ref, sums_ref, frac_ref, own_ref
):
    atoms, width = feat_ref.shape
    kblock = kvec_ref.shape[1]

    @pl.when(pl.program_id(0) == 0)
    def _():
        rows = []
        for axis in range(3):
            place = place_ref[axis].astype(F32)
            frac = (place + pos_ref[axis : axis + 1, :]) / sizes[axis]
            high = frac.astype(BF16).astype(F32)
            middle = (frac - high).astype(BF16).astype(F32)
            rows += [high, middle, frac - high - middle]
        stacked = jnp.concatenate(rows + [jnp.zeros((16 - len(rows), atoms), F32)], axis=0)
        frac_ref[...] = stacked.T.astype(BF16)
        atom = lax.broadcasted_iota(jnp.int32, (atoms, width), 0)
        own = jnp.where(atom < count_ref[0], feat_ref[...].astype(F32), 0.0)
        own_ref[...] = own.T.astype(BF16)

    kvec = kvec_ref[...].astype(F32)
    weights = jnp.concatenate(
        [kvec[axis : axis + 1, :] for axis in range(3) for _ in range(3)]
        + [jnp.zeros((7, kblock), F32)],
        axis=0,
    ).astype(BF16)
    chunk = min(256, atoms)

    def turn(number, carry):
        rows = pl.ds(pl.multiple_of(number * chunk, chunk), chunk)
        theta = jnp.dot(frac_ref[rows, :], weights, preferred_element_type=F32)
        r = theta - jnp.round(theta)
        u = r * r
        even = horner(EVEN, u)
        odd = horner(ODD, u) * r
        table_ref[rows, :kblock] = (1.0 - odd * odd).astype(BF16)
        table_ref[rows, kblock:] = (even * odd).astype(BF16)
        return carry

    lax.fori_loop(0, atoms // chunk, turn, 0)
    sums = jnp.dot(own_ref[...], table_ref[...], preferred_element_type=F32)
    sums_ref[...] = sums.T


def phases(place, count, sizes, pos, feats, kvec):
    atoms, width = feats.shape
    kcount = kvec.shape[1]
    kblock = 128
    whole = lambda *shape: pl.BlockSpec(shape, lambda b: (0,) * len(shape))
    smem = pl.BlockSpec(memory_space=pltpu.SMEM)

    def body(place_ref, count_ref, *refs):
        phase_kernel(place_ref, count_ref, sizes, *refs)

    return pl.pallas_call(
        body,
        grid=(kcount // kblock,),
        in_specs=[
            smem,
            smem,
            whole(3, atoms),
            whole(atoms, width),
            pl.BlockSpec((3, kblock), lambda b: (0, b)),
        ],
        out_specs=[
            pl.BlockSpec((atoms, 2 * kblock), lambda b: (0, b)),
            pl.BlockSpec((2 * kblock, width), lambda b: (b, 0)),
        ],
        out_shape=[
            jax.ShapeDtypeStruct((atoms, 2 * kcount), BF16),
            jax.ShapeDtypeStruct((2 * kcount, width), F32),
        ],
        scratch_shapes=[pltpu.VMEM((atoms, 16), BF16), pltpu.VMEM((width, atoms), BF16)],
        compiler_params=pltpu.CompilerParams(vmem_limit_bytes=VMEM_LIMIT),
        name="phases",
    )(place, count, pos, feats, kvec)


def message_kernel(
    low,
    count_ref,
    nbr_ref,
    weight_ref,
    feat_ref,
    *refs,
):
    halo_refs = refs[:6]
    wmsg_ref, out_ref, high_key, low_key, edge, table_ref, adj_ref, msg_ref = refs[6:]
    slots, atoms = nbr_ref.shape
    width = feat_ref.shape[1]
    lanes = 8 * slots
    groups = atoms // 8
    span = adj_ref.shape[0] // 8
    highs = table_ref.shape[0] // low
    step = pl.program_id(0)

    @pl.when(step == 0)
    def _():
        picks = jnp.concatenate([nbr_ref[:, i * groups : (i + 1) * groups] for i in range(8)], axis=0)
        picks = picks.astype(F32).T
        upper = jnp.floor(picks * (1.0 / low))
        lane = lax.broadcasted_iota(jnp.int32, (groups, lanes), 1)
        high_key[...] = upper * 8.0 + (lane // slots).astype(F32)
        low_key[...] = picks - upper * low
        edge[...] = jnp.concatenate(
            [weight_ref[:, i * groups : (i + 1) * groups].astype(F32) for i in range(8)], axis=0
        ).T
        atom = lax.broadcasted_iota(jnp.int32, (atoms, width), 0)
        table_ref[:atoms, :] = jnp.where(atom < count_ref[0], feat_ref[...].astype(F32), 0.0).astype(BF16)
        for face, halo in enumerate(halo_refs):
            rows = halo.shape[0]
            table_ref[atoms + face * rows : atoms + (face + 1) * rows, :] = halo[...]

    high_iota = lax.broadcasted_iota(jnp.int32, (highs * 8, lanes), 0).astype(F32).astype(BF16)
    low_iota = lax.broadcasted_iota(jnp.int32, (low, lanes), 0).astype(F32).astype(BF16)

    def group(number):
        row = pl.ds(number, 1)
        high = jnp.broadcast_to(high_key[row, :], (16, lanes)).astype(BF16)
        lower = jnp.broadcast_to(low_key[row, :], (16, lanes)).astype(BF16)
        value = jnp.broadcast_to(edge[row, :], (16, lanes)).astype(BF16)
        tile = lambda x, n: jnp.concatenate([x] * (n // 16), axis=0)
        zero = jnp.zeros((), BF16)
        left = jnp.where(tile(high, highs * 8) == high_iota, tile(value, highs * 8), zero)
        right = jnp.where(tile(lower, low) == low_iota, jnp.ones((), BF16), zero)
        return lax.dot_general(left, right, (((1,), (1,)), ((), ())), preferred_element_type=F32)

    def pair(number, carry):
        first = group(step * span + 2 * number)
        second = group(step * span + 2 * number + 1)
        rows = pl.ds(pl.multiple_of(number * 16, 16), 16)
        for upper in range(highs):
            here = slice(upper * 8, upper * 8 + 8)
            block = jnp.concatenate([first[here], second[here]], axis=0).astype(BF16)
            adj_ref[rows, upper * low : (upper + 1) * low] = block
        return carry

    lax.fori_loop(0, span // 2, pair, 0, unroll=2)
    summed = jnp.dot(adj_ref[...], table_ref[...], preferred_element_type=F32)
    message = (summed / math.sqrt(slots)).astype(BF16)
    hidden = jnp.dot(message, wmsg_ref[...], preferred_element_type=F32)
    msg_ref[...] = hidden / (1.0 + jnp.exp(-hidden))
    for i in range(8):
        start = pl.multiple_of(i * groups + step * span, span)
        own = table_ref[pl.ds(start, span), :].astype(F32)
        gate = msg_ref[pl.ds(i, span, stride=8), :]
        atom = lax.broadcasted_iota(jnp.int32, (span, width), 0) + start
        out_ref[i] = jnp.where(atom < count_ref[0], own + gate, 0.0).astype(BF16)


def messages(count, nbr, weights, feats, halos, wmsg):
    slots, atoms = nbr.shape
    width = feats.shape[1]
    groups = atoms // 8
    rows = atoms + sum(halo.shape[0] for halo in halos)
    low = 256
    span = min(32, groups)
    whole = lambda *shape: pl.BlockSpec(shape, lambda b: (0,) * len(shape))
    out = pl.pallas_call(
        functools.partial(message_kernel, low),
        grid=(groups // span,),
        in_specs=[
            pl.BlockSpec(memory_space=pltpu.SMEM),
            whole(slots, atoms),
            whole(slots, atoms),
            whole(atoms, width),
            *[whole(*halo.shape) for halo in halos],
            whole(width, width),
        ],
        out_specs=pl.BlockSpec((8, span, width), lambda b: (0, b, 0)),
        out_shape=jax.ShapeDtypeStruct((8, groups, width), BF16),
        scratch_shapes=[
            pltpu.VMEM((groups, 8 * slots), F32),
            pltpu.VMEM((groups, 8 * slots), F32),
            pltpu.VMEM((groups, 8 * slots), F32),
            pltpu.VMEM((rows, width), BF16),
            pltpu.VMEM((8 * span, rows), BF16),
            pltpu.VMEM((8 * span, width), F32),
        ],
        compiler_params=pltpu.CompilerParams(vmem_limit_bytes=VMEM_LIMIT),
        name="messages",
    )(count, nbr, weights, feats, *halos, wmsg)
    return out.reshape(atoms, width)


def back_kernel(scale, count_ref, table_ref, g_ref, out_ref):
    rows, width = out_ref.shape
    back = jnp.dot(table_ref[...], g_ref[...], preferred_element_type=F32)
    atom = lax.broadcasted_iota(jnp.int32, (rows, width), 0) + pl.program_id(0) * rows
    out_ref[...] = jnp.where(atom < count_ref[0], back * scale, 0.0)


def back(count, table, g, scale):
    atoms, depth = table.shape
    width = g.shape[1]
    block = min(512, atoms)
    return pl.pallas_call(
        functools.partial(back_kernel, scale),
        grid=(atoms // block,),
        in_specs=[
            pl.BlockSpec(memory_space=pltpu.SMEM),
            pl.BlockSpec((block, depth), lambda b: (b, 0)),
            pl.BlockSpec((depth, width), lambda b: (0, 0)),
        ],
        out_specs=pl.BlockSpec((block, width), lambda b: (b, 0)),
        out_shape=jax.ShapeDtypeStruct((atoms, width), F32),
        compiler_params=pltpu.CompilerParams(vmem_limit_bytes=VMEM_LIMIT),
        name="back",
    )(count, table, g)


def passed_along(value, axis, steps):
    size = lax.axis_size(axis)
    pairs = [(source, (source + steps) % size) for source in range(size)]
    return lax.ppermute(value, axis, pairs)


def filtered(sums, ksq, sigma, w_mix):
    mixed = jnp.dot(sums, w_mix, precision=lax.Precision.HIGHEST)
    return (mixed * jnp.exp(-sigma[None, :] * ksq[:, None])).astype(BF16)


def reduced_and_filtered(sums, ksq, sigma, w_mix, scale):
    size_z = lax.axis_size("gz")
    plane = lax.axis_size("gx") * lax.axis_size("gy")
    rows, width = sums.shape
    part = rows // (size_z * plane)
    here_z = lax.axis_index("gz")
    here_xy = lax.axis_index("gx") * lax.axis_size("gy") + lax.axis_index("gy")
    sums = lax.all_to_all(sums, "gz", 0, 0, tiled=True)
    sums = jnp.sum(sums.reshape(size_z, rows // size_z, width), axis=0)
    sums = lax.all_to_all(sums, ("gx", "gy"), 0, 0, tiled=True)
    sums = jnp.sum(sums.reshape(plane, part, width), axis=0)
    mine = lax.dynamic_slice_in_dim(ksq, (here_z * plane + here_xy) * part, part)
    g = filtered(sums * scale, mine, sigma, w_mix)
    g = jnp.broadcast_to(g[None], (plane, part, width))
    g = lax.all_to_all(g, ("gx", "gy"), 0, 0, tiled=True).reshape(plane * part, width)
    g = jnp.broadcast_to(g[None], (size_z, plane * part, width))
    return lax.all_to_all(g, "gz", 0, 0, tiled=True).reshape(rows, width)


def shards(
    features, positions, counts, kvec, sigma, w_mix, neighbours, edge_weight, send_list, w_message
):
    atoms = features.shape[3]
    width = features.shape[4]
    kcount = kvec.shape[1]
    slots = neighbours.shape[3]
    feats = features.reshape(atoms, width)
    count = counts.reshape(1)
    sizes = [lax.axis_size(axis) for axis in ("gx", "gy", "gz")]
    devices = sizes[0] * sizes[1] * sizes[2]
    place = jnp.stack([lax.axis_index(axis) for axis in ("gx", "gy", "gz")]).astype(jnp.int32)

    alive = jnp.arange(atoms, dtype=jnp.int32) < count[0]
    own = jnp.where(alive[:, None], feats, jnp.zeros_like(feats))
    selector = (
        send_list.reshape(-1)[:, None] == jnp.arange(atoms, dtype=jnp.int32)[None, :]
    ).astype(BF16)
    outgoing = jnp.dot(selector, own, preferred_element_type=F32).astype(BF16)
    outgoing = outgoing.reshape(6, -1, width)
    halos = [
        passed_along(outgoing[2 * number + side], axis, 1 - 2 * side)
        for number, axis in enumerate(("gx", "gy", "gz"))
        for side in range(2)
    ]

    table, sums = phases(place, count, sizes, positions.reshape(3, atoms), feats, kvec)
    kvec_f = kvec.astype(F32)
    ksq = jnp.sum(kvec_f * kvec_f, axis=0).reshape(-1, 1, 128)
    ksq = jnp.broadcast_to(ksq, (kcount // 128, 2, 128)).reshape(2 * kcount)
    g = reduced_and_filtered(sums, ksq, sigma, w_mix, 1.0 / math.sqrt(atoms * devices))
    updated = messages(
        count, neighbours.reshape(slots, atoms), edge_weight.reshape(slots, atoms), feats, halos, w_message
    )
    long_range = back(count, table, g, 2.0 / math.sqrt(kcount))
    return (updated.reshape(1, 1, 1, atoms, width), long_range.reshape(1, 1, 1, atoms, width))


def solution(mesh):
    split = P("gx", "gy", "gz", None, None)
    placed = (split, split, P("gx", "gy", "gz"), P(), P(), P(), split, split, split, P())
    return jax.shard_map(
        shards, mesh=mesh, in_specs=placed, out_specs=(split, split), check_vma=False
    )
```

time: 429 us -> 111 us (0.26)
  other arithmetic: 215 us -> 3.12 us
  matrix products: 168 us -> 3.63 us
  Pallas kernels: 0 us -> 54.3 us
  waiting for transfers between devices: 0.82 us -> 16.1 us
  between operations: 15.5 us -> 1.46 us
  starting transfers between devices: 8.89 us -> 19.6 us
  blocking collectives: 0 us -> 8.72 us
  loops' own time: 7.91 us -> 0 us
  local copies, waits for them, and re-layouts: 9.96 us -> 3.44 us
    reduce_sum x5 -> x3, other arithmetic: 213 us -> 1.66 us  [the longest x1 0.89 us: reduced_and_filtered(): sums = jnp.sum(sums.reshape(size_z, rows // size_z, width), axis=0)]
    dot_general x28 -> x2, matrix products: 168 us -> 3.63 us  [the longest x1 3.44 us: shards(): outgoing = jnp.dot(selector, own, preferred_element_type=F32).astype(BF16)]
    pallas_call x0 -> x3, Pallas kernels: none -> 54.3 us  [the longest x1 27.2 us: messages(): pl.pallas_call(functools.partial(message_kernel, low), grid=(groups // sp...]
    all_to_all x0 -> x2, waiting for transfers between devices: none -> 13.2 us  [the longest x1 13.2 us: reduced_and_filtered(): sums = lax.all_to_all(sums, ('gx', 'gy'), 0, 0, tiled=True)]
    all_to_all x0 -> x2, starting transfers between devices: none -> 12.2 us  [the longest x1 8.31 us: reduced_and_filtered(): sums = lax.all_to_all(sums, ('gx', 'gy'), 0, 0, tiled=True)]
    all_to_all x0 -> x2, blocking collectives: none -> 8.72 us  [the longest x1 4.56 us: reduced_and_filtered(): sums = lax.all_to_all(sums, 'gz', 0, 0, tiled=True)]
    another operation x1 -> x0, loops' own time: 7.91 us -> none  [shards(): message = lax.map(message_block, starts).reshape(atoms, width)]
    dynamic_slice x12 -> x1, local copies, waits for them, and re-layouts: 6.54 us -> 0.08 us  [reduced_and_filtered(): lax.dynamic_slice_in_dim(ksq, (here_z * plane + here_xy) * part, part)]
  transfers between devices with their start and end apart: 7 -> 8, of which waited for: 1 -> 3; matrix products, arithmetic and copies ran while one was open for 75% -> 5% of each run, Pallas kernels for 0% -> 25%
where the time goes in v1:
time: 111 us; the launch traced here: 110 us
  Pallas kernels  54.3 us (49%)
  starting transfers between devices  19.6 us (18%)
  waiting for transfers between devices  16.1 us (15%)
  blocking collectives  8.72 us (8%)
  matrix products  3.63 us (3%)
  local copies, waits for them, and re-layouts  3.44 us (3%)
  other arithmetic  3.12 us (3%)
  between operations  1.46 us (1%)
    pallas_call x1, Pallas kernels, messages(): pl.pallas_call(functools.partial(message_kernel, low), grid=(groups // sp...  27.2 us
    pallas_call x1, Pallas kernels, phases(): pl.pallas_call(body, grid=(kcount // kblock,), in_specs=[smem, smem, whol...  20.8 us
    all_to_all x1, waiting for transfers between devices, reduced_and_filtered(): sums = lax.all_to_all(sums, ('gx', 'gy'), 0, 0, tiled=True)  13.2 us
    all_to_all x1, starting transfers between devices, reduced_and_filtered(): sums = lax.all_to_all(sums, ('gx', 'gy'), 0, 0, tiled=True)  8.31 us
    ppermute x6, starting transfers between devices, passed_along(): return lax.ppermute(value, axis, pairs)  7.31 us
    pallas_call x1, Pallas kernels, back(): pl.pallas_call(functools.partial(back_kernel, scale), grid=(atoms // bloc...  6.29 us
    all_to_all x1, blocking collectives, reduced_and_filtered(): sums = lax.all_to_all(sums, 'gz', 0, 0, tiled=True)  4.56 us
    all_to_all x1, blocking collectives, reduced_and_filtered(): return lax.all_to_all(g, 'gz', 0, 0, tiled=True).reshape(rows, width)  4.15 us
  transfers between devices with their start and end apart: 8, of which 3 were waited for; matrix products, arithmetic and copies ran while one was open for 5% of the time, Pallas kernels for 25%

profile of v1, /device:TPU:0, one launch (start us, length us, event | category | flops | bytes accessed | tf_op | source)
XLA Modules:
  0.0 110.3 jit_solution(5183084296583195139)
XLA Ops:
  0.6 0.0 copy-start
  0.6 0.0 copy-start.6
  1.3 0.8 copy.14
  2.1 0.1 pad_add_fusion.place_ref
  2.2 0.0 copy-start.1
  2.2 1.0 copy-done.1
  3.2 0.0 copy-start.5
  3.2 0.7 copy-done.5
  3.9 0.0 copy-start.2
  3.9 0.0 copy-start.3
  3.9 0.0 copy-start.4
  3.9 20.8 %phases.1 = (bf16[2048,2048]{1,0:T(8,128)(2,1)}, f32[2048,128]{1,0:T(8,128)S(1)}) custom-call(s32[3]{0:T(128)S(1)} %pad_add_fusion.place_ref, s32[1]{0:T(128)} %bitcast.25.count_ref, f32[3,2048]{1,0:T(4,128)S(1)} %bitcast.34, bf16[2048,128]{1,0:T(8,128)(2,1)S(1)} %bitcast.29, s32[3,1024]{1,0:T(4,128)S(1)} %copy-done.5), custom_call_target="tpu_custom_call" | custom-call | tf_op jit(solution)/shard_map/phases/pallas_call | solution.py:93
  24.8 4.6 %all_to_all.28 = f32[2,1024,128]{2,1,0:T(8,128)S(1)} all-to-all(f32[2,1024,128]{2,1,0:T(8,128)S(1)} %bitcast.31), channel_id=1, replica_groups=mesh['gx'=4,'gy'=4,'gz'=2] {'gz'}, dimensions={0} | all-to-all | bytes 2097152 | tf_op jit(solution)/shard_map/all_to_all | solution.py:268
  29.3 0.9 reduce_sum.27
  30.2 8.3 %all-to-all-start.1 = ((f32[16,64,128]{2,1,0:T(8,128)}), f32[16,64,128]{2,1,0:T(8,128)S(1)}, u32[]{:S(2)}, u32[]{:S(2)}) async-start(f32[16,64,128]{2,1,0:T(8,128)} %bitcast.10), calls=%async_computation.1 | async-start | bytes 1048576 | tf_op jit(solution)/shard_map/all_to_all | solution.py:270
  38.5 0.7 neg.4
  39.2 0.7 reduce.2
  39.9 0.7 multiply_reduce_fusion
  40.7 0.1 dynamic_slice.3
  40.8 13.2 %all-to-all-done.1 = f32[16,64,128]{2,1,0:T(8,128)S(1)} async-done(((f32[16,64,128]{2,1,0:T(8,128)}), f32[16,64,128]{2,1,0:T(8,128)S(1)}, u32[]{:S(2)}, u32[]{:S(2)}) %all-to-all-start.1) | async-done | bytes 524320 | tf_op jit(solution)/shard_map/all_to_all | solution.py:270
  54.0 0.0 copy-done
  54.0 0.2 fusion.3
  54.2 0.8 broadcast_in_dim.39
  54.9 3.9 %all-to-all-start.2 = ((bf16[16,64,128]{2,1,0:T(8,128)(2,1)}), bf16[16,64,128]{2,1,0:T(8,128)(2,1)S(1)}, u32[]{:S(2)}, u32[]{:S(2)}) async-start(bf16[16,64,128]{2,1,0:T(8,128)(2,1)} %broadcast_in_dim.39), calls=%async_computation.2 | async-start | bytes 524288 | tf_op jit(solution)/shard_map/all_to_all | solution.py:275
  58.9 3.4 %fusion.2 = bf16[1536,128]{1,0:T(8,128)(2,1)S(1)} fusion(s32[1536]{0:T(1024)S(1)} %eq.15, pred[2048]{0:T(1024)(128)(4,1)S(1)} %iota_compare_fusion.4, bf16[1,1,1,2048,128]{4,3,2,1,0:T(8,128)(2,1)} %param.10), kind=kOutput, calls=%fused_computation.3 | convolution fusion | flops 808910848 | bytes 925696 | tf_op jit(solution)/shard_map/dot_general | solution.py:298
  62.3 2.0 %collective-permute-start = (bf16[256,128]{1,0:T(8,128)(2,1)S(1)}, bf16[256,128]{1,0:T(8,128)(2,1)S(1)}, u32[]{:S(2)}, u32[]{:S(2)}) collective-permute-start(bf16[256,128]{1,0:T(8,128)(2,1)S(1)} %get-tuple-element.11), channel_id=1, source_target_pairs={{0,8},{8,16},{16,24},{24,0},{1,9},{9,17},{17,25},{25,1},{2,10},{10... | collective-permute-start | bytes 196616 | tf_op jit(solution)/shard_map/ppermute | solution.py:253
  64.3 1.9 %collective-permute-start.1 = (bf16[256,128]{1,0:T(8,128)(2,1)S(1)}, bf16[256,128]{1,0:T(8,128)(2,1)S(1)}, u32[]{:S(2)}, u32[]{:S(2)}) collective-permute-start(bf16[256,128]{1,0:T(8,128)(2,1)S(1)} %get-tuple-element.10), channel_id=1, source_target_pairs={{0,24},{8,0},{16,8},{24,16},{1,25},{9,1},{17,9},{25,17},{2,26},{10... | collective-permute-start | bytes 196616 | tf_op jit(solution)/shard_map/ppermute | solution.py:253
  66.2 1.9 %collective-permute-start.2 = (bf16[256,128]{1,0:T(8,128)(2,1)S(1)}, bf16[256,128]{1,0:T(8,128)(2,1)S(1)}, u32[]{:S(2)}, u32[]{:S(2)}) collective-permute-start(bf16[256,128]{1,0:T(8,128)(2,1)S(1)} %get-tuple-element.9), channel_id=1, source_target_pairs={{0,2},{2,4},{4,6},{6,0},{1,3},{3,5},{5,7},{7,1},{8,10},{10,12},{12... | collective-permute-start | bytes 196616 | tf_op jit(solution)/shard_map/ppermute | solution.py:253
  68.1 1.0 collective-permute-start.3
  69.1 0.0 collective-permute-start.4
  69.2 0.0 collective-permute-done.refs_0_
  69.2 0.5 collective-permute-start.5
  69.7 0.0 collective-permute-done.1.refs_1_
  69.7 1.7 %collective-permute-done.2.refs_2_ = bf16[256,128]{1,0:T(8,128)(2,1)S(1)} collective-permute-done((bf16[256,128]{1,0:T(8,128)(2,1)S(1)}, bf16[256,128]{1,0:T(8,128)(2,1)S(1)}, u32[]{:S(2)}, u32[]{:S(2)}) %collective-permute-start.2) | collective-permute-done | bytes 65568 | tf_op jit(solution)/shard_map/ppermute | solution.py:253
  71.4 1.2 %collective-permute-done.3.refs_3_ = bf16[256,128]{1,0:T(8,128)(2,1)S(1)} collective-permute-done((bf16[256,128]{1,0:T(8,128)(2,1)S(1)}, bf16[256,128]{1,0:T(8,128)(2,1)S(1)}, u32[]{:S(2)}, u32[]{:S(2)}) %collective-permute-start.3) | collective-permute-done | bytes 65568 | tf_op jit(solution)/shard_map/ppermute | solution.py:253
  72.6 0.0 collective-permute-done.4.refs_4_
  72.6 0.0 collective-permute-done.5.refs_5_
  72.6 0.0 copy-done.6
  72.6 0.0 copy-done.2
  72.6 0.0 copy-done.3
  72.6 0.0 copy-done.4
  72.6 27.2 %messages.1 = bf16[8,256,128]{2,1,0:T(8,128)(2,1)} custom-call(s32[1]{0:T(128)} %bitcast.24.count_ref, s32[32,2048]{1,0:T(8,128)S(1)} %bitcast.32, bf16[32,2048]{1,0:T(8,128)(2,1)S(1)} %bitcast.33, bf16[2048,128]{1,0:T(8,128)(2,1)S(1)} %bitcast.30, bf16[256,128]{1,0:T(8,128)(2,1)S(1)} %collective-permute-done.refs_0_, ...), custom_call_target="tpu_custom_call" | custom-call | tf_op jit(solution)/shard_map/messages/pallas_call | solution.py:197
  99.8 0.0 all-to-all-done.2
  99.9 4.2 %all_to_all.29 = bf16[2,1024,128]{2,1,0:T(8,128)(2,1)S(1)} all-to-all(bf16[2,1024,128]{2,1,0:T(8,128)(2,1)S(1)} %broadcast_in_dim.41), channel_id=1, replica_groups=mesh['gx'=4,'gy'=4,'gz'=2] {'gz'}, dimensions={0} | all-to-all | bytes 1048576 | tf_op jit(solution)/shard_map/all_to_all | solution.py:277
  104.0 6.3 %back.1 = f32[2048,128]{1,0:T(8,128)} custom-call(s32[1]{0:T(128)} %bitcast.26.count_ref, bf16[2048,2048]{1,0:T(8,128)(2,1)} %get-tuple-element.4.table_ref, bf16[2048,128]{1,0:T(8,128)(2,1)S(1)} %bitcast.28), custom_call_target="tpu_custom_call" | custom-call | tf_op jit(solution)/shard_map/back/pallas_call | solution.py:235
  (6 shorter events, 0.1 us)
Async XLA Ops:
  0.6 53.3 %copy-start = (f32[128,128]{1,0:T(8,128)S(1)}, f32[128,128]{1,0:T(8,128)}, u32[]{:S(2)}) copy-start(f32[128,128]{1,0:T(8,128)} %param.15) | copy-start | bytes 196612
  0.6 71.9 %copy-start.6 = (bf16[128,128]{1,0:T(8,128)(2,1)S(1)}, bf16[128,128]{1,0:T(8,128)(2,1)}, u32[]{:S(2)}) copy-start(bf16[128,128]{1,0:T(8,128)(2,1)} %refs_6_.1) | copy-start | bytes 98308
  2.2 1.0 copy-start.1
  3.2 0.7 copy-start.5
  3.9 68.6 %copy-start.2 = (bf16[1,1,1,2048,128]{4,3,2,1,0:T(8,128)(2,1)S(1)}, bf16[1,1,1,2048,128]{4,3,2,1,0:T(8,128)(2,1)}, u32[]{:S(2)}) copy-start(bf16[1,1,1,2048,128]{4,3,2,1,0:T(8,128)(2,1)} %param.10) | copy-start | bytes 1572868
  3.9 68.6 %copy-start.3 = (s32[1,1,1,32,2048]{4,3,2,1,0:T(8,128)S(1)}, s32[1,1,1,32,2048]{4,3,2,1,0:T(8,128)}, u32[]{:S(2)}) copy-start(s32[1,1,1,32,2048]{4,3,2,1,0:T(8,128)} %param.16) | copy-start | bytes 786436
  3.9 68.6 %copy-start.4 = (bf16[1,1,1,32,2048]{4,3,2,1,0:T(8,128)(2,1)S(1)}, bf16[1,1,1,32,2048]{4,3,2,1,0:T(8,128)(2,1)}, u32[]{:S(2)}) copy-start(bf16[1,1,1,32,2048]{4,3,2,1,0:T(8,128)(2,1)} %param.17) | copy-start | bytes 393220
  30.2 23.7 %all-to-all-start.1 = ((f32[16,64,128]{2,1,0:T(8,128)}), f32[16,64,128]{2,1,0:T(8,128)S(1)}, u32[]{:S(2)}, u32[]{:S(2)}) async-start(f32[16,64,128]{2,1,0:T(8,128)} %bitcast.10), calls=%async_computation.1 | async-start | bytes 1048576 | tf_op jit(solution)/shard_map/all_to_all | solution.py:270
  54.9 44.9 %all-to-all-start.2 = ((bf16[16,64,128]{2,1,0:T(8,128)(2,1)}), bf16[16,64,128]{2,1,0:T(8,128)(2,1)S(1)}, u32[]{:S(2)}, u32[]{:S(2)}) async-start(bf16[16,64,128]{2,1,0:T(8,128)(2,1)} %broadcast_in_dim.39), calls=%async_computation.2 | async-start | bytes 524288 | tf_op jit(solution)/shard_map/all_to_all | solution.py:275
  62.3 6.8 %collective-permute-start = (bf16[256,128]{1,0:T(8,128)(2,1)S(1)}, bf16[256,128]{1,0:T(8,128)(2,1)S(1)}, u32[]{:S(2)}, u32[]{:S(2)}) collective-permute-start(bf16[256,128]{1,0:T(8,128)(2,1)S(1)} %get-tuple-element.11), channel_id=1, source_target_pairs={{0,8},{8,16},{16,24},{24,0},{1,9},{9,17},{17,25},{25,1},{2,10},{10... | collective-permute-start | bytes 196616 | tf_op jit(solution)/shard_map/ppermute | solution.py:253
  64.3 5.3 %collective-permute-start.1 = (bf16[256,128]{1,0:T(8,128)(2,1)S(1)}, bf16[256,128]{1,0:T(8,128)(2,1)S(1)}, u32[]{:S(2)}, u32[]{:S(2)}) collective-permute-start(bf16[256,128]{1,0:T(8,128)(2,1)S(1)} %get-tuple-element.10), channel_id=1, source_target_pairs={{0,24},{8,0},{16,8},{24,16},{1,25},{9,1},{17,9},{25,17},{2,26},{10... | collective-permute-start | bytes 196616 | tf_op jit(solution)/shard_map/ppermute | solution.py:253
  66.2 5.2 %collective-permute-start.2 = (bf16[256,128]{1,0:T(8,128)(2,1)S(1)}, bf16[256,128]{1,0:T(8,128)(2,1)S(1)}, u32[]{:S(2)}, u32[]{:S(2)}) collective-permute-start(bf16[256,128]{1,0:T(8,128)(2,1)S(1)} %get-tuple-element.9), channel_id=1, source_target_pairs={{0,2},{2,4},{4,6},{6,0},{1,3},{3,5},{5,7},{7,1},{8,10},{10,12},{12... | collective-permute-start | bytes 196616 | tf_op jit(solution)/shard_map/ppermute | solution.py:253
  68.1 4.4 %collective-permute-start.3 = (bf16[256,128]{1,0:T(8,128)(2,1)S(1)}, bf16[256,128]{1,0:T(8,128)(2,1)S(1)}, u32[]{:S(2)}, u32[]{:S(2)}) collective-permute-start(bf16[256,128]{1,0:T(8,128)(2,1)S(1)} %get-tuple-element.8), channel_id=1, source_target_pairs={{0,6},{2,0},{4,2},{6,4},{1,7},{3,1},{5,3},{7,5},{8,14},{10,8},{12,... | collective-permute-start | bytes 196616 | tf_op jit(solution)/shard_map/ppermute | solution.py:253
  69.1 3.4 %collective-permute-start.4 = (bf16[256,128]{1,0:T(8,128)(2,1)S(1)}, bf16[256,128]{1,0:T(8,128)(2,1)S(1)}, u32[]{:S(2)}, u32[]{:S(2)}) collective-permute-start(bf16[256,128]{1,0:T(8,128)(2,1)S(1)} %get-tuple-element.7), channel_id=1, source_target_pairs={{0,1},{1,0},{2,3},{3,2},{4,5},{5,4},{6,7},{7,6},{8,9},{9,8},{10,11... | collective-permute-start | bytes 196616 | tf_op jit(solution)/shard_map/ppermute | solution.py:253
  69.2 3.4 %collective-permute-start.5 = (bf16[256,128]{1,0:T(8,128)(2,1)S(1)}, bf16[256,128]{1,0:T(8,128)(2,1)S(1)}, u32[]{:S(2)}, u32[]{:S(2)}) collective-permute-start(bf16[256,128]{1,0:T(8,128)(2,1)S(1)} %get-tuple-element.6), channel_id=1, source_target_pairs={{0,1},{1,0},{2,3},{3,2},{4,5},{5,4},{6,7},{7,6},{8,9},{9,8},{10,11... | collective-permute-start | bytes 196616 | tf_op jit(solution)/shard_map/ppermute | solution.py:253

commit v2 on v1

v2 whole, which is shorter than its diff:
```python
import functools
import math

import jax
import jax.numpy as jnp
import numpy as np
from jax import lax
from jax.experimental import pallas as pl
from jax.experimental.pallas import tpu as pltpu
from jax.sharding import PartitionSpec as P

F32 = jnp.float32
BF16 = jnp.bfloat16
VMEM_LIMIT = 14 << 20


def half_turn_series():
    angle = np.cos((np.arange(400) + 0.5) * np.pi / 800)
    r = 0.5 * angle
    u = r * r
    root = math.sqrt(2.0)
    even = np.polynomial.chebyshev.Chebyshev.fit(u, root * np.cos(np.pi * r), 4, domain=[0, 0.25])
    odd = np.polynomial.chebyshev.Chebyshev.fit(u, root * np.sin(np.pi * r) / r, 3, domain=[0, 0.25])
    take = lambda fit: [float(v) for v in fit.convert(kind=np.polynomial.Polynomial).coef]
    return take(even), take(odd)


EVEN, ODD = half_turn_series()


def in_hbm(*values):
    return [pltpu.with_memory_space_constraint(value, pltpu.HBM) for value in values]


def horner(coefs, u):
    total = coefs[-1] * u + coefs[-2]
    for coef in coefs[-3::-1]:
        total = total * u + coef
    return total


def phase_kernel(
    sizes,
    scale,
    paired,
    place_ref,
    count_ref,
    pos_ref,
    feat_ref,
    kvec_ref,
    sigma_ref,
    mix_ref,
    table_ref,
    *refs,
):
    out_refs = refs[: 1 + paired]
    frac_ref, own_ref, mix_turned, decay_ref = refs[1 + paired :]
    atoms, width = feat_ref.shape
    kblock = kvec_ref.shape[1]
    step = pl.program_id(0)

    @pl.when(step == 0)
    def _():
        rows = []
        for axis in range(3):
            frac = (place_ref[axis].astype(F32) + pos_ref[axis]) / sizes[axis]
            high = frac.astype(BF16).astype(F32)
            middle = (frac - high).astype(BF16).astype(F32)
            rows += [high, middle, frac - high - middle]
        stacked = jnp.concatenate(rows + [jnp.zeros((16 - len(rows), atoms), F32)], axis=0)
        frac_ref[...] = stacked.T.astype(BF16)
        atom = lax.broadcasted_iota(jnp.int32, (atoms, width), 0)
        own = jnp.where(atom < count_ref[0], feat_ref[...].astype(F32), 0.0)
        own_ref[...] = own.T.astype(BF16)
        mix_turned[...] = mix_ref[...].T
        decay_ref[...] = jnp.broadcast_to(-sigma_ref[...], (width, width)).T

    kvec = kvec_ref[...].astype(F32)
    weights = jnp.concatenate(
        [kvec[axis : axis + 1, :] for axis in range(3) for _ in range(3)]
        + [jnp.zeros((7, kblock), F32)],
        axis=0,
    ).astype(BF16)
    chunk = min(256, atoms)
    for start in range(0, atoms, chunk):
        rows = slice(start, start + chunk)
        theta = jnp.dot(frac_ref[rows, :], weights, preferred_element_type=F32)
        r = theta - jnp.round(theta)
        u = r * r
        even = horner(EVEN, u)
        odd = horner(ODD, u) * r
        cosine = (1.0 - odd * odd).astype(BF16)
        sine = (even * odd).astype(BF16)
        table_ref[rows, :kblock] = cosine
        table_ref[rows, kblock:] = sine

    sums = jnp.dot(own_ref[...], table_ref[...], preferred_element_type=F32)
    ksq = jnp.sum(kvec * kvec, axis=0, keepdims=True)
    decay = jnp.exp(decay_ref[:, :1] * ksq)
    mixed = jnp.dot(
        mix_turned[...], sums * scale, precision=lax.Precision.HIGHEST, preferred_element_type=F32
    )
    result = (mixed * jnp.concatenate([decay, decay], axis=1)).T
    if paired:
        half = pl.num_programs(0) // 2

        @pl.when(step < half)
        def _():
            out_refs[0][...] = result

        @pl.when(step >= half)
        def _():
            out_refs[1][...] = result
    else:
        out_refs[0][...] = result


def phases(place, count, sizes, scale, pos, feats, kvec, sigma, w_mix):
    atoms, width = feats.shape
    kcount = kvec.shape[1]
    kblock = 256 if kcount % 512 == 0 else 128
    steps = kcount // kblock
    half = steps // 2
    paired = sizes[2] == 2
    whole = lambda *shape: pl.BlockSpec(shape, lambda b, *_: (0,) * len(shape))

    def kvec_map(b, place_ref, count_ref):
        return (0, lax.rem(b + (1 - place_ref[2]) * half, steps) if paired else b)

    if paired:
        out_specs = [
            pl.BlockSpec((2 * kblock, width), lambda b, *_: (jnp.minimum(b, half - 1), 0)),
            pl.BlockSpec((2 * kblock, width), lambda b, *_: (jnp.maximum(b - half, 0), 0)),
        ]
        out_shape = [jax.ShapeDtypeStruct((kcount, width), F32)] * 2
    else:
        out_specs = [pl.BlockSpec((2 * kblock, width), lambda b, *_: (b, 0))]
        out_shape = [jax.ShapeDtypeStruct((2 * kcount, width), F32)]
    return pl.pallas_call(
        functools.partial(phase_kernel, sizes, scale, paired),
        grid_spec=pltpu.PrefetchScalarGridSpec(
            num_scalar_prefetch=2,
            grid=(steps,),
            in_specs=[
                whole(3, 1, atoms),
                whole(atoms, width),
                pl.BlockSpec((3, kblock), kvec_map),
                whole(1, width),
                whole(width, width),
            ],
            out_specs=[pl.BlockSpec((atoms, 2 * kblock), lambda b, *_: (0, b)), *out_specs],
            scratch_shapes=[
                pltpu.VMEM((atoms, 16), BF16),
                pltpu.VMEM((width, atoms), BF16),
                pltpu.VMEM((width, width), F32),
                pltpu.VMEM((width, width), F32),
            ],
        ),
        out_shape=[pltpu.HBM((atoms, 2 * kcount), BF16), *out_shape],
        compiler_params=pltpu.CompilerParams(vmem_limit_bytes=VMEM_LIMIT),
        name="phases",
    )(place, count, *in_hbm(pos.reshape(3, 1, atoms), feats, kvec, sigma.reshape(1, width), w_mix))


def select_kernel(count_ref, send_ref, feat_ref, *refs):
    *out_refs, own_ref = refs
    faces, _, picks = send_ref.shape
    atoms, width = feat_ref.shape
    atom = lax.broadcasted_iota(jnp.int32, (atoms, width), 0)
    own_ref[...] = jnp.where(atom < count_ref[0], feat_ref[...].astype(F32), 0.0).astype(BF16)
    rows = jnp.concatenate([send_ref[face] for face in range(faces)], axis=0).astype(F32)
    columns = jnp.concatenate([rows, jnp.zeros((8 - faces, picks), F32)], axis=0).T
    chunk = min(256, atoms)
    lane = lax.broadcasted_iota(jnp.int32, (picks, chunk), 1).astype(F32).astype(BF16)
    one, zero = jnp.ones((), BF16), jnp.zeros((), BF16)
    for face in range(faces):
        spread = jnp.broadcast_to(columns[:, face : face + 1], (picks, 128))
        total = jnp.zeros((picks, width), F32)
        for start in range(0, atoms, chunk):
            key = (spread - float(start)).astype(BF16)
            hot = jnp.where(jnp.concatenate([key] * (chunk // 128), axis=1) == lane, one, zero)
            total += jnp.dot(hot, own_ref[start : start + chunk, :], preferred_element_type=F32)
        if face < 4:
            out_refs[face][...] = total.astype(BF16)
        else:
            out_refs[4][face - 4] = total.astype(BF16)


def selected(count, send, feats):
    atoms, width = feats.shape
    faces, picks = send.shape
    return pl.pallas_call(
        select_kernel,
        in_specs=[
            pl.BlockSpec(memory_space=pltpu.SMEM),
            pl.BlockSpec((faces, 1, picks), lambda: (0, 0, 0)),
            pl.BlockSpec((atoms, width), lambda: (0, 0)),
        ],
        out_specs=[pl.BlockSpec(memory_space=pltpu.VMEM)] * 5,
        out_shape=[jax.ShapeDtypeStruct((picks, width), BF16)] * 4
        + [jax.ShapeDtypeStruct((2, picks, width), BF16)],
        scratch_shapes=[pltpu.VMEM((atoms, width), BF16)],
        compiler_params=pltpu.CompilerParams(vmem_limit_bytes=VMEM_LIMIT),
        name="selected",
    )(count, *in_hbm(send.reshape(faces, 1, picks), feats))


def total_kernel(parts_ref, out_ref):
    total = parts_ref[0].astype(F32)
    for part in range(1, parts_ref.shape[0]):
        total += parts_ref[part].astype(F32)
    total = total.astype(BF16)
    for part in range(parts_ref.shape[0]):
        out_ref[part] = total


def totals(parts):
    return pl.pallas_call(
        total_kernel,
        in_specs=[pl.BlockSpec(memory_space=pltpu.VMEM)],
        out_specs=pl.BlockSpec(memory_space=pltpu.VMEM),
        out_shape=jax.ShapeDtypeStruct(parts.shape, BF16),
        compiler_params=pltpu.CompilerParams(vmem_limit_bytes=4 << 20),
        name="totals",
    )(parts)


def message_kernel(low, count_ref, nbr_ref, weight_ref, feat_ref, *refs):
    halo_refs = [*refs[:4], refs[4].at[0], refs[4].at[1]]
    wmsg_ref, out_ref, high_key, low_key, edge, table_ref, adj_ref, msg_ref = refs[5:]
    slots, atoms = nbr_ref.shape
    width = feat_ref.shape[1]
    lanes = 8 * slots
    groups = atoms // 8
    span = adj_ref.shape[0] // 8
    highs = table_ref.shape[0] // low
    step = pl.program_id(0)

    @pl.when(step == 0)
    def _():
        stack = lambda ref: jnp.concatenate(
            [ref[:, i * groups : (i + 1) * groups].astype(F32) for i in range(8)], axis=0
        )
        picks = stack(nbr_ref)
        upper = jnp.floor(picks * (1.0 / low))
        low_key[...] = picks - upper * low
        place = lax.broadcasted_iota(jnp.int32, (lanes, groups), 0) // slots
        high_key[...] = (upper * 8.0 + place.astype(F32)).T
        edge[...] = stack(weight_ref).T
        atom = lax.broadcasted_iota(jnp.int32, (atoms, width), 0)
        table_ref[:atoms, :] = jnp.where(atom < count_ref[0], feat_ref[...].astype(F32), 0.0).astype(BF16)
        for face, halo in enumerate(halo_refs):
            rows = halo.shape[0]
            table_ref[atoms + face * rows : atoms + (face + 1) * rows, :] = halo[...]

    high_iota = lax.broadcasted_iota(jnp.int32, (highs * 8, lanes), 0).astype(F32).astype(BF16)
    lane = lax.broadcasted_iota(jnp.int32, (lanes, 128), 1).astype(F32)
    low_iota = [(lane + 128.0 * part).astype(BF16) for part in range(low // 128)]
    tile = lambda x, n: jnp.concatenate([x] * (n // 16), axis=0)
    zero = jnp.zeros((), BF16)
    one = jnp.ones((), BF16)
    first_lane = pl.multiple_of((step * span) // 128 * 128, 128)
    lows = pltpu.roll(low_key[:, pl.ds(first_lane, 128)], (128 - (step * span) % 128) % 128, 1)

    def group(number):
        row = pl.ds(step * span + number, 1)
        high = jnp.broadcast_to(high_key[row, :], (16, lanes)).astype(BF16)
        value = jnp.broadcast_to(edge[row, :], (16, lanes)).astype(BF16)
        left = jnp.where(tile(high, highs * 8) == high_iota, tile(value, highs * 8), zero)
        lower = jnp.broadcast_to(lows[:, number : number + 1], (lanes, 128)).astype(BF16)
        right = jnp.concatenate([jnp.where(lower == iota, one, zero) for iota in low_iota], axis=1)
        return jnp.dot(left, right, preferred_element_type=F32)

    for number in range(0, span, 2):
        first = group(number)
        second = group(number + 1)
        for upper in range(highs):
            here = slice(upper * 8, upper * 8 + 8)
            block = jnp.concatenate([first[here], second[here]], axis=0).astype(BF16)
            adj_ref[number * 8 : number * 8 + 16, upper * low : (upper + 1) * low] = block

    summed = jnp.dot(adj_ref[...], table_ref[...], preferred_element_type=F32)
    message = (summed / math.sqrt(slots)).astype(BF16)
    hidden = jnp.dot(message, wmsg_ref[...], preferred_element_type=F32)
    msg_ref[...] = hidden / (1.0 + jnp.exp(-hidden))
    for i in range(8):
        start = pl.multiple_of(i * groups + step * span, span)
        own = table_ref[pl.ds(start, span), :].astype(F32)
        gate = msg_ref[pl.ds(i, span, stride=8), :]
        atom = lax.broadcasted_iota(jnp.int32, (span, width), 0) + start
        out_ref[i] = jnp.where(atom < count_ref[0], own + gate, 0.0).astype(BF16)


def messages(count, nbr, weights, feats, halos, wmsg):
    slots, atoms = nbr.shape
    width = feats.shape[1]
    groups = atoms // 8
    rows = atoms + 6 * halos[0].shape[0]
    low = 256
    span = min(64, groups)
    whole = lambda *shape: pl.BlockSpec(shape, lambda b: (0,) * len(shape))
    out = pl.pallas_call(
        functools.partial(message_kernel, low),
        grid=(groups // span,),
        in_specs=[
            pl.BlockSpec(memory_space=pltpu.SMEM),
            whole(slots, atoms),
            whole(slots, atoms),
            whole(atoms, width),
            *[whole(*halo.shape) for halo in halos],
            whole(width, width),
        ],
        out_specs=pl.BlockSpec((8, span, width), lambda b: (0, b, 0)),
        out_shape=jax.ShapeDtypeStruct((8, groups, width), BF16),
        scratch_shapes=[
            pltpu.VMEM((groups, 8 * slots), F32),
            pltpu.VMEM((8 * slots, groups), F32),
            pltpu.VMEM((groups, 8 * slots), F32),
            pltpu.VMEM((rows, width), BF16),
            pltpu.VMEM((8 * span, rows), BF16),
            pltpu.VMEM((8 * span, width), F32),
        ],
        compiler_params=pltpu.CompilerParams(vmem_limit_bytes=VMEM_LIMIT),
        name="messages",
    )(count, *in_hbm(nbr, weights, feats), *halos, *in_hbm(wmsg))
    return out.reshape(atoms, width)


def back_kernel(scale, count_ref, table_hbm, *refs):
    *g_refs, out_ref, table_ref, sems = refs
    atoms, width = out_ref.shape
    pieces = sems.shape[0]
    rows = atoms // pieces
    copies = []
    for piece in range(pieces):
        here = pl.ds(piece * rows, rows)
        copies.append(pltpu.make_async_copy(table_hbm.at[here], table_ref.at[here], sems.at[piece]))
        copies[-1].start()
    for piece in range(pieces):
        copies[piece].wait()
        here = slice(piece * rows, (piece + 1) * rows)
        back = jnp.zeros((rows, width), F32)
        start = 0
        for g_ref in g_refs:
            depth = g_ref.shape[0]
            back += jnp.dot(
                table_ref[here, start : start + depth], g_ref[...], preferred_element_type=F32
            )
            start += depth
        atom = lax.broadcasted_iota(jnp.int32, (rows, width), 0) + piece * rows
        out_ref[here, :] = jnp.where(atom < count_ref[0], back * scale, 0.0)


def back(count, table, gs, scale):
    atoms, depth = table.shape
    width = gs[0].shape[1]
    vmem = pl.BlockSpec(memory_space=pltpu.VMEM)
    return pl.pallas_call(
        functools.partial(back_kernel, scale),
        in_specs=[
            pl.BlockSpec(memory_space=pltpu.SMEM),
            pl.BlockSpec(memory_space=pltpu.HBM),
            *[vmem for _ in gs],
        ],
        out_specs=vmem,
        out_shape=jax.ShapeDtypeStruct((atoms, width), F32),
        scratch_shapes=[pltpu.VMEM((atoms, depth), BF16), pltpu.SemaphoreType.DMA((8,))],
        compiler_params=pltpu.CompilerParams(vmem_limit_bytes=VMEM_LIMIT),
        name="back",
    )(count, *in_hbm(table), *gs)


def passed_along(value, axis, steps):
    size = lax.axis_size(axis)
    pairs = [(source, (source + steps) % size) for source in range(size)]
    return lax.ppermute(value, axis, pairs)


def shards(
    features, positions, counts, kvec, sigma, w_mix, neighbours, edge_weight, send_list, w_message
):
    atoms = features.shape[3]
    width = features.shape[4]
    kcount = kvec.shape[1]
    slots = neighbours.shape[3]
    feats = features.reshape(atoms, width)
    count = counts.reshape(1)
    sizes = [lax.axis_size(axis) for axis in ("gx", "gy", "gz")]
    plane = sizes[0] * sizes[1]
    devices = plane * sizes[2]
    place = jnp.stack([lax.axis_index(axis) for axis in ("gx", "gy", "gz")]).astype(jnp.int32)
    paired = sizes[2] == 2

    outgoing = selected(count, send_list.reshape(6, -1), feats)
    halos = [
        passed_along(outgoing[2 * number + side], axis, 1 - 2 * side)
        for number, axis in enumerate(("gx", "gy"))
        for side in range(2)
    ]
    if paired:
        halos.append(passed_along(outgoing[4], "gz", 1))
    else:
        halos.append(jnp.stack([passed_along(outgoing[4][side], "gz", 1 - 2 * side) for side in range(2)]))
    positions, _ = lax.optimization_barrier((positions, outgoing))
    scale = 1.0 / math.sqrt(atoms * devices)
    table, *sums = phases(
        place, count, sizes, scale, positions.reshape(3, atoms), feats, kvec, sigma, w_mix
    )
    if paired:
        mine = sums[1] + passed_along(sums[0], "gz", 1)
    else:
        parts = lax.all_to_all(sums[0], "gz", 0, 0, tiled=True)
        mine = jnp.sum(parts.reshape(sizes[2], -1, width), axis=0)
    mine, halos = lax.optimization_barrier((mine, halos))
    part = mine.shape[0] // plane
    received = lax.all_to_all(mine.reshape(plane, part, width), ("gx", "gy"), 0, 0, tiled=True)

    neighbours, _ = lax.optimization_barrier((neighbours, mine))
    updated = messages(
        count, neighbours.reshape(slots, atoms), edge_weight.reshape(slots, atoms), feats, halos, w_message
    )

    received, updated = lax.optimization_barrier((received, updated))
    g = lax.all_to_all(totals(received), ("gx", "gy"), 0, 0, tiled=True).reshape(plane * part, width)
    if paired:
        gs = [passed_along(g, "gz", 1), g]
    else:
        gs = [lax.all_gather(g, "gz", tiled=True)]
    long_range = back(count, table, gs, 2.0 / math.sqrt(kcount))
    return (updated.reshape(1, 1, 1, atoms, width), long_range.reshape(1, 1, 1, atoms, width))


def solution(mesh):
    split = P("gx", "gy", "gz", None, None)
    placed = (split, split, P("gx", "gy", "gz"), P(), P(), P(), split, split, split, P())
    return jax.shard_map(
        shards, mesh=mesh, in_specs=placed, out_specs=(split, split), check_vma=False
    )
```

time: 111 us -> 71.4 us (0.64)
  Pallas kernels: 54.3 us -> 36.2 us
  waiting for transfers between devices: 16.1 us -> 3.91 us
  blocking collectives: 8.72 us -> 15.2 us
  starting transfers between devices: 19.6 us -> 13.3 us
  matrix products: 3.63 us -> 0 us
  local copies, waits for them, and re-layouts: 3.44 us -> 0 us
  other arithmetic: 3.12 us -> 0.93 us
    all_to_all x2 -> x1, waiting for transfers between devices: 13.2 us -> 0.01 us  [shards(): lax.all_to_all(mine.reshape(plane, part, width), ('gx', 'gy'), 0, 0, tile...]
    pallas_call x1, Pallas kernels: 27.2 us -> 14.2 us  [messages(): pl.pallas_call(functools.partial(message_kernel, low), grid=(groups // sp...]
    all_to_all x2 -> x1, starting transfers between devices: 12.2 us -> 4.84 us  [shards(): lax.all_to_all(mine.reshape(plane, part, width), ('gx', 'gy'), 0, 0, tile...]
    all_to_all x2 -> x1, blocking collectives: 8.72 us -> 15.2 us  [shards(): lax.all_to_all(totals(received), ('gx', 'gy'), 0, 0, tiled=True)]
    pallas_call x2 -> x4, Pallas kernels: 27.1 us -> 22 us  [the longest x1 13.2 us: phases(): pl.pallas_call(functools.partial(phase_kernel, sizes, scale, paired), gri...]
    dot_general x2 -> x0, matrix products: 3.63 us -> none  [the longest x1 3.44 us: shards(): outgoing = jnp.dot(selector, own, preferred_element_type=F32).astype(BF16)]
    unnamed x15 -> x0, local copies, waits for them, and re-layouts: 2.54 us -> none
    reduce_sum x3 -> x0, other arithmetic: 1.66 us -> none  [the longest x1 0.89 us: reduced_and_filtered(): sums = jnp.sum(sums.reshape(size_z, rows // size_z, width), axis=0)]
  transfers between devices with their start and end apart: 8 -> 8, of which waited for: 3 -> 3; matrix products, arithmetic and copies ran while one was open for 5% -> 1% of each run, Pallas kernels for 25% -> 20%
where the time goes in v2:
time: 71.4 us; the launch traced here: 71.1 us
  Pallas kernels  36.2 us (51%)
  blocking collectives  15.2 us (21%)
  starting transfers between devices  13.3 us (19%)
  waiting for transfers between devices  3.91 us (5%)
  between operations  1.47 us (2%)
  other arithmetic  0.93 us (1%)
    all_to_all x1, blocking collectives, shards(): lax.all_to_all(totals(received), ('gx', 'gy'), 0, 0, tiled=True)  15.2 us
    pallas_call x1, Pallas kernels, messages(): pl.pallas_call(functools.partial(message_kernel, low), grid=(groups // sp...  14.2 us
    pallas_call x1, Pallas kernels, phases(): pl.pallas_call(functools.partial(phase_kernel, sizes, scale, paired), gri...  13.2 us
    ppermute x7, starting transfers between devices, passed_along(): return lax.ppermute(value, axis, pairs)  8.49 us
    pallas_call x1, Pallas kernels, back(): pl.pallas_call(functools.partial(back_kernel, scale), in_specs=[pl.BlockS...  5.67 us
    all_to_all x1, starting transfers between devices, shards(): lax.all_to_all(mine.reshape(plane, part, width), ('gx', 'gy'), 0, 0, tile...  4.84 us
    ppermute x7, waiting for transfers between devices, passed_along(): return lax.ppermute(value, axis, pairs)  3.91 us
    pallas_call x1, Pallas kernels, selected(): pl.pallas_call(select_kernel, in_specs=[pl.BlockSpec(memory_space=pltpu.S...  3.11 us
  transfers between devices with their start and end apart: 8, of which 3 were waited for; matrix products, arithmetic and copies ran while one was open for 1% of the time, Pallas kernels for 20%

profile of v2, /device:TPU:0, one launch (start us, length us, event | category | flops | bytes accessed | tf_op | source)
XLA Modules:
  0.0 71.1 jit_solution(17119860513752925377)
XLA Ops:
  1.3 3.1 %selected.1 = (bf16[256,128]{1,0:T(8,128)(2,1)S(1)}, bf16[256,128]{1,0:T(8,128)(2,1)S(1)}, bf16[256,128]{1,0:T(8,128)(2,1)S(1)}, bf16[256,128]{1,0:T(8,128)(2,1)S(1)}, bf16[2,256,128]{2,1,0:T(8,128)(2,1)S(1)}) custom-call(s32[1]{0:T(128)} %bitcast.15.count_ref, s32[6,1,256]{2,1,0:T(1,128)} %bitcast.29, bf16[2048,128]{1,0:T(8,128)(2,1)} %bitcast.21), custom_call_target="tpu_custom_call" | custom-call | tf_op jit(solution)/shard_map/selected/pallas_call | solution.py:192
  4.4 0.1 pad_add_fusion.place_ref
  4.5 13.2 %phases.1 = (bf16[2048,2048]{1,0:T(8,128)(2,1)}, f32[1024,128]{1,0:T(8,128)S(1)}, f32[1024,128]{1,0:T(8,128)S(1)}) custom-call(s32[3]{0:T(128)S(1)} %pad_add_fusion.place_ref, s32[1]{0:T(128)} %bitcast.16.count_ref, f32[3,1,2048]{2,1,0:T(1,128)} %bitcast.28, bf16[2048,128]{1,0:T(8,128)(2,1)} %bitcast.22, s32[3,1024]{1,0:T(4,128)} %kvec_ref.1, ...), custom_call_target="tpu_custom_call" | custom-call | tf_op jit(solution)/shard_map/phases/pallas_call | solution.py:139
  17.7 0.4 collective-permute-start
  18.1 0.1 collective-permute-start.5
  18.2 3.0 %collective-permute-start.1 = (bf16[256,128]{1,0:T(8,128)(2,1)S(1)}, bf16[256,128]{1,0:T(8,128)(2,1)S(1)}, u32[]{:S(2)}, u32[]{:S(2)}) collective-permute-start(bf16[256,128]{1,0:T(8,128)(2,1)S(1)} %get-tuple-element.20), channel_id=1, source_target_pairs={{0,8},{8,16},{16,24},{24,0},{1,9},{9,17},{17,25},{25,1},{2,10},{10... | collective-permute-start | bytes 196616 | tf_op jit(solution)/shard_map/ppermute | solution.py:376
  21.2 2.0 %collective-permute-start.2 = (bf16[256,128]{1,0:T(8,128)(2,1)S(1)}, bf16[256,128]{1,0:T(8,128)(2,1)S(1)}, u32[]{:S(2)}, u32[]{:S(2)}) collective-permute-start(bf16[256,128]{1,0:T(8,128)(2,1)S(1)} %get-tuple-element.21), channel_id=1, source_target_pairs={{0,24},{8,0},{16,8},{24,16},{1,25},{9,1},{17,9},{25,17},{2,26},{10... | collective-permute-start | bytes 196616 | tf_op jit(solution)/shard_map/ppermute | solution.py:376
  23.2 1.7 %collective-permute-start.3 = (bf16[256,128]{1,0:T(8,128)(2,1)S(1)}, bf16[256,128]{1,0:T(8,128)(2,1)S(1)}, u32[]{:S(2)}, u32[]{:S(2)}) collective-permute-start(bf16[256,128]{1,0:T(8,128)(2,1)S(1)} %get-tuple-element.22), channel_id=1, source_target_pairs={{0,2},{2,4},{4,6},{6,0},{1,3},{3,5},{5,7},{7,1},{8,10},{10,12},{12... | collective-permute-start | bytes 196616 | tf_op jit(solution)/shard_map/ppermute | solution.py:376
  24.9 0.0 collective-permute-done
  25.0 1.2 %collective-permute-start.4 = (bf16[256,128]{1,0:T(8,128)(2,1)S(1)}, bf16[256,128]{1,0:T(8,128)(2,1)S(1)}, u32[]{:S(2)}, u32[]{:S(2)}) collective-permute-start(bf16[256,128]{1,0:T(8,128)(2,1)S(1)} %get-tuple-element.23), channel_id=1, source_target_pairs={{0,6},{2,0},{4,2},{6,4},{1,7},{3,1},{5,3},{7,5},{8,14},{10,8},{12,... | collective-permute-start | bytes 196616 | tf_op jit(solution)/shard_map/ppermute | solution.py:376
  26.2 0.8 %add.3 = f32[1024,128]{1,0:T(8,128)} add(f32[1024,128]{1,0:T(8,128)S(1)} %get-tuple-element.26, f32[1024,128]{1,0:T(8,128)S(1)} %collective-permute-done) | non-fusion elementwise | flops 131072 | bytes 1572864 | tf_op jit(solution)/shard_map/add | solution.py:410
  27.0 0.0 collective-permute-done.1.refs_0_
  27.0 0.0 collective-permute-done.2.refs_1_
  27.0 2.1 %collective-permute-done.3.refs_2_ = bf16[256,128]{1,0:T(8,128)(2,1)S(1)} collective-permute-done((bf16[256,128]{1,0:T(8,128)(2,1)S(1)}, bf16[256,128]{1,0:T(8,128)(2,1)S(1)}, u32[]{:S(2)}, u32[]{:S(2)}) %collective-permute-start.3) | collective-permute-done | bytes 65568 | tf_op jit(solution)/shard_map/ppermute | solution.py:376
  29.1 0.3 collective-permute-done.4.refs_3_
  29.4 0.0 collective-permute-done.5.refs_4_
  29.4 4.8 %all-to-all-start = ((f32[16,64,128]{2,1,0:T(8,128)}), f32[16,64,128]{2,1,0:T(8,128)S(1)}, u32[]{:S(2)}, u32[]{:S(2)}) async-start(f32[16,64,128]{2,1,0:T(8,128)} %bitcast.8), calls=%async_computation | async-start | bytes 1048576 | tf_op jit(solution)/shard_map/all_to_all | solution.py:416
  34.2 14.2 %messages.1 = bf16[8,256,128]{2,1,0:T(8,128)(2,1)} custom-call(s32[1]{0:T(128)} %bitcast.17.count_ref, s32[32,2048]{1,0:T(8,128)} %bitcast.26, bf16[32,2048]{1,0:T(8,128)(2,1)} %bitcast.27, bf16[2048,128]{1,0:T(8,128)(2,1)} %bitcast.23, bf16[256,128]{1,0:T(8,128)(2,1)S(1)} %collective-permute-done.1.refs_0_, ...), custom_call_target="tpu_custom_call" | custom-call | tf_op jit(solution)/shard_map/messages/pallas_call | solution.py:302
  48.5 0.0 all-to-all-done.parts_ref
  48.5 15.2 %all_to_all.10 = bf16[16,64,128]{2,1,0:T(8,128)(2,1)S(1)} all-to-all(bf16[16,64,128]{2,1,0:T(8,128)(2,1)S(1)} %totals.1), channel_id=1, replica_groups=mesh['gx'=4,'gy'=4,'gz'=2] {'gx','gy'}, dimensions={0} | all-to-all | bytes 524288 | tf_op jit(solution)/shard_map/all_to_all | solution.py:424
  63.7 0.0 collective-permute-start.6
  63.7 1.5 %collective-permute-done.6.refs_0_ = bf16[1024,128]{1,0:T(8,128)(2,1)S(1)} collective-permute-done((bf16[1024,128]{1,0:T(8,128)(2,1)S(1)}, bf16[1024,128]{1,0:T(8,128)(2,1)S(1)}, u32[]{:S(2)}, u32[]{:S(2)}) %collective-permute-start.6) | collective-permute-done | bytes 262176 | tf_op jit(solution)/shard_map/ppermute | solution.py:376
  65.2 5.7 %back.1 = f32[2048,128]{1,0:T(8,128)} custom-call(s32[1]{0:T(128)} %bitcast.18.count_ref, bf16[2048,2048]{1,0:T(8,128)(2,1)} %get-tuple-element.36.table_hbm, bf16[1024,128]{1,0:T(8,128)(2,1)S(1)} %collective-permute-done.6.refs_0_, bf16[1024,128]{1,0:T(8,128)(2,1)S(1)} %bitcast.20), custom_call_target="tpu_custom_call" | custom-call | tf_op jit(solution)/shard_map/back/pallas_call | solution.py:358
  (1 shorter events, 0.0 us)
Async XLA Ops:
  17.7 7.3 %collective-permute-start = (f32[1024,128]{1,0:T(8,128)S(1)}, f32[1024,128]{1,0:T(8,128)S(1)}, u32[]{:S(2)}, u32[]{:S(2)}) collective-permute-start(f32[1024,128]{1,0:T(8,128)S(1)} %get-tuple-element.27), channel_id=1, source_target_pairs={{0,1},{1,0},{2,3},{3,2},{4,5},{5,4},{6,7},{7,6},{8,9},{9,8},{10,11... | collective-permute-start | bytes 1572872 | tf_op jit(solution)/shard_map/ppermute | solution.py:376
  18.1 11.3 %collective-permute-start.5 = (bf16[2,256,128]{2,1,0:T(8,128)(2,1)S(1)}, bf16[2,256,128]{2,1,0:T(8,128)(2,1)S(1)}, u32[]{:S(2)}, u32[]{:S(2)}) collective-permute-start(bf16[2,256,128]{2,1,0:T(8,128)(2,1)S(1)} %get-tuple-element.24), channel_id=1, source_target_pairs={{0,1},{1,0},{2,3},{3,2},{4,5},{5,4},{6,7},{7,6},{8,9},{9,8},{10,11... | collective-permute-start | bytes 393224 | tf_op jit(solution)/shard_map/ppermute | solution.py:376
  18.2 8.8 %collective-permute-start.1 = (bf16[256,128]{1,0:T(8,128)(2,1)S(1)}, bf16[256,128]{1,0:T(8,128)(2,1)S(1)}, u32[]{:S(2)}, u32[]{:S(2)}) collective-permute-start(bf16[256,128]{1,0:T(8,128)(2,1)S(1)} %get-tuple-element.20), channel_id=1, source_target_pairs={{0,8},{8,16},{16,24},{24,0},{1,9},{9,17},{17,25},{25,1},{2,10},{10... | collective-permute-start | bytes 196616 | tf_op jit(solution)/shard_map/ppermute | solution.py:376
  21.2 5.8 %collective-permute-start.2 = (bf16[256,128]{1,0:T(8,128)(2,1)S(1)}, bf16[256,128]{1,0:T(8,128)(2,1)S(1)}, u32[]{:S(2)}, u32[]{:S(2)}) collective-permute-start(bf16[256,128]{1,0:T(8,128)(2,1)S(1)} %get-tuple-element.21), channel_id=1, source_target_pairs={{0,24},{8,0},{16,8},{24,16},{1,25},{9,1},{17,9},{25,17},{2,26},{10... | collective-permute-start | bytes 196616 | tf_op jit(solution)/shard_map/ppermute | solution.py:376
  23.2 5.8 %collective-permute-start.3 = (bf16[256,128]{1,0:T(8,128)(2,1)S(1)}, bf16[256,128]{1,0:T(8,128)(2,1)S(1)}, u32[]{:S(2)}, u32[]{:S(2)}) collective-permute-start(bf16[256,128]{1,0:T(8,128)(2,1)S(1)} %get-tuple-element.22), channel_id=1, source_target_pairs={{0,2},{2,4},{4,6},{6,0},{1,3},{3,5},{5,7},{7,1},{8,10},{10,12},{12... | collective-permute-start | bytes 196616 | tf_op jit(solution)/shard_map/ppermute | solution.py:376
  25.0 4.4 %collective-permute-start.4 = (bf16[256,128]{1,0:T(8,128)(2,1)S(1)}, bf16[256,128]{1,0:T(8,128)(2,1)S(1)}, u32[]{:S(2)}, u32[]{:S(2)}) collective-permute-start(bf16[256,128]{1,0:T(8,128)(2,1)S(1)} %get-tuple-element.23), channel_id=1, source_target_pairs={{0,6},{2,0},{4,2},{6,4},{1,7},{3,1},{5,3},{7,5},{8,14},{10,8},{12,... | collective-permute-start | bytes 196616 | tf_op jit(solution)/shard_map/ppermute | solution.py:376
  29.4 19.1 %all-to-all-start = ((f32[16,64,128]{2,1,0:T(8,128)}), f32[16,64,128]{2,1,0:T(8,128)S(1)}, u32[]{:S(2)}, u32[]{:S(2)}) async-start(f32[16,64,128]{2,1,0:T(8,128)} %bitcast.8), calls=%async_computation | async-start | bytes 1048576 | tf_op jit(solution)/shard_map/all_to_all | solution.py:416
  63.7 1.5 %collective-permute-start.6 = (bf16[1024,128]{1,0:T(8,128)(2,1)S(1)}, bf16[1024,128]{1,0:T(8,128)(2,1)S(1)}, u32[]{:S(2)}, u32[]{:S(2)}) collective-permute-start(bf16[1024,128]{1,0:T(8,128)(2,1)S(1)} %bitcast.19), channel_id=1, source_target_pairs={{0,1},{1,0},{2,3},{3,2},{4,5},{5,4},{6,7},{7,6},{8,9},{9,8},{10,11... | collective-permute-start | bytes 786440 | tf_op jit(solution)/shard_map/ppermute | solution.py:376

commit v3 on v2

--- a/solution.py
+++ b/solution.py
@@ -12,6 +12,7 @@
 F32 = jnp.float32
 BF16 = jnp.bfloat16
 VMEM_LIMIT = 14 << 20
+EARLY = 2
 
 
 def half_turn_series():
@@ -20,7 +21,7 @@
     u = r * r
     root = math.sqrt(2.0)
     even = np.polynomial.chebyshev.Chebyshev.fit(u, root * np.cos(np.pi * r), 4, domain=[0, 0.25])
-    odd = np.polynomial.chebyshev.Chebyshev.fit(u, root * np.sin(np.pi * r) / r, 3, domain=[0, 0.25])
+    odd = np.polynomial.chebyshev.Chebyshev.fit(u, root * np.sin(np.pi * r) / r, 4, domain=[0, 0.25])
     take = lambda fit: [float(v) for v in fit.convert(kind=np.polynomial.Polynomial).coef]
     return take(even), take(odd)
 
@@ -188,7 +189,7 @@
 
 def selected(count, send, feats):
     atoms, width = feats.shape
-    faces, picks = send.shape
+    faces, _, picks = send.shape
     return pl.pallas_call(
         select_kernel,
         in_specs=[
@@ -196,13 +197,12 @@
             pl.BlockSpec((faces, 1, picks), lambda: (0, 0, 0)),
             pl.BlockSpec((atoms, width), lambda: (0, 0)),
         ],
-        out_specs=[pl.BlockSpec(memory_space=pltpu.VMEM)] * 5,
+        out_specs=[pl.BlockSpec(memory_space=pltpu.VMEM)] * 6,
         out_shape=[jax.ShapeDtypeStruct((picks, width), BF16)] * 4
-        + [jax.ShapeDtypeStruct((2, picks, width), BF16)],
-        scratch_shapes=[pltpu.VMEM((atoms, width), BF16)],
+        + [jax.ShapeDtypeStruct((2, picks, width), BF16), jax.ShapeDtypeStruct((atoms, width), BF16)],
         compiler_params=pltpu.CompilerParams(vmem_limit_bytes=VMEM_LIMIT),
         name="selected",
-    )(count, *in_hbm(send.reshape(faces, 1, picks), feats))
+    )(count, *in_hbm(send, feats))
 
 
 def total_kernel(parts_ref, out_ref):
@@ -225,45 +225,52 @@
     )(parts)
 
 
-def message_kernel(low, count_ref, nbr_ref, weight_ref, feat_ref, *refs):
-    halo_refs = [*refs[:4], refs[4].at[0], refs[4].at[1]]
-    wmsg_ref, out_ref, high_key, low_key, edge, table_ref, adj_ref, msg_ref = refs[5:]
+def prepare_kernel(low, nbr_ref, weight_ref, high_key, low_key, edge):
     slots, atoms = nbr_ref.shape
-    width = feat_ref.shape[1]
-    lanes = 8 * slots
-    groups = atoms // 8
-    span = adj_ref.shape[0] // 8
-    highs = table_ref.shape[0] // low
-    step = pl.program_id(0)
-
-    @pl.when(step == 0)
-    def _():
-        stack = lambda ref: jnp.concatenate(
-            [ref[:, i * groups : (i + 1) * groups].astype(F32) for i in range(8)], axis=0
-        )
-        picks = stack(nbr_ref)
-        upper = jnp.floor(picks * (1.0 / low))
-        low_key[...] = picks - upper * low
-        place = lax.broadcasted_iota(jnp.int32, (lanes, groups), 0) // slots
-        high_key[...] = (upper * 8.0 + place.astype(F32)).T
-        edge[...] = stack(weight_ref).T
-        atom = lax.broadcasted_iota(jnp.int32, (atoms, width), 0)
-        table_ref[:atoms, :] = jnp.where(atom < count_ref[0], feat_ref[...].astype(F32), 0.0).astype(BF16)
-        for face, halo in enumerate(halo_refs):
-            rows = halo.shape[0]
-            table_ref[atoms + face * rows : atoms + (face + 1) * rows, :] = halo[...]
-
+    groups, lanes = high_key.shape
+    stack = lambda ref: jnp.concatenate(
+        [ref[:, i * groups : (i + 1) * groups].astype(F32) for i in range(8)], axis=0
+    )
+    picks = stack(nbr_ref)
+    upper = jnp.floor(picks * (1.0 / low))
+    low_key[...] = picks - upper * low
+    place = lax.broadcasted_iota(jnp.int32, (lanes, groups), 0) // slots
+    high_key[...] = (upper * 8.0 + place.astype(F32)).T
+    edge[...] = stack(weight_ref).T
+
+
+def prepared(low, nbr, weights):
+    slots, atoms = nbr.shape
+    lanes, groups = 8 * slots, atoms // 8
+    whole = lambda *shape: pl.BlockSpec(shape, lambda: (0,) * len(shape))
+    return pl.pallas_call(
+        functools.partial(prepare_kernel, low),
+        in_specs=[whole(slots, atoms), whole(slots, atoms)],
+        out_specs=[pl.BlockSpec(memory_space=pltpu.VMEM)] * 3,
+        out_shape=[
+            jax.ShapeDtypeStruct((groups, lanes), F32),
+            jax.ShapeDtypeStruct((lanes, groups), F32),
+            jax.ShapeDtypeStruct((groups, lanes), F32),
+        ],
+        compiler_params=pltpu.CompilerParams(vmem_limit_bytes=VMEM_LIMIT),
+        name="prepared",
+    )(*in_hbm(nbr, weights))
+
+
+def build_adjacency(low, base, span, high_key, low_key, edge, store):
+    groups, lanes = high_key.shape
+    highs = store.highs
     high_iota = lax.broadcasted_iota(jnp.int32, (highs * 8, lanes), 0).astype(F32).astype(BF16)
     lane = lax.broadcasted_iota(jnp.int32, (lanes, 128), 1).astype(F32)
     low_iota = [(lane + 128.0 * part).astype(BF16) for part in range(low // 128)]
     tile = lambda x, n: jnp.concatenate([x] * (n // 16), axis=0)
     zero = jnp.zeros((), BF16)
     one = jnp.ones((), BF16)
-    first_lane = pl.multiple_of((step * span) // 128 * 128, 128)
-    lows = pltpu.roll(low_key[:, pl.ds(first_lane, 128)], (128 - (step * span) % 128) % 128, 1)
+    lane_tile = pl.multiple_of(base // 128 * 128, 128)
+    lows = pltpu.roll(low_key[:, pl.ds(lane_tile, 128)], (128 - base % 128) % 128, 1)
 
     def group(number):
-        row = pl.ds(step * span + number, 1)
+        row = pl.ds(base + number, 1)
         high = jnp.broadcast_to(high_key[row, :], (16, lanes)).astype(BF16)
         value = jnp.broadcast_to(edge[row, :], (16, lanes)).astype(BF16)
         left = jnp.where(tile(high, highs * 8) == high_iota, tile(value, highs * 8), zero)
@@ -272,57 +279,113 @@
         return jnp.dot(left, right, preferred_element_type=F32)
 
     for number in range(0, span, 2):
-        first = group(number)
-        second = group(number + 1)
+        one_group = group(number)
+        next_group = group(number + 1)
         for upper in range(highs):
-            here = slice(upper * 8, upper * 8 + 8)
-            block = jnp.concatenate([first[here], second[here]], axis=0).astype(BF16)
-            adj_ref[number * 8 : number * 8 + 16, upper * low : (upper + 1) * low] = block
-
-    summed = jnp.dot(adj_ref[...], table_ref[...], preferred_element_type=F32)
+            rows = slice(upper * 8, upper * 8 + 8)
+            block = jnp.concatenate([one_group[rows], next_group[rows]], axis=0).astype(BF16)
+            store(number * 8, upper, block)
+
+
+class Store:
+    def __init__(self, ref, low):
+        self.ref, self.low, self.highs = ref, low, ref.shape[1] // low
+
+    def __call__(self, row, upper, block):
+        self.ref[row : row + 16, upper * self.low : (upper + 1) * self.low] = block
+
+
+def build_kernel(low, span, high_key, low_key, edge, adj_ref):
+    build_adjacency(low, pl.program_id(0) * span, span, high_key, low_key, edge, Store(adj_ref, low))
+
+
+def built(low, keys, rows, here):
+    span = min(32, here)
+    vmem = pl.BlockSpec(memory_space=pltpu.VMEM)
+    return pl.pallas_call(
+        functools.partial(build_kernel, low, span),
+        grid=(here // span,),
+        in_specs=[vmem] * 3,
+        out_specs=pl.BlockSpec((8 * span, rows), lambda b: (b, 0)),
+        out_shape=pltpu.HBM((8 * here, rows), BF16),
+        compiler_params=pltpu.CompilerParams(vmem_limit_bytes=VMEM_LIMIT),
+        name="built",
+    )(*keys)
+
+
+def message_kernel(
+    low, span, slots, count_ref, adj_hbm, high_key, low_key, edge, own_ref, *refs
+):
+    halo_refs = [*refs[:4], refs[4].at[0], refs[4].at[1]]
+    wmsg_ref, out_ref, slots_ref, msg_ref, sems = refs[-5:]
+    atoms, width = own_ref.shape
+    groups = high_key.shape[0]
+    step = pl.program_id(0)
+    steps = pl.num_programs(0)
+    early = sems.shape[0]
+
+    def fetch(piece):
+        rows = pl.ds(piece * 8 * span, 8 * span)
+        return pltpu.make_async_copy(adj_hbm.at[rows], slots_ref.at[piece + 1], sems.at[piece])
+
+    @pl.when(step == 0)
+    def _():
+        for piece in range(early):
+            fetch(piece).start()
+
+    for piece in range(early):
+
+        @pl.when(step == steps - early + piece)
+        def _():
+            fetch(piece).wait()
+
+    @pl.when(step < steps - early)
+    def _():
+        start = (step + early) * span
+        build_adjacency(low, start, span, high_key, low_key, edge, Store(slots_ref.at[0], low))
+
+    base = lax.rem(step + early, steps) * span
+    adj_ref = slots_ref.at[jnp.maximum(step + early - steps + 1, 0)]
+    summed = jnp.dot(adj_ref[:, :atoms], own_ref[...], preferred_element_type=F32)
+    halo = jnp.concatenate([ref[...] for ref in halo_refs], axis=0)
+    summed += jnp.dot(adj_ref[:, atoms:], halo, preferred_element_type=F32)
     message = (summed / math.sqrt(slots)).astype(BF16)
     hidden = jnp.dot(message, wmsg_ref[...], preferred_element_type=F32)
     msg_ref[...] = hidden / (1.0 + jnp.exp(-hidden))
+    inside = pl.multiple_of(base, span)
     for i in range(8):
-        start = pl.multiple_of(i * groups + step * span, span)
-        own = table_ref[pl.ds(start, span), :].astype(F32)
+        start = pl.multiple_of(i * groups + inside, span)
+        own = own_ref[pl.ds(start, span), :].astype(F32)
         gate = msg_ref[pl.ds(i, span, stride=8), :]
         atom = lax.broadcasted_iota(jnp.int32, (span, width), 0) + start
         out_ref[i] = jnp.where(atom < count_ref[0], own + gate, 0.0).astype(BF16)
 
 
-def messages(count, nbr, weights, feats, halos, wmsg):
-    slots, atoms = nbr.shape
-    width = feats.shape[1]
-    groups = atoms // 8
-    rows = atoms + 6 * halos[0].shape[0]
-    low = 256
-    span = min(64, groups)
-    whole = lambda *shape: pl.BlockSpec(shape, lambda b: (0,) * len(shape))
+def messages(low, count, adjacency, keys, own, halos, wmsg, slots):
+    groups = keys[0].shape[0]
+    atoms, width = own.shape
+    rows = adjacency.shape[1]
+    span = min(64, groups // 2)
+    vmem = pl.BlockSpec(memory_space=pltpu.VMEM)
+    arrays = [*keys, own, *halos, wmsg]
+    steps = groups // span
+    early = adjacency.shape[0] // (8 * span)
     out = pl.pallas_call(
-        functools.partial(message_kernel, low),
-        grid=(groups // span,),
-        in_specs=[
-            pl.BlockSpec(memory_space=pltpu.SMEM),
-            whole(slots, atoms),
-            whole(slots, atoms),
-            whole(atoms, width),
-            *[whole(*halo.shape) for halo in halos],
-            whole(width, width),
-        ],
-        out_specs=pl.BlockSpec((8, span, width), lambda b: (0, b, 0)),
+        functools.partial(message_kernel, low, span, slots),
+        grid=(steps,),
+        in_specs=[pl.BlockSpec(memory_space=pltpu.SMEM), pl.BlockSpec(memory_space=pltpu.HBM)]
+        + [vmem] * len(arrays),
+        out_specs=pl.BlockSpec((8, span, width), lambda b: (0, lax.rem(b + early, steps), 0)),
         out_shape=jax.ShapeDtypeStruct((8, groups, width), BF16),
         scratch_shapes=[
-            pltpu.VMEM((groups, 8 * slots), F32),
-            pltpu.VMEM((8 * slots, groups), F32),
-            pltpu.VMEM((groups, 8 * slots), F32),
-            pltpu.VMEM((rows, width), BF16),
-            pltpu.VMEM((8 * span, rows), BF16),
+            pltpu.VMEM((1 + early, 8 * span, rows), BF16),
             pltpu.VMEM((8 * span, width), F32),
+            pltpu.SemaphoreType.DMA((early,)),
         ],
-        compiler_params=pltpu.CompilerParams(vmem_limit_bytes=VMEM_LIMIT),
+        cost_estimate=pl.CostEstimate(flops=10**10, transcendentals=0, bytes_accessed=10**7),
+        compiler_params=pltpu.CompilerParams(vmem_limit_bytes=20 << 20),
         name="messages",
-    )(count, *in_hbm(nbr, weights, feats), *halos, *in_hbm(wmsg))
+    )(count, *in_hbm(adjacency), *arrays)
     return out.reshape(atoms, width)
 
 
@@ -391,7 +454,23 @@
     place = jnp.stack([lax.axis_index(axis) for axis in ("gx", "gy", "gz")]).astype(jnp.int32)
     paired = sizes[2] == 2
 
-    outgoing = selected(count, send_list.reshape(6, -1), feats)
+    scale = 1.0 / math.sqrt(atoms * devices)
+    table, *sums = phases(
+        place, count, sizes, scale, positions.reshape(3, atoms), feats, kvec, sigma, w_mix
+    )
+    low = 256
+    nbr, _ = lax.optimization_barrier((neighbours.reshape(slots, atoms), sums))
+    keys = prepared(low, nbr, edge_weight.reshape(slots, atoms))
+    if paired:
+        mine = sums[1] + passed_along(sums[0], "gz", 1)
+    else:
+        parts = lax.all_to_all(sums[0], "gz", 0, 0, tiled=True)
+        mine = jnp.sum(parts.reshape(sizes[2], -1, width), axis=0)
+    part = mine.shape[0] // plane
+    mine, keys, send, feats = lax.optimization_barrier((mine, keys, send_list, feats))
+
+    received = lax.all_to_all(mine.reshape(plane, part, width), ("gx", "gy"), 0, 0, tiled=True)
+    *outgoing, own = selected(count, send.reshape(6, 1, -1), feats)
     halos = [
         passed_along(outgoing[2 * number + side], axis, 1 - 2 * side)
         for number, axis in enumerate(("gx", "gy"))
@@ -401,27 +480,14 @@
         halos.append(passed_along(outgoing[4], "gz", 1))
     else:
         halos.append(jnp.stack([passed_along(outgoing[4][side], "gz", 1 - 2 * side) for side in range(2)]))
-    positions, _ = lax.optimization_barrier((positions, outgoing))
-    scale = 1.0 / math.sqrt(atoms * devices)
-    table, *sums = phases(
-        place, count, sizes, scale, positions.reshape(3, atoms), feats, kvec, sigma, w_mix
-    )
-    if paired:
-        mine = sums[1] + passed_along(sums[0], "gz", 1)
-    else:
-        parts = lax.all_to_all(sums[0], "gz", 0, 0, tiled=True)
-        mine = jnp.sum(parts.reshape(sizes[2], -1, width), axis=0)
-    mine, halos = lax.optimization_barrier((mine, halos))
-    part = mine.shape[0] // plane
-    received = lax.all_to_all(mine.reshape(plane, part, width), ("gx", "gy"), 0, 0, tiled=True)
-
-    neighbours, _ = lax.optimization_barrier((neighbours, mine))
-    updated = messages(
-        count, neighbours.reshape(slots, atoms), edge_weight.reshape(slots, atoms), feats, halos, w_message
-    )
-
-    received, updated = lax.optimization_barrier((received, updated))
-    g = lax.all_to_all(totals(received), ("gx", "gy"), 0, 0, tiled=True).reshape(plane * part, width)
+    adjacency = built(low, keys, atoms + send.size, atoms // 8 // 4 * EARLY)
+    received, halos, adjacency = lax.optimization_barrier((received, halos, adjacency))
+
+    shares = totals(received)
+    g = lax.all_to_all(shares, ("gx", "gy"), 0, 0, tiled=True).reshape(plane * part, width)
+    halos, _ = lax.optimization_barrier((halos, shares))
+    updated = messages(low, count, adjacency, keys, own, halos, w_message, slots)
+    g, updated = lax.optimization_barrier((g, updated))
     if paired:
         gs = [passed_along(g, "gz", 1), g]
     else:

time: 71.4 us -> 65.9 us (0.923)
  blocking collectives: 15.2 us -> 0 us
  starting transfers between devices: 13.3 us -> 20.3 us
  Pallas kernels: 36.2 us -> 39.6 us
  waiting for transfers between devices: 3.91 us -> 3.11 us
    all_to_all x1 -> x0, blocking collectives: 15.2 us -> none  [shards(): lax.all_to_all(totals(received), ('gx', 'gy'), 0, 0, tiled=True)]
    all_to_all x0 -> x1, starting transfers between devices: none -> 4.65 us  [shards(): lax.all_to_all(shares, ('gx', 'gy'), 0, 0, tiled=True)]
    all_to_all x1, starting transfers between devices: 4.84 us -> 8.24 us  [shards(): lax.all_to_all(mine.reshape(plane, part, width), ('gx', 'gy'), 0, 0, tile...]
    pallas_call x1 -> x3, Pallas kernels: 14.2 us -> 16.4 us  [the longest x1 9.64 us: messages(): pl.pallas_call(functools.partial(message_kernel, low, span, slots), grid=...]
    ppermute x7, waiting for transfers between devices: 3.91 us -> 1.91 us  [passed_along(): return lax.ppermute(value, axis, pairs)]
    all_to_all x1, waiting for transfers between devices: 0.01 us -> 1.2 us  [shards(): lax.all_to_all(mine.reshape(plane, part, width), ('gx', 'gy'), 0, 0, tile...]
    ppermute x7, starting transfers between devices: 8.49 us -> 7.39 us  [passed_along(): return lax.ppermute(value, axis, pairs)]
  transfers between devices with their start and end apart: 8 -> 9, of which waited for: 3 -> 3; matrix products, arithmetic and copies ran while one was open for 1% -> 0% of each run, Pallas kernels for 20% -> 30%
where the time goes in v3:
time: 65.9 us; the launch traced here: 65.5 us
  Pallas kernels  39.6 us (60%)
  starting transfers between devices  20.3 us (31%)
  waiting for transfers between devices  3.11 us (5%)
  between operations  1.55 us (2%)
  other arithmetic  0.92 us (1%)
    pallas_call x1, Pallas kernels, phases(): pl.pallas_call(functools.partial(phase_kernel, sizes, scale, paired), gri...  13.7 us
    pallas_call x1, Pallas kernels, messages(): pl.pallas_call(functools.partial(message_kernel, low, span, slots), grid=...  9.64 us
    all_to_all x1, starting transfers between devices, shards(): lax.all_to_all(mine.reshape(plane, part, width), ('gx', 'gy'), 0, 0, tile...  8.24 us
    ppermute x7, starting transfers between devices, passed_along(): return lax.ppermute(value, axis, pairs)  7.39 us
    pallas_call x1, Pallas kernels, back(): pl.pallas_call(functools.partial(back_kernel, scale), in_specs=[pl.BlockS...  5.67 us
    pallas_call x1, Pallas kernels, built(): pl.pallas_call(functools.partial(build_kernel, low, span), grid=(here //...  5.56 us
    all_to_all x1, starting transfers between devices, shards(): lax.all_to_all(shares, ('gx', 'gy'), 0, 0, tiled=True)  4.65 us
    pallas_call x1, Pallas kernels, selected(): pl.pallas_call(select_kernel, in_specs=[pl.BlockSpec(memory_space=pltpu.S...  3.12 us
  transfers between devices with their start and end apart: 9, of which 3 were waited for; matrix products, arithmetic and copies ran while one was open for 0% of the time, Pallas kernels for 30%

profile of v3, /device:TPU:0, one launch (start us, length us, event | category | flops | bytes accessed | tf_op | source)
XLA Modules:
  0.0 65.5 jit_solution(17572383186906748871)
XLA Ops:
  0.6 0.0 copy-start
  1.3 0.1 pad_add_fusion.place_ref
  1.4 13.7 %phases.1 = (bf16[2048,2048]{1,0:T(8,128)(2,1)}, f32[1024,128]{1,0:T(8,128)S(1)}, f32[1024,128]{1,0:T(8,128)S(1)}) custom-call(s32[3]{0:T(128)S(1)} %pad_add_fusion.place_ref, s32[1]{0:T(128)} %bitcast.15.count_ref, f32[3,1,2048]{2,1,0:T(1,128)} %bitcast.26, bf16[2048,128]{1,0:T(8,128)(2,1)} %bitcast.21, s32[3,1024]{1,0:T(4,128)} %kvec_ref.1, ...), custom_call_target="tpu_custom_call" | custom-call | tf_op jit(solution)/shard_map/phases/pallas_call | solution.py:140
  15.1 0.5 collective-permute-start
  15.5 1.2 %prepared.1 = (f32[256,256]{1,0:T(8,128)S(1)}, f32[256,256]{1,0:T(8,128)S(1)}, f32[256,256]{1,0:T(8,128)S(1)}) custom-call(s32[32,2048]{1,0:T(8,128)} %bitcast.24, bf16[32,2048]{1,0:T(8,128)(2,1)} %bitcast.25), custom_call_target="tpu_custom_call" | custom-call | tf_op jit(solution)/shard_map/prepared/pallas_call | solution.py:246
  16.7 0.4 collective-permute-done
  17.1 0.8 %add.3 = f32[1024,128]{1,0:T(8,128)} add(f32[1024,128]{1,0:T(8,128)S(1)} %get-tuple-element.35, f32[1024,128]{1,0:T(8,128)S(1)} %collective-permute-done) | non-fusion elementwise | flops 131072 | bytes 1572864 | tf_op jit(solution)/shard_map/add | solution.py:465
  17.9 8.2 %all-to-all-start = ((f32[16,64,128]{2,1,0:T(8,128)}), f32[16,64,128]{2,1,0:T(8,128)S(1)}, u32[]{:S(2)}, u32[]{:S(2)}) async-start(f32[16,64,128]{2,1,0:T(8,128)} %bitcast.9), calls=%async_computation | async-start | bytes 1048576 | tf_op jit(solution)/shard_map/all_to_all | solution.py:472
  26.2 3.1 %selected.1 = (bf16[256,128]{1,0:T(8,128)(2,1)S(1)}, bf16[256,128]{1,0:T(8,128)(2,1)S(1)}, bf16[256,128]{1,0:T(8,128)(2,1)S(1)}, bf16[256,128]{1,0:T(8,128)(2,1)...) custom-call(s32[1]{0:T(128)} %bitcast.16.count_ref, s32[6,1,256]{2,1,0:T(1,128)} %bitcast.27, ...), custom_call_target="tpu_custom_call" | custom-call | tf_op jit(solution)/shard_map/selected/pallas_call | solution.py:193
  29.3 0.1 collective-permute-start.5
  29.4 2.0 %collective-permute-start.1 = (bf16[256,128]{1,0:T(8,128)(2,1)S(1)}, bf16[256,128]{1,0:T(8,128)(2,1)S(1)}, u32[]{:S(2)}, u32[]{:S(2)}) collective-permute-start(bf16[256,128]{1,0:T(8,128)(2,1)S(1)} %get-tuple-element.44), channel_id=1, source_target_pairs={{0,8},{8,16},{16,24},{24,0},{1,9},{9,17},{17,25},{25,1},{2,10},{10... | collective-permute-start | bytes 196616 | tf_op jit(solution)/shard_map/ppermute | solution.py:439
  31.3 1.9 %collective-permute-start.2 = (bf16[256,128]{1,0:T(8,128)(2,1)S(1)}, bf16[256,128]{1,0:T(8,128)(2,1)S(1)}, u32[]{:S(2)}, u32[]{:S(2)}) collective-permute-start(bf16[256,128]{1,0:T(8,128)(2,1)S(1)} %get-tuple-element.45), channel_id=1, source_target_pairs={{0,24},{8,0},{16,8},{24,16},{1,25},{9,1},{17,9},{25,17},{2,26},{10... | collective-permute-start | bytes 196616 | tf_op jit(solution)/shard_map/ppermute | solution.py:439
  33.2 1.9 %collective-permute-start.3 = (bf16[256,128]{1,0:T(8,128)(2,1)S(1)}, bf16[256,128]{1,0:T(8,128)(2,1)S(1)}, u32[]{:S(2)}, u32[]{:S(2)}) collective-permute-start(bf16[256,128]{1,0:T(8,128)(2,1)S(1)} %get-tuple-element.46), channel_id=1, source_target_pairs={{0,2},{2,4},{4,6},{6,0},{1,3},{3,5},{5,7},{7,1},{8,10},{10,12},{12... | collective-permute-start | bytes 196616 | tf_op jit(solution)/shard_map/ppermute | solution.py:439
  35.2 1.0 %collective-permute-start.4 = (bf16[256,128]{1,0:T(8,128)(2,1)S(1)}, bf16[256,128]{1,0:T(8,128)(2,1)S(1)}, u32[]{:S(2)}, u32[]{:S(2)}) collective-permute-start(bf16[256,128]{1,0:T(8,128)(2,1)S(1)} %get-tuple-element.47), channel_id=1, source_target_pairs={{0,6},{2,0},{4,2},{6,4},{1,7},{3,1},{5,3},{7,5},{8,14},{10,8},{12,... | collective-permute-start | bytes 196616 | tf_op jit(solution)/shard_map/ppermute | solution.py:439
  36.2 5.6 %built.1.adj_hbm = bf16[1024,3584]{1,0:T(8,128)(2,1)} custom-call(f32[256,256]{1,0:T(8,128)S(1)} %get-tuple-element.49.high_key, f32[256,256]{1,0:T(8,128)S(1)} %get-tuple-element.50.low_key, f32[256,256]{1,0:T(8,128)S(1)} %get-tuple-element.51.edge), custom_call_target="tpu_custom_call" | custom-call | tf_op jit(solution)/shard_map/built/pallas_call | solution.py:305
  41.7 0.0 collective-permute-done.1.refs_0_
  41.7 0.0 collective-permute-done.2.refs_1_
  41.7 0.0 collective-permute-done.3.refs_2_
  41.7 0.0 collective-permute-done.4.refs_3_
  41.7 0.0 collective-permute-done.5.refs_4_
  41.7 1.2 %all-to-all-done.parts_ref = f32[16,64,128]{2,1,0:T(8,128)S(1)} async-done(((f32[16,64,128]{2,1,0:T(8,128)}), f32[16,64,128]{2,1,0:T(8,128)S(1)}, u32[]{:S(2)}, u32[]{:S(2)}) %all-to-all-start) | async-done | bytes 524320 | tf_op jit(solution)/shard_map/all_to_all | solution.py:472
  43.0 0.7 %totals.1 = bf16[16,64,128]{2,1,0:T(8,128)(2,1)} custom-call(f32[16,64,128]{2,1,0:T(8,128)S(1)} %all-to-all-done.parts_ref), custom_call_target="tpu_custom_call" | custom-call | tf_op jit(solution)/shard_map/totals/pallas_call | solution.py:218
  43.7 4.6 %all-to-all-start.1 = ((bf16[16,64,128]{2,1,0:T(8,128)(2,1)}), bf16[16,64,128]{2,1,0:T(8,128)(2,1)S(1)}, u32[]{:S(2)}, u32[]{:S(2)}) async-start(bf16[16,64,128]{2,1,0:T(8,128)(2,1)} %totals.1), calls=%async_computation.1 | async-start | bytes 524288 | tf_op jit(solution)/shard_map/all_to_all | solution.py:487
  48.4 0.0 copy-done
  48.4 9.6 %messages.1 = bf16[8,256,128]{2,1,0:T(8,128)(2,1)} custom-call(s32[1]{0:T(128)} %bitcast.17.count_ref, bf16[1024,3584]{1,0:T(8,128)(2,1)} %built.1.adj_hbm, f32[256,256]{1,0:T(8,128)S(1)} %get-tuple-element.49.high_key, f32[256,256]{1,0:T(8,128)S(1)} %get-tuple-element.50.low_key, f32[256,256]{1,0:T(8,128)S(1)} %get-tuple-element.51.edge, ...), custom_call_target="tpu_custom_call" | custom-call | flops 10000000000 | bytes 10000000 | tf_op jit(solution)/shard_map/messages/pallas_call | solution.py:373
  58.0 0.0 all-to-all-done.1
  58.0 0.1 collective-permute-start.6
  58.1 1.5 %collective-permute-done.6.refs_0_ = bf16[1024,128]{1,0:T(8,128)(2,1)S(1)} collective-permute-done((bf16[1024,128]{1,0:T(8,128)(2,1)S(1)}, bf16[1024,128]{1,0:T(8,128)(2,1)S(1)}, u32[]{:S(2)}, u32[]{:S(2)}) %collective-permute-start.6) | collective-permute-done | bytes 262176 | tf_op jit(solution)/shard_map/ppermute | solution.py:439
  59.6 5.7 %back.1 = f32[2048,128]{1,0:T(8,128)} custom-call(s32[1]{0:T(128)} %bitcast.18.count_ref, bf16[2048,2048]{1,0:T(8,128)(2,1)} %get-tuple-element.66.table_hbm, bf16[1024,128]{1,0:T(8,128)(2,1)S(1)} %collective-permute-done.6.refs_0_, bf16[1024,128]{1,0:T(8,128)(2,1)S(1)} %bitcast.20), custom_call_target="tpu_custom_call" | custom-call | tf_op jit(solution)/shard_map/back/pallas_call | solution.py:421
Async XLA Ops:
  0.6 47.7 %copy-start = (bf16[128,128]{1,0:T(8,128)(2,1)S(1)}, bf16[128,128]{1,0:T(8,128)(2,1)}, u32[]{:S(2)}) copy-start(bf16[128,128]{1,0:T(8,128)(2,1)} %refs_5_.1) | copy-start | bytes 98308
  15.1 2.0 %collective-permute-start = (f32[1024,128]{1,0:T(8,128)S(1)}, f32[1024,128]{1,0:T(8,128)S(1)}, u32[]{:S(2)}, u32[]{:S(2)}) collective-permute-start(f32[1024,128]{1,0:T(8,128)S(1)} %get-tuple-element.36), channel_id=1, source_target_pairs={{0,1},{1,0},{2,3},{3,2},{4,5},{5,4},{6,7},{7,6},{8,9},{9,8},{10,11... | collective-permute-start | bytes 1572872 | tf_op jit(solution)/shard_map/ppermute | solution.py:439
  17.9 25.0 %all-to-all-start = ((f32[16,64,128]{2,1,0:T(8,128)}), f32[16,64,128]{2,1,0:T(8,128)S(1)}, u32[]{:S(2)}, u32[]{:S(2)}) async-start(f32[16,64,128]{2,1,0:T(8,128)} %bitcast.9), calls=%async_computation | async-start | bytes 1048576 | tf_op jit(solution)/shard_map/all_to_all | solution.py:472
  29.3 12.5 %collective-permute-start.5 = (bf16[2,256,128]{2,1,0:T(8,128)(2,1)S(1)}, bf16[2,256,128]{2,1,0:T(8,128)(2,1)S(1)}, u32[]{:S(2)}, u32[]{:S(2)}) collective-permute-start(bf16[2,256,128]{2,1,0:T(8,128)(2,1)S(1)} %get-tuple-element.48), channel_id=1, source_target_pairs={{0,1},{1,0},{2,3},{3,2},{4,5},{5,4},{6,7},{7,6},{8,9},{9,8},{10,11... | collective-permute-start | bytes 393224 | tf_op jit(solution)/shard_map/ppermute | solution.py:439
  29.4 12.4 %collective-permute-start.1 = (bf16[256,128]{1,0:T(8,128)(2,1)S(1)}, bf16[256,128]{1,0:T(8,128)(2,1)S(1)}, u32[]{:S(2)}, u32[]{:S(2)}) collective-permute-start(bf16[256,128]{1,0:T(8,128)(2,1)S(1)} %get-tuple-element.44), channel_id=1, source_target_pairs={{0,8},{8,16},{16,24},{24,0},{1,9},{9,17},{17,25},{25,1},{2,10},{10... | collective-permute-start | bytes 196616 | tf_op jit(solution)/shard_map/ppermute | solution.py:439
  31.3 10.4 %collective-permute-start.2 = (bf16[256,128]{1,0:T(8,128)(2,1)S(1)}, bf16[256,128]{1,0:T(8,128)(2,1)S(1)}, u32[]{:S(2)}, u32[]{:S(2)}) collective-permute-start(bf16[256,128]{1,0:T(8,128)(2,1)S(1)} %get-tuple-element.45), channel_id=1, source_target_pairs={{0,24},{8,0},{16,8},{24,16},{1,25},{9,1},{17,9},{25,17},{2,26},{10... | collective-permute-start | bytes 196616 | tf_op jit(solution)/shard_map/ppermute | solution.py:439
  33.2 8.5 %collective-permute-start.3 = (bf16[256,128]{1,0:T(8,128)(2,1)S(1)}, bf16[256,128]{1,0:T(8,128)(2,1)S(1)}, u32[]{:S(2)}, u32[]{:S(2)}) collective-permute-start(bf16[256,128]{1,0:T(8,128)(2,1)S(1)} %get-tuple-element.46), channel_id=1, source_target_pairs={{0,2},{2,4},{4,6},{6,0},{1,3},{3,5},{5,7},{7,1},{8,10},{10,12},{12... | collective-permute-start | bytes 196616 | tf_op jit(solution)/shard_map/ppermute | solution.py:439
  35.2 6.6 %collective-permute-start.4 = (bf16[256,128]{1,0:T(8,128)(2,1)S(1)}, bf16[256,128]{1,0:T(8,128)(2,1)S(1)}, u32[]{:S(2)}, u32[]{:S(2)}) collective-permute-start(bf16[256,128]{1,0:T(8,128)(2,1)S(1)} %get-tuple-element.47), channel_id=1, source_target_pairs={{0,6},{2,0},{4,2},{6,4},{1,7},{3,1},{5,3},{7,5},{8,14},{10,8},{12,... | collective-permute-start | bytes 196616 | tf_op jit(solution)/shard_map/ppermute | solution.py:439
  43.7 14.3 %all-to-all-start.1 = ((bf16[16,64,128]{2,1,0:T(8,128)(2,1)}), bf16[16,64,128]{2,1,0:T(8,128)(2,1)S(1)}, u32[]{:S(2)}, u32[]{:S(2)}) async-start(bf16[16,64,128]{2,1,0:T(8,128)(2,1)} %totals.1), calls=%async_computation.1 | async-start | bytes 524288 | tf_op jit(solution)/shard_map/all_to_all | solution.py:487
  58.0 1.6 %collective-permute-start.6 = (bf16[1024,128]{1,0:T(8,128)(2,1)S(1)}, bf16[1024,128]{1,0:T(8,128)(2,1)S(1)}, u32[]{:S(2)}, u32[]{:S(2)}) collective-permute-start(bf16[1024,128]{1,0:T(8,128)(2,1)S(1)} %bitcast.19), channel_id=1, source_target_pairs={{0,1},{1,0},{2,3},{3,2},{4,5},{5,4},{6,7},{7,6},{8,9},{9,8},{10,11... | collective-permute-start | bytes 786440 | tf_op jit(solution)/shard_map/ppermute | solution.py:439

commit v4 on v3

--- a/solution.py
+++ b/solution.py
@@ -55,7 +55,7 @@
     *refs,
 ):
     out_refs = refs[: 1 + paired]
-    frac_ref, own_ref, mix_turned, decay_ref = refs[1 + paired :]
+    frac_ref, own_ref, mix_turned, decay_ref, block_ref, sems = refs[1 + paired :]
     atoms, width = feat_ref.shape
     kblock = kvec_ref.shape[1]
     step = pl.program_id(0)
@@ -82,7 +82,21 @@
         + [jnp.zeros((7, kblock), F32)],
         axis=0,
     ).astype(BF16)
-    chunk = min(256, atoms)
+    chunk = atoms // sems.shape[1]
+    slot = lax.rem(step, 2)
+
+    def store(number, which, column):
+        rows = pl.ds(number * chunk, chunk)
+        columns = pl.ds(pl.multiple_of(column * 2 * kblock, 2 * kblock), 2 * kblock)
+        return pltpu.make_async_copy(
+            block_ref.at[which, rows], table_ref.at[rows, columns], sems.at[which, number]
+        )
+
+    @pl.when(step >= 2)
+    def _():
+        for number in range(atoms // chunk):
+            store(number, slot, step - 2).wait()
+
     for start in range(0, atoms, chunk):
         rows = slice(start, start + chunk)
         theta = jnp.dot(frac_ref[rows, :], weights, preferred_element_type=F32)
@@ -92,10 +106,11 @@
         odd = horner(ODD, u) * r
         cosine = (1.0 - odd * odd).astype(BF16)
         sine = (even * odd).astype(BF16)
-        table_ref[rows, :kblock] = cosine
-        table_ref[rows, kblock:] = sine
-
-    sums = jnp.dot(own_ref[...], table_ref[...], preferred_element_type=F32)
+        block_ref[slot, rows, :kblock] = cosine
+        block_ref[slot, rows, kblock:] = sine
+        store(start // chunk, slot, step).start()
+
+    sums = jnp.dot(own_ref[...], block_ref[slot], preferred_element_type=F32)
     ksq = jnp.sum(kvec * kvec, axis=0, keepdims=True)
     decay = jnp.exp(decay_ref[:, :1] * ksq)
     mixed = jnp.dot(
@@ -114,6 +129,12 @@
             out_refs[1][...] = result
     else:
         out_refs[0][...] = result
+
+    @pl.when(step == pl.num_programs(0) - 1)
+    def _():
+        for number in range(atoms // chunk):
+            store(number, 1 - slot, step - 1).wait()
+            store(number, slot, step).wait()
 
 
 def phases(place, count, sizes, scale, pos, feats, kvec, sigma, w_mix):
@@ -149,12 +170,14 @@
                 whole(1, width),
                 whole(width, width),
             ],
-            out_specs=[pl.BlockSpec((atoms, 2 * kblock), lambda b, *_: (0, b)), *out_specs],
+            out_specs=[pl.BlockSpec(memory_space=pltpu.HBM), *out_specs],
             scratch_shapes=[
                 pltpu.VMEM((atoms, 16), BF16),
                 pltpu.VMEM((width, atoms), BF16),
                 pltpu.VMEM((width, width), F32),
                 pltpu.VMEM((width, width), F32),
+                pltpu.VMEM((2, atoms, 2 * kblock), BF16),
+                pltpu.SemaphoreType.DMA((2, 8)),
             ],
         ),
         out_shape=[pltpu.HBM((atoms, 2 * kcount), BF16), *out_shape],
@@ -225,7 +248,8 @@
     )(parts)
 
 
-def prepare_kernel(low, nbr_ref, weight_ref, high_key, low_key, edge):
+def prepare_kernel(low, nbr_ref, weight_ref, wmsg_ref, high_key, low_key, edge, wmsg_out):
+    wmsg_out[...] = wmsg_ref[...]
     slots, atoms = nbr_ref.shape
     groups, lanes = high_key.shape
     stack = lambda ref: jnp.concatenate(
@@ -239,22 +263,23 @@
     edge[...] = stack(weight_ref).T
 
 
-def prepared(low, nbr, weights):
+def prepared(low, nbr, weights, wmsg):
     slots, atoms = nbr.shape
     lanes, groups = 8 * slots, atoms // 8
     whole = lambda *shape: pl.BlockSpec(shape, lambda: (0,) * len(shape))
     return pl.pallas_call(
         functools.partial(prepare_kernel, low),
-        in_specs=[whole(slots, atoms), whole(slots, atoms)],
-        out_specs=[pl.BlockSpec(memory_space=pltpu.VMEM)] * 3,
+        in_specs=[whole(slots, atoms), whole(slots, atoms), whole(*wmsg.shape)],
+        out_specs=[pl.BlockSpec(memory_space=pltpu.VMEM)] * 4,
         out_shape=[
             jax.ShapeDtypeStruct((groups, lanes), F32),
             jax.ShapeDtypeStruct((lanes, groups), F32),
             jax.ShapeDtypeStruct((groups, lanes), F32),
+            jax.ShapeDtypeStruct(wmsg.shape, BF16),
         ],
         compiler_params=pltpu.CompilerParams(vmem_limit_bytes=VMEM_LIMIT),
         name="prepared",
-    )(*in_hbm(nbr, weights))
+    )(*in_hbm(nbr, weights, wmsg))
 
 
 def build_adjacency(low, base, span, high_key, low_key, edge, store):
@@ -288,71 +313,79 @@
 
 
 class Store:
-    def __init__(self, ref, low):
-        self.ref, self.low, self.highs = ref, low, ref.shape[1] // low
+    def __init__(self, own_ref, halo_ref, low):
+        self.own_ref, self.halo_ref, self.low = own_ref, halo_ref, low
+        self.split = own_ref.shape[1] // low
+        self.highs = self.split + halo_ref.shape[1] // low
 
     def __call__(self, row, upper, block):
-        self.ref[row : row + 16, upper * self.low : (upper + 1) * self.low] = block
-
-
-def build_kernel(low, span, high_key, low_key, edge, adj_ref):
-    build_adjacency(low, pl.program_id(0) * span, span, high_key, low_key, edge, Store(adj_ref, low))
-
-
-def built(low, keys, rows, here):
-    span = min(32, here)
+        ref = self.own_ref if upper < self.split else self.halo_ref
+        upper -= 0 if upper < self.split else self.split
+        ref[row : row + 16, upper * self.low : (upper + 1) * self.low] = block
+
+
+def build_kernel(low, span, high_key, low_key, edge, own_ref, halo_adj, partial_ref, own_adj):
+    store = Store(own_adj, halo_adj, low)
+    build_adjacency(low, pl.program_id(0) * span, span, high_key, low_key, edge, store)
+    partial_ref[...] = jnp.dot(own_adj[...], own_ref[...], preferred_element_type=F32)
+
+
+def built(low, keys, own, halo_rows, here):
+    atoms, width = own.shape
+    span = min(64, here)
     vmem = pl.BlockSpec(memory_space=pltpu.VMEM)
     return pl.pallas_call(
         functools.partial(build_kernel, low, span),
         grid=(here // span,),
-        in_specs=[vmem] * 3,
-        out_specs=pl.BlockSpec((8 * span, rows), lambda b: (b, 0)),
-        out_shape=pltpu.HBM((8 * here, rows), BF16),
+        in_specs=[vmem] * 4,
+        out_specs=[
+            pl.BlockSpec((8 * span, halo_rows), lambda b: (b, 0)),
+            pl.BlockSpec((8 * span, width), lambda b: (b, 0)),
+        ],
+        out_shape=[pltpu.HBM((8 * here, halo_rows), BF16), jax.ShapeDtypeStruct((8 * here, width), F32)],
+        scratch_shapes=[pltpu.VMEM((8 * span, atoms), BF16)],
         compiler_params=pltpu.CompilerParams(vmem_limit_bytes=VMEM_LIMIT),
         name="built",
-    )(*keys)
+    )(*keys, own)
 
 
 def message_kernel(
-    low, span, slots, count_ref, adj_hbm, high_key, low_key, edge, own_ref, *refs
+    low, span, slots, early, count_ref, early_hbm, partial_ref, high_key, low_key, edge, own_ref, *refs
 ):
     halo_refs = [*refs[:4], refs[4].at[0], refs[4].at[1]]
-    wmsg_ref, out_ref, slots_ref, msg_ref, sems = refs[-5:]
+    wmsg_ref, out_ref, early_adj, own_adj, halo_adj, msg_ref, sem = refs[-7:]
     atoms, width = own_ref.shape
     groups = high_key.shape[0]
     step = pl.program_id(0)
     steps = pl.num_programs(0)
-    early = sems.shape[0]
-
-    def fetch(piece):
-        rows = pl.ds(piece * 8 * span, 8 * span)
-        return pltpu.make_async_copy(adj_hbm.at[rows], slots_ref.at[piece + 1], sems.at[piece])
+    halo = jnp.concatenate([ref[...] for ref in halo_refs], axis=0)
+    fetch = pltpu.make_async_copy(early_hbm, early_adj, sem)
 
     @pl.when(step == 0)
     def _():
-        for piece in range(early):
-            fetch(piece).start()
-
-    for piece in range(early):
-
-        @pl.when(step == steps - early + piece)
-        def _():
-            fetch(piece).wait()
+        fetch.start()
+
+    @pl.when(step == steps - early)
+    def _():
+        fetch.wait()
 
     @pl.when(step < steps - early)
     def _():
-        start = (step + early) * span
-        build_adjacency(low, start, span, high_key, low_key, edge, Store(slots_ref.at[0], low))
-
-    base = lax.rem(step + early, steps) * span
-    adj_ref = slots_ref.at[jnp.maximum(step + early - steps + 1, 0)]
-    summed = jnp.dot(adj_ref[:, :atoms], own_ref[...], preferred_element_type=F32)
-    halo = jnp.concatenate([ref[...] for ref in halo_refs], axis=0)
-    summed += jnp.dot(adj_ref[:, atoms:], halo, preferred_element_type=F32)
-    message = (summed / math.sqrt(slots)).astype(BF16)
+        store = Store(own_adj, halo_adj, low)
+        build_adjacency(low, (step + early) * span, span, high_key, low_key, edge, store)
+        summed = jnp.dot(own_adj[...], own_ref[...], preferred_element_type=F32)
+        msg_ref[...] = summed + jnp.dot(halo_adj[...], halo, preferred_element_type=F32)
+
+    @pl.when(step >= steps - early)
+    def _():
+        rows = pl.ds(pl.multiple_of((step + early - steps) * 8 * span, 8 * span), 8 * span)
+        more = jnp.dot(early_adj[rows, :], halo, preferred_element_type=F32)
+        msg_ref[...] = partial_ref[rows, :] + more
+
+    message = (msg_ref[...] / math.sqrt(slots)).astype(BF16)
     hidden = jnp.dot(message, wmsg_ref[...], preferred_element_type=F32)
     msg_ref[...] = hidden / (1.0 + jnp.exp(-hidden))
-    inside = pl.multiple_of(base, span)
+    inside = pl.multiple_of(lax.rem(step + early, steps) * span, span)
     for i in range(8):
         start = pl.multiple_of(i * groups + inside, span)
         own = own_ref[pl.ds(start, span), :].astype(F32)
@@ -361,36 +394,37 @@
         out_ref[i] = jnp.where(atom < count_ref[0], own + gate, 0.0).astype(BF16)
 
 
-def messages(low, count, adjacency, keys, own, halos, wmsg, slots):
+def messages(low, count, early_adj, partial, keys, own, halos, wmsg, slots):
     groups = keys[0].shape[0]
     atoms, width = own.shape
-    rows = adjacency.shape[1]
-    span = min(64, groups // 2)
+    halo_rows = early_adj.shape[1]
+    span = min(64, groups // 4)
     vmem = pl.BlockSpec(memory_space=pltpu.VMEM)
-    arrays = [*keys, own, *halos, wmsg]
+    arrays = [partial, *keys, own, *halos, wmsg]
     steps = groups // span
-    early = adjacency.shape[0] // (8 * span)
+    early = early_adj.shape[0] // (8 * span)
     out = pl.pallas_call(
-        functools.partial(message_kernel, low, span, slots),
+        functools.partial(message_kernel, low, span, slots, early),
         grid=(steps,),
         in_specs=[pl.BlockSpec(memory_space=pltpu.SMEM), pl.BlockSpec(memory_space=pltpu.HBM)]
         + [vmem] * len(arrays),
         out_specs=pl.BlockSpec((8, span, width), lambda b: (0, lax.rem(b + early, steps), 0)),
         out_shape=jax.ShapeDtypeStruct((8, groups, width), BF16),
         scratch_shapes=[
-            pltpu.VMEM((1 + early, 8 * span, rows), BF16),
+            pltpu.VMEM(early_adj.shape, BF16),
+            pltpu.VMEM((8 * span, atoms), BF16),
+            pltpu.VMEM((8 * span, halo_rows), BF16),
             pltpu.VMEM((8 * span, width), F32),
-            pltpu.SemaphoreType.DMA((early,)),
+            pltpu.SemaphoreType.DMA,
         ],
-        cost_estimate=pl.CostEstimate(flops=10**10, transcendentals=0, bytes_accessed=10**7),
-        compiler_params=pltpu.CompilerParams(vmem_limit_bytes=20 << 20),
+        compiler_params=pltpu.CompilerParams(vmem_limit_bytes=VMEM_LIMIT),
         name="messages",
-    )(count, *in_hbm(adjacency), *arrays)
+    )(count, *in_hbm(early_adj), *arrays)
     return out.reshape(atoms, width)
 
 
 def back_kernel(scale, count_ref, table_hbm, *refs):
-    *g_refs, out_ref, table_ref, sems = refs
+    *g_refs, out_hbm, table_ref, out_ref, sems, out_sems = refs
     atoms, width = out_ref.shape
     pieces = sems.shape[0]
     rows = atoms // pieces
@@ -412,6 +446,11 @@
             start += depth
         atom = lax.broadcasted_iota(jnp.int32, (rows, width), 0) + piece * rows
         out_ref[here, :] = jnp.where(atom < count_ref[0], back * scale, 0.0)
+        here = pl.ds(piece * rows, rows)
+        copies.append(pltpu.make_async_copy(out_ref.at[here], out_hbm.at[here], out_sems.at[piece]))
+        copies[-1].start()
+    for copy in copies[pieces:]:
+        copy.wait()
 
 
 def back(count, table, gs, scale):
@@ -425,9 +464,14 @@
             pl.BlockSpec(memory_space=pltpu.HBM),
             *[vmem for _ in gs],
         ],
-        out_specs=vmem,
-        out_shape=jax.ShapeDtypeStruct((atoms, width), F32),
-        scratch_shapes=[pltpu.VMEM((atoms, depth), BF16), pltpu.SemaphoreType.DMA((8,))],
+        out_specs=pl.BlockSpec(memory_space=pltpu.HBM),
+        out_shape=pltpu.HBM((atoms, width), F32),
+        scratch_shapes=[
+            pltpu.VMEM((atoms, depth), BF16),
+            pltpu.VMEM((atoms, width), F32),
+            pltpu.SemaphoreType.DMA((8,)),
+            pltpu.SemaphoreType.DMA((8,)),
+        ],
         compiler_params=pltpu.CompilerParams(vmem_limit_bytes=VMEM_LIMIT),
         name="back",
     )(count, *in_hbm(table), *gs)
@@ -460,14 +504,14 @@
     )
     low = 256
     nbr, _ = lax.optimization_barrier((neighbours.reshape(slots, atoms), sums))
-    keys = prepared(low, nbr, edge_weight.reshape(slots, atoms))
+    *keys, wmsg = prepared(low, nbr, edge_weight.reshape(slots, atoms), w_message)
     if paired:
         mine = sums[1] + passed_along(sums[0], "gz", 1)
     else:
         parts = lax.all_to_all(sums[0], "gz", 0, 0, tiled=True)
         mine = jnp.sum(parts.reshape(sizes[2], -1, width), axis=0)
     part = mine.shape[0] // plane
-    mine, keys, send, feats = lax.optimization_barrier((mine, keys, send_list, feats))
+    mine, keys, wmsg, send, feats = lax.optimization_barrier((mine, keys, wmsg, send_list, feats))
 
     received = lax.all_to_all(mine.reshape(plane, part, width), ("gx", "gy"), 0, 0, tiled=True)
     *outgoing, own = selected(count, send.reshape(6, 1, -1), feats)
@@ -480,13 +524,13 @@
         halos.append(passed_along(outgoing[4], "gz", 1))
     else:
         halos.append(jnp.stack([passed_along(outgoing[4][side], "gz", 1 - 2 * side) for side in range(2)]))
-    adjacency = built(low, keys, atoms + send.size, atoms // 8 // 4 * EARLY)
+    adjacency = built(low, keys, own, send.size, atoms // 8 // 4 * EARLY)
     received, halos, adjacency = lax.optimization_barrier((received, halos, adjacency))
 
     shares = totals(received)
     g = lax.all_to_all(shares, ("gx", "gy"), 0, 0, tiled=True).reshape(plane * part, width)
     halos, _ = lax.optimization_barrier((halos, shares))
-    updated = messages(low, count, adjacency, keys, own, halos, w_message, slots)
+    updated = messages(low, count, *adjacency, keys, own, halos, wmsg, slots)
     g, updated = lax.optimization_barrier((g, updated))
     if paired:
         gs = [passed_along(g, "gz", 1), g]

time: 65.9 us -> 64.5 us (0.979)
  Pallas kernels: 39.6 us -> 37.3 us
  waiting for transfers between devices: 3.11 us -> 4.11 us
    pallas_call x1, Pallas kernels: 13.7 us -> 12.7 us  [phases(): pl.pallas_call(functools.partial(phase_kernel, sizes, scale, paired), gri...]
    pallas_call x1, Pallas kernels: 9.64 us -> 8.8 us  [messages(): pl.pallas_call(functools.partial(message_kernel, low, span, slots, early)...]
    all_to_all x1, waiting for transfers between devices: 0.01 us -> 0.71 us  [shards(): lax.all_to_all(shares, ('gx', 'gy'), 0, 0, tiled=True)]
  transfers between devices with their start and end apart: 9 -> 9, of which waited for: 3 -> 4; matrix products, arithmetic and copies ran while one was open for 0% -> 0% of each run, Pallas kernels for 30% -> 29%
where the time goes in v4:
time: 64.5 us; the launch traced here: 64.1 us
  Pallas kernels  37.3 us (58%)
  starting transfers between devices  20.3 us (31%)
  waiting for transfers between devices  4.11 us (6%)
  between operations  1.52 us (2%)
  other arithmetic  0.92 us (1%)
    pallas_call x1, Pallas kernels, phases(): pl.pallas_call(functools.partial(phase_kernel, sizes, scale, paired), gri...  12.7 us
    pallas_call x1, Pallas kernels, messages(): pl.pallas_call(functools.partial(message_kernel, low, span, slots, early)...  8.8 us
    all_to_all x1, starting transfers between devices, shards(): lax.all_to_all(mine.reshape(plane, part, width), ('gx', 'gy'), 0, 0, tile...  8.23 us
    ppermute x7, starting transfers between devices, passed_along(): return lax.ppermute(value, axis, pairs)  7.4 us
    pallas_call x1, Pallas kernels, back(): pl.pallas_call(functools.partial(back_kernel, scale), in_specs=[pl.BlockS...  5.43 us
    pallas_call x1, Pallas kernels, built(): pl.pallas_call(functools.partial(build_kernel, low, span), grid=(here //...  5.24 us
    all_to_all x1, starting transfers between devices, shards(): lax.all_to_all(shares, ('gx', 'gy'), 0, 0, tiled=True)  4.65 us
    pallas_call x1, Pallas kernels, selected(): pl.pallas_call(select_kernel, in_specs=[pl.BlockSpec(memory_space=pltpu.S...  3.11 us
  transfers between devices with their start and end apart: 9, of which 4 were waited for; matrix products, arithmetic and copies ran while one was open for 0% of the time, Pallas kernels for 29%

profile of v4, /device:TPU:0, one launch (start us, length us, event | category | flops | bytes accessed | tf_op | source)
XLA Modules:
  0.0 64.1 jit_solution(997031970777452352)
XLA Ops:
  1.3 0.1 pad_add_fusion.place_ref
  1.4 12.7 %phases.1 = (bf16[2048,2048]{1,0:T(8,128)(2,1)}, f32[1024,128]{1,0:T(8,128)S(1)}, f32[1024,128]{1,0:T(8,128)S(1)}) custom-call(s32[3]{0:T(128)S(1)} %pad_add_fusion.place_ref, s32[1]{0:T(128)} %bitcast.15.count_ref, f32[3,1,2048]{2,1,0:T(1,128)} %bitcast.27, bf16[2048,128]{1,0:T(8,128)(2,1)} %bitcast.21, s32[3,1024]{1,0:T(4,128)} %kvec_ref.1, ...), custom_call_target="tpu_custom_call" | custom-call | tf_op jit(solution)/shard_map/phases/pallas_call | solution.py:161
  14.1 0.5 collective-permute-start
  14.6 1.2 %prepared.1 = (f32[256,256]{1,0:T(8,128)S(1)}, f32[256,256]{1,0:T(8,128)S(1)}, f32[256,256]{1,0:T(8,128)S(1)}, bf16[128,128]{1,0:T(8,128)(2,1)S(1)}) custom-call(s32[32,2048]{1,0:T(8,128)} %bitcast.25, bf16[32,2048]{1,0:T(8,128)(2,1)} %bitcast.26, bf16[128,128]{1,0:T(8,128)(2,1)} %wmsg_ref.1), custom_call_target="tpu_custom_call" | custom-call | tf_op jit(solution)/shard_map/prepared/pallas_call | solution.py:270
  15.8 0.3 collective-permute-done
  16.2 0.8 %add.3 = f32[1024,128]{1,0:T(8,128)} add(f32[1024,128]{1,0:T(8,128)S(1)} %get-tuple-element.40, f32[1024,128]{1,0:T(8,128)S(1)} %collective-permute-done) | non-fusion elementwise | flops 131072 | bytes 1572864 | tf_op jit(solution)/shard_map/add | solution.py:509
  17.0 8.2 %all-to-all-start = ((f32[16,64,128]{2,1,0:T(8,128)}), f32[16,64,128]{2,1,0:T(8,128)S(1)}, u32[]{:S(2)}, u32[]{:S(2)}) async-start(f32[16,64,128]{2,1,0:T(8,128)} %bitcast.9), calls=%async_computation | async-start | bytes 1048576 | tf_op jit(solution)/shard_map/all_to_all | solution.py:516
  25.3 3.1 %selected.1 = (bf16[256,128]{1,0:T(8,128)(2,1)S(1)}, bf16[256,128]{1,0:T(8,128)(2,1)S(1)}, bf16[256,128]{1,0:T(8,128)(2,1)S(1)}, bf16[256,128]{1,0:T(8,128)(2,1)...) custom-call(s32[1]{0:T(128)} %bitcast.16.count_ref, s32[6,1,256]{2,1,0:T(1,128)} %bitcast.28, ...), custom_call_target="tpu_custom_call" | custom-call | tf_op jit(solution)/shard_map/selected/pallas_call | solution.py:216
  28.4 0.1 collective-permute-start.5
  28.5 2.0 %collective-permute-start.1 = (bf16[256,128]{1,0:T(8,128)(2,1)S(1)}, bf16[256,128]{1,0:T(8,128)(2,1)S(1)}, u32[]{:S(2)}, u32[]{:S(2)}) collective-permute-start(bf16[256,128]{1,0:T(8,128)(2,1)S(1)} %get-tuple-element.50), channel_id=1, source_target_pairs={{0,8},{8,16},{16,24},{24,0},{1,9},{9,17},{17,25},{25,1},{2,10},{10... | collective-permute-start | bytes 196616 | tf_op jit(solution)/shard_map/ppermute | solution.py:483
  30.4 1.9 %collective-permute-start.2 = (bf16[256,128]{1,0:T(8,128)(2,1)S(1)}, bf16[256,128]{1,0:T(8,128)(2,1)S(1)}, u32[]{:S(2)}, u32[]{:S(2)}) collective-permute-start(bf16[256,128]{1,0:T(8,128)(2,1)S(1)} %get-tuple-element.51), channel_id=1, source_target_pairs={{0,24},{8,0},{16,8},{24,16},{1,25},{9,1},{17,9},{25,17},{2,26},{10... | collective-permute-start | bytes 196616 | tf_op jit(solution)/shard_map/ppermute | solution.py:483
  32.3 1.9 %collective-permute-start.3 = (bf16[256,128]{1,0:T(8,128)(2,1)S(1)}, bf16[256,128]{1,0:T(8,128)(2,1)S(1)}, u32[]{:S(2)}, u32[]{:S(2)}) collective-permute-start(bf16[256,128]{1,0:T(8,128)(2,1)S(1)} %get-tuple-element.52), channel_id=1, source_target_pairs={{0,2},{2,4},{4,6},{6,0},{1,3},{3,5},{5,7},{7,1},{8,10},{10,12},{12... | collective-permute-start | bytes 196616 | tf_op jit(solution)/shard_map/ppermute | solution.py:483
  34.3 1.0 %collective-permute-start.4 = (bf16[256,128]{1,0:T(8,128)(2,1)S(1)}, bf16[256,128]{1,0:T(8,128)(2,1)S(1)}, u32[]{:S(2)}, u32[]{:S(2)}) collective-permute-start(bf16[256,128]{1,0:T(8,128)(2,1)S(1)} %get-tuple-element.53), channel_id=1, source_target_pairs={{0,6},{2,0},{4,2},{6,4},{1,7},{3,1},{5,3},{7,5},{8,14},{10,8},{12,... | collective-permute-start | bytes 196616 | tf_op jit(solution)/shard_map/ppermute | solution.py:483
  35.3 5.2 %built.1 = (bf16[1024,1536]{1,0:T(8,128)(2,1)}, f32[1024,128]{1,0:T(8,128)S(1)}) custom-call(f32[256,256]{1,0:T(8,128)S(1)} %get-tuple-element.55.high_key, f32[256,256]{1,0:T(8,128)S(1)} %get-tuple-element.56.low_key, f32[256,256]{1,0:T(8,128)S(1)} %get-tuple-element.57.edge, bf16[2048,128]{1,0:T(8,128)(2,1)S(1)} %get-tuple-element.58.own_ref), custom_call_target="tpu_custom_call" | custom-call | tf_op jit(solution)/shard_map/built/pallas_call | solution.py:337
  40.5 0.0 collective-permute-done.1.refs_0_
  40.5 0.0 collective-permute-done.2.refs_1_
  40.5 0.0 collective-permute-done.3.refs_2_
  40.5 0.0 collective-permute-done.4.refs_3_
  40.5 0.0 collective-permute-done.5.refs_4_
  40.5 1.5 %all-to-all-done.parts_ref = f32[16,64,128]{2,1,0:T(8,128)S(1)} async-done(((f32[16,64,128]{2,1,0:T(8,128)}), f32[16,64,128]{2,1,0:T(8,128)S(1)}, u32[]{:S(2)}, u32[]{:S(2)}) %all-to-all-start) | async-done | bytes 524320 | tf_op jit(solution)/shard_map/all_to_all | solution.py:516
  42.1 0.7 %totals.1 = bf16[16,64,128]{2,1,0:T(8,128)(2,1)} custom-call(f32[16,64,128]{2,1,0:T(8,128)S(1)} %all-to-all-done.parts_ref), custom_call_target="tpu_custom_call" | custom-call | tf_op jit(solution)/shard_map/totals/pallas_call | solution.py:241
  42.8 4.6 %all-to-all-start.1 = ((bf16[16,64,128]{2,1,0:T(8,128)(2,1)}), bf16[16,64,128]{2,1,0:T(8,128)(2,1)S(1)}, u32[]{:S(2)}, u32[]{:S(2)}) async-start(bf16[16,64,128]{2,1,0:T(8,128)(2,1)} %totals.1), calls=%async_computation.1 | async-start | bytes 524288 | tf_op jit(solution)/shard_map/all_to_all | solution.py:531
  47.5 8.8 %messages.1 = bf16[8,256,128]{2,1,0:T(8,128)(2,1)} custom-call(s32[1]{0:T(128)} %bitcast.17.count_ref, bf16[1024,1536]{1,0:T(8,128)(2,1)} %get-tuple-element.62.early_hbm, f32[1024,128]{1,0:T(8,128)S(1)} %get-tuple-element.63.partial_ref, f32[256,256]{1,0:T(8,128)S(1)} %get-tuple-element.55.high_key, f32[256,256]{1,0:T(8,128)S(1)} %get-tuple-element.56.low_key, ...), custom_call_target="tpu_custom_call" | custom-call | tf_op jit(solution)/shard_map/messages/pallas_call | solution.py:406
  56.3 0.7 %all-to-all-done.1 = bf16[16,64,128]{2,1,0:T(8,128)(2,1)S(1)} async-done(((bf16[16,64,128]{2,1,0:T(8,128)(2,1)}), bf16[16,64,128]{2,1,0:T(8,128)(2,1)S(1)}, u32[]{:S(2)}, u32[]{:S(2)}) %all-to-all-start.1) | async-done | bytes 262176 | tf_op jit(solution)/shard_map/all_to_all | solution.py:531
  57.0 0.0 collective-permute-start.6
  57.0 1.5 %collective-permute-done.6.refs_0_ = bf16[1024,128]{1,0:T(8,128)(2,1)S(1)} collective-permute-done((bf16[1024,128]{1,0:T(8,128)(2,1)S(1)}, bf16[1024,128]{1,0:T(8,128)(2,1)S(1)}, u32[]{:S(2)}, u32[]{:S(2)}) %collective-permute-start.6) | collective-permute-done | bytes 262176 | tf_op jit(solution)/shard_map/ppermute | solution.py:483
  58.5 5.4 %back.1 = f32[2048,128]{1,0:T(8,128)} custom-call(s32[1]{0:T(128)} %bitcast.18.count_ref, bf16[2048,2048]{1,0:T(8,128)(2,1)} %get-tuple-element.76.table_hbm, bf16[1024,128]{1,0:T(8,128)(2,1)S(1)} %collective-permute-done.6.refs_0_, bf16[1024,128]{1,0:T(8,128)(2,1)S(1)} %bitcast.20), custom_call_target="tpu_custom_call" | custom-call | tf_op jit(solution)/shard_map/back/pallas_call | solution.py:460
Async XLA Ops:
  14.1 2.1 %collective-permute-start = (f32[1024,128]{1,0:T(8,128)S(1)}, f32[1024,128]{1,0:T(8,128)S(1)}, u32[]{:S(2)}, u32[]{:S(2)}) collective-permute-start(f32[1024,128]{1,0:T(8,128)S(1)} %get-tuple-element.41), channel_id=1, source_target_pairs={{0,1},{1,0},{2,3},{3,2},{4,5},{5,4},{6,7},{7,6},{8,9},{9,8},{10,11... | collective-permute-start | bytes 1572872 | tf_op jit(solution)/shard_map/ppermute | solution.py:483
  17.0 25.0 %all-to-all-start = ((f32[16,64,128]{2,1,0:T(8,128)}), f32[16,64,128]{2,1,0:T(8,128)S(1)}, u32[]{:S(2)}, u32[]{:S(2)}) async-start(f32[16,64,128]{2,1,0:T(8,128)} %bitcast.9), calls=%async_computation | async-start | bytes 1048576 | tf_op jit(solution)/shard_map/all_to_all | solution.py:516
  28.4 12.1 %collective-permute-start.5 = (bf16[2,256,128]{2,1,0:T(8,128)(2,1)S(1)}, bf16[2,256,128]{2,1,0:T(8,128)(2,1)S(1)}, u32[]{:S(2)}, u32[]{:S(2)}) collective-permute-start(bf16[2,256,128]{2,1,0:T(8,128)(2,1)S(1)} %get-tuple-element.54), channel_id=1, source_target_pairs={{0,1},{1,0},{2,3},{3,2},{4,5},{5,4},{6,7},{7,6},{8,9},{9,8},{10,11... | collective-permute-start | bytes 393224 | tf_op jit(solution)/shard_map/ppermute | solution.py:483
  28.5 12.0 %collective-permute-start.1 = (bf16[256,128]{1,0:T(8,128)(2,1)S(1)}, bf16[256,128]{1,0:T(8,128)(2,1)S(1)}, u32[]{:S(2)}, u32[]{:S(2)}) collective-permute-start(bf16[256,128]{1,0:T(8,128)(2,1)S(1)} %get-tuple-element.50), channel_id=1, source_target_pairs={{0,8},{8,16},{16,24},{24,0},{1,9},{9,17},{17,25},{25,1},{2,10},{10... | collective-permute-start | bytes 196616 | tf_op jit(solution)/shard_map/ppermute | solution.py:483
  30.4 10.1 %collective-permute-start.2 = (bf16[256,128]{1,0:T(8,128)(2,1)S(1)}, bf16[256,128]{1,0:T(8,128)(2,1)S(1)}, u32[]{:S(2)}, u32[]{:S(2)}) collective-permute-start(bf16[256,128]{1,0:T(8,128)(2,1)S(1)} %get-tuple-element.51), channel_id=1, source_target_pairs={{0,24},{8,0},{16,8},{24,16},{1,25},{9,1},{17,9},{25,17},{2,26},{10... | collective-permute-start | bytes 196616 | tf_op jit(solution)/shard_map/ppermute | solution.py:483
  32.3 8.2 %collective-permute-start.3 = (bf16[256,128]{1,0:T(8,128)(2,1)S(1)}, bf16[256,128]{1,0:T(8,128)(2,1)S(1)}, u32[]{:S(2)}, u32[]{:S(2)}) collective-permute-start(bf16[256,128]{1,0:T(8,128)(2,1)S(1)} %get-tuple-element.52), channel_id=1, source_target_pairs={{0,2},{2,4},{4,6},{6,0},{1,3},{3,5},{5,7},{7,1},{8,10},{10,12},{12... | collective-permute-start | bytes 196616 | tf_op jit(solution)/shard_map/ppermute | solution.py:483
  34.3 6.3 %collective-permute-start.4 = (bf16[256,128]{1,0:T(8,128)(2,1)S(1)}, bf16[256,128]{1,0:T(8,128)(2,1)S(1)}, u32[]{:S(2)}, u32[]{:S(2)}) collective-permute-start(bf16[256,128]{1,0:T(8,128)(2,1)S(1)} %get-tuple-element.53), channel_id=1, source_target_pairs={{0,6},{2,0},{4,2},{6,4},{1,7},{3,1},{5,3},{7,5},{8,14},{10,8},{12,... | collective-permute-start | bytes 196616 | tf_op jit(solution)/shard_map/ppermute | solution.py:483
  42.8 14.2 %all-to-all-start.1 = ((bf16[16,64,128]{2,1,0:T(8,128)(2,1)}), bf16[16,64,128]{2,1,0:T(8,128)(2,1)S(1)}, u32[]{:S(2)}, u32[]{:S(2)}) async-start(bf16[16,64,128]{2,1,0:T(8,128)(2,1)} %totals.1), calls=%async_computation.1 | async-start | bytes 524288 | tf_op jit(solution)/shard_map/all_to_all | solution.py:531
  57.0 1.5 %collective-permute-start.6 = (bf16[1024,128]{1,0:T(8,128)(2,1)S(1)}, bf16[1024,128]{1,0:T(8,128)(2,1)S(1)}, u32[]{:S(2)}, u32[]{:S(2)}) collective-permute-start(bf16[1024,128]{1,0:T(8,128)(2,1)S(1)} %bitcast.19), channel_id=1, source_target_pairs={{0,1},{1,0},{2,3},{3,2},{4,5},{5,4},{6,7},{7,6},{8,9},{9,8},{10,11... | collective-permute-start | bytes 786440 | tf_op jit(solution)/shard_map/ppermute | solution.py:483

commit v5 on v4

--- a/solution.py
+++ b/solution.py
@@ -11,7 +11,7 @@
 
 F32 = jnp.float32
 BF16 = jnp.bfloat16
-VMEM_LIMIT = 14 << 20
+VMEM_LIMIT = 18 << 20
 EARLY = 2
 
 
@@ -52,6 +52,7 @@
     sigma_ref,
     mix_ref,
     table_ref,
+    live_ref,
     *refs,
 ):
     out_refs = refs[: 1 + paired]
@@ -73,6 +74,7 @@
         atom = lax.broadcasted_iota(jnp.int32, (atoms, width), 0)
         own = jnp.where(atom < count_ref[0], feat_ref[...].astype(F32), 0.0)
         own_ref[...] = own.T.astype(BF16)
+        live_ref[...] = own.astype(BF16)
         mix_turned[...] = mix_ref[...].T
         decay_ref[...] = jnp.broadcast_to(-sigma_ref[...], (width, width)).T
 
@@ -140,7 +142,7 @@
 def phases(place, count, sizes, scale, pos, feats, kvec, sigma, w_mix):
     atoms, width = feats.shape
     kcount = kvec.shape[1]
-    kblock = 256 if kcount % 512 == 0 else 128
+    kblock = 512 if kcount % 1024 == 0 else 128
     steps = kcount // kblock
     half = steps // 2
     paired = sizes[2] == 2
@@ -170,7 +172,11 @@
                 whole(1, width),
                 whole(width, width),
             ],
-            out_specs=[pl.BlockSpec(memory_space=pltpu.HBM), *out_specs],
+            out_specs=[
+                pl.BlockSpec(memory_space=pltpu.HBM),
+                pl.BlockSpec(memory_space=pltpu.VMEM),
+                *out_specs,
+            ],
             scratch_shapes=[
                 pltpu.VMEM((atoms, 16), BF16),
                 pltpu.VMEM((width, atoms), BF16),
@@ -180,18 +186,19 @@
                 pltpu.SemaphoreType.DMA((2, 8)),
             ],
         ),
-        out_shape=[pltpu.HBM((atoms, 2 * kcount), BF16), *out_shape],
+        out_shape=[
+            pltpu.HBM((atoms, 2 * kcount), BF16),
+            jax.ShapeDtypeStruct((atoms, width), BF16),
+            *out_shape,
+        ],
         compiler_params=pltpu.CompilerParams(vmem_limit_bytes=VMEM_LIMIT),
         name="phases",
     )(place, count, *in_hbm(pos.reshape(3, 1, atoms), feats, kvec, sigma.reshape(1, width), w_mix))
 
 
-def select_kernel(count_ref, send_ref, feat_ref, *refs):
-    *out_refs, own_ref = refs
+def select_kernel(send_ref, own_ref, *out_refs):
     faces, _, picks = send_ref.shape
-    atoms, width = feat_ref.shape
-    atom = lax.broadcasted_iota(jnp.int32, (atoms, width), 0)
-    own_ref[...] = jnp.where(atom < count_ref[0], feat_ref[...].astype(F32), 0.0).astype(BF16)
+    atoms, width = own_ref.shape
     rows = jnp.concatenate([send_ref[face] for face in range(faces)], axis=0).astype(F32)
     columns = jnp.concatenate([rows, jnp.zeros((8 - faces, picks), F32)], axis=0).T
     chunk = min(256, atoms)
@@ -210,22 +217,21 @@
             out_refs[4][face - 4] = total.astype(BF16)
 
 
-def selected(count, send, feats):
-    atoms, width = feats.shape
+def selected(send, own):
+    width = own.shape[1]
     faces, _, picks = send.shape
     return pl.pallas_call(
         select_kernel,
         in_specs=[
-            pl.BlockSpec(memory_space=pltpu.SMEM),
             pl.BlockSpec((faces, 1, picks), lambda: (0, 0, 0)),
-            pl.BlockSpec((atoms, width), lambda: (0, 0)),
-        ],
-        out_specs=[pl.BlockSpec(memory_space=pltpu.VMEM)] * 6,
+            pl.BlockSpec(memory_space=pltpu.VMEM),
+        ],
+        out_specs=[pl.BlockSpec(memory_space=pltpu.VMEM)] * 5,
         out_shape=[jax.ShapeDtypeStruct((picks, width), BF16)] * 4
-        + [jax.ShapeDtypeStruct((2, picks, width), BF16), jax.ShapeDtypeStruct((atoms, width), BF16)],
+        + [jax.ShapeDtypeStruct((2, picks, width), BF16)],
         compiler_params=pltpu.CompilerParams(vmem_limit_bytes=VMEM_LIMIT),
         name="selected",
-    )(count, *in_hbm(send, feats))
+    )(*in_hbm(send), own)
 
 
 def total_kernel(parts_ref, out_ref):
@@ -499,7 +505,7 @@
     paired = sizes[2] == 2
 
     scale = 1.0 / math.sqrt(atoms * devices)
-    table, *sums = phases(
+    table, own, *sums = phases(
         place, count, sizes, scale, positions.reshape(3, atoms), feats, kvec, sigma, w_mix
     )
     low = 256
@@ -511,10 +517,10 @@
         parts = lax.all_to_all(sums[0], "gz", 0, 0, tiled=True)
         mine = jnp.sum(parts.reshape(sizes[2], -1, width), axis=0)
     part = mine.shape[0] // plane
-    mine, keys, wmsg, send, feats = lax.optimization_barrier((mine, keys, wmsg, send_list, feats))
+    mine, keys, wmsg, send, own = lax.optimization_barrier((mine, keys, wmsg, send_list, own))
 
     received = lax.all_to_all(mine.reshape(plane, part, width), ("gx", "gy"), 0, 0, tiled=True)
-    *outgoing, own = selected(count, send.reshape(6, 1, -1), feats)
+    outgoing = selected(send.reshape(6, 1, -1), own)
     halos = [
         passed_along(outgoing[2 * number + side], axis, 1 - 2 * side)
         for number, axis in enumerate(("gx", "gy"))

time: 64.5 us -> 63.2 us (0.980)
  Pallas kernels: 37.3 us -> 35.6 us
    pallas_call x1, Pallas kernels: 12.7 us -> 11.5 us  [phases(): pl.pallas_call(functools.partial(phase_kernel, sizes, scale, paired), gri...]
  transfers between devices with their start and end apart: 9 -> 9, of which waited for: 4 -> 5; matrix products, arithmetic and copies ran while one was open for 0% -> 0% of each run, Pallas kernels for 29% -> 29%
where the time goes in v5:
time: 63.2 us; the launch traced here: 62.8 us
  Pallas kernels  35.6 us (56%)
  starting transfers between devices  20.3 us (32%)
  waiting for transfers between devices  4.56 us (7%)
  between operations  1.51 us (2%)
  other arithmetic  0.92 us (1%)
    pallas_call x1, Pallas kernels, phases(): pl.pallas_call(functools.partial(phase_kernel, sizes, scale, paired), gri...  11.5 us
    pallas_call x1, Pallas kernels, messages(): pl.pallas_call(functools.partial(message_kernel, low, span, slots, early)...  8.79 us
    all_to_all x1, starting transfers between devices, shards(): lax.all_to_all(mine.reshape(plane, part, width), ('gx', 'gy'), 0, 0, tile...  8.24 us
    ppermute x7, starting transfers between devices, passed_along(): return lax.ppermute(value, axis, pairs)  7.39 us
    pallas_call x1, Pallas kernels, back(): pl.pallas_call(functools.partial(back_kernel, scale), in_specs=[pl.BlockS...  5.43 us
    pallas_call x1, Pallas kernels, built(): pl.pallas_call(functools.partial(build_kernel, low, span), grid=(here //...  5.23 us
    all_to_all x1, starting transfers between devices, shards(): lax.all_to_all(shares, ('gx', 'gy'), 0, 0, tiled=True)  4.65 us
    pallas_call x1, Pallas kernels, selected(): pl.pallas_call(select_kernel, in_specs=[pl.BlockSpec((faces, 1, picks), l...  2.7 us
  transfers between devices with their start and end apart: 9, of which 5 were waited for; matrix products, arithmetic and copies ran while one was open for 0% of the time, Pallas kernels for 29%

profile of v5, /device:TPU:0, one launch (start us, length us, event | category | flops | bytes accessed | tf_op | source)
XLA Modules:
  0.0 62.8 jit_solution(15946641057511719673)
XLA Ops:
  1.3 0.1 pad_add_fusion.place_ref
  1.4 11.5 %phases.1 = (bf16[2048,2048]{1,0:T(8,128)(2,1)}, bf16[2048,128]{1,0:T(8,128)(2,1)S(1)}, f32[1024,128]{1,0:T(8,128)S(1)}, f32[1024,128]{1,0:T(8,128)S(1)}) custom-call(s32[3]{0:T(128)S(1)} %pad_add_fusion.place_ref, s32[1]{0:T(128)} %bitcast.15.count_ref, f32[3,1,2048]{2,1,0:T(1,128)} %bitcast.25, bf16[2048,128]{1,0:T(8,128)(2,1)} %bitcast.22, ...), custom_call_target="tpu_custom_call" | custom-call | tf_op jit(solution)/shard_map/phases/pallas_call | solution.py:163
  12.8 0.5 collective-permute-start
  13.3 1.2 %prepared.1 = (f32[256,256]{1,0:T(8,128)S(1)}, f32[256,256]{1,0:T(8,128)S(1)}, f32[256,256]{1,0:T(8,128)S(1)}, bf16[128,128]{1,0:T(8,128)(2,1)S(1)}) custom-call(s32[32,2048]{1,0:T(8,128)} %bitcast.23, bf16[32,2048]{1,0:T(8,128)(2,1)} %bitcast.24, bf16[128,128]{1,0:T(8,128)(2,1)} %wmsg_ref.1), custom_call_target="tpu_custom_call" | custom-call | tf_op jit(solution)/shard_map/prepared/pallas_call | solution.py:276
  14.5 0.3 collective-permute-done
  14.9 0.8 %add.3 = f32[1024,128]{1,0:T(8,128)} add(f32[1024,128]{1,0:T(8,128)S(1)} %get-tuple-element.40, f32[1024,128]{1,0:T(8,128)S(1)} %collective-permute-done) | non-fusion elementwise | flops 131072 | bytes 1572864 | tf_op jit(solution)/shard_map/add | solution.py:515
  15.7 8.2 %all-to-all-start = ((f32[16,64,128]{2,1,0:T(8,128)}), f32[16,64,128]{2,1,0:T(8,128)S(1)}, u32[]{:S(2)}, u32[]{:S(2)}) async-start(f32[16,64,128]{2,1,0:T(8,128)} %bitcast.9), calls=%async_computation | async-start | bytes 1048576 | tf_op jit(solution)/shard_map/all_to_all | solution.py:522
  24.0 2.7 %selected.1 = (bf16[256,128]{1,0:T(8,128)(2,1)S(1)}, bf16[256,128]{1,0:T(8,128)(2,1)S(1)}, bf16[256,128]{1,0:T(8,128)(2,1)S(1)}, bf16[256,128]{1,0:T(8,128)(2,1)S(1)}, bf16[2,256,128]{2,1,0:T(8,128)(2,1)S(1)}) custom-call(s32[6,1,256]{2,1,0:T(1,128)} %bitcast.26, bf16[2048,128]{1,0:T(8,128)(2,1)S(1)} %get-tuple-element.50.own_ref), custom_call_target="tpu_custom_call" | custom-call | tf_op jit(solution)/shard_map/selected/pallas_call | solution.py:223
  26.7 0.1 collective-permute-start.5
  26.8 2.0 %collective-permute-start.1 = (bf16[256,128]{1,0:T(8,128)(2,1)S(1)}, bf16[256,128]{1,0:T(8,128)(2,1)S(1)}, u32[]{:S(2)}, u32[]{:S(2)}) collective-permute-start(bf16[256,128]{1,0:T(8,128)(2,1)S(1)} %get-tuple-element.51), channel_id=1, source_target_pairs={{0,8},{8,16},{16,24},{24,0},{1,9},{9,17},{17,25},{25,1},{2,10},{10... | collective-permute-start | bytes 196616 | tf_op jit(solution)/shard_map/ppermute | solution.py:489
  28.7 1.9 %collective-permute-start.2 = (bf16[256,128]{1,0:T(8,128)(2,1)S(1)}, bf16[256,128]{1,0:T(8,128)(2,1)S(1)}, u32[]{:S(2)}, u32[]{:S(2)}) collective-permute-start(bf16[256,128]{1,0:T(8,128)(2,1)S(1)} %get-tuple-element.52), channel_id=1, source_target_pairs={{0,24},{8,0},{16,8},{24,16},{1,25},{9,1},{17,9},{25,17},{2,26},{10... | collective-permute-start | bytes 196616 | tf_op jit(solution)/shard_map/ppermute | solution.py:489
  30.6 1.9 %collective-permute-start.3 = (bf16[256,128]{1,0:T(8,128)(2,1)S(1)}, bf16[256,128]{1,0:T(8,128)(2,1)S(1)}, u32[]{:S(2)}, u32[]{:S(2)}) collective-permute-start(bf16[256,128]{1,0:T(8,128)(2,1)S(1)} %get-tuple-element.53), channel_id=1, source_target_pairs={{0,2},{2,4},{4,6},{6,0},{1,3},{3,5},{5,7},{7,1},{8,10},{10,12},{12... | collective-permute-start | bytes 196616 | tf_op jit(solution)/shard_map/ppermute | solution.py:489
  32.5 1.0 %collective-permute-start.4 = (bf16[256,128]{1,0:T(8,128)(2,1)S(1)}, bf16[256,128]{1,0:T(8,128)(2,1)S(1)}, u32[]{:S(2)}, u32[]{:S(2)}) collective-permute-start(bf16[256,128]{1,0:T(8,128)(2,1)S(1)} %get-tuple-element.54), channel_id=1, source_target_pairs={{0,6},{2,0},{4,2},{6,4},{1,7},{3,1},{5,3},{7,5},{8,14},{10,8},{12,... | collective-permute-start | bytes 196616 | tf_op jit(solution)/shard_map/ppermute | solution.py:489
  33.6 5.2 %built.1 = (bf16[1024,1536]{1,0:T(8,128)(2,1)}, f32[1024,128]{1,0:T(8,128)S(1)}) custom-call(f32[256,256]{1,0:T(8,128)S(1)} %get-tuple-element.56.high_key, f32[256,256]{1,0:T(8,128)S(1)} %get-tuple-element.57.low_key, f32[256,256]{1,0:T(8,128)S(1)} %get-tuple-element.58.edge, bf16[2048,128]{1,0:T(8,128)(2,1)S(1)} %get-tuple-element.50.own_ref), custom_call_target="tpu_custom_call" | custom-call | tf_op jit(solution)/shard_map/built/pallas_call | solution.py:343
  38.8 0.2 collective-permute-done.1.refs_0_
  39.0 0.0 collective-permute-done.2.refs_1_
  39.0 0.0 collective-permute-done.3.refs_2_
  39.0 0.0 collective-permute-done.4.refs_3_
  39.0 0.0 collective-permute-done.5.refs_4_
  39.0 1.7 %all-to-all-done.parts_ref = f32[16,64,128]{2,1,0:T(8,128)S(1)} async-done(((f32[16,64,128]{2,1,0:T(8,128)}), f32[16,64,128]{2,1,0:T(8,128)S(1)}, u32[]{:S(2)}, u32[]{:S(2)}) %all-to-all-start) | async-done | bytes 524320 | tf_op jit(solution)/shard_map/all_to_all | solution.py:522
  40.8 0.7 %totals.1 = bf16[16,64,128]{2,1,0:T(8,128)(2,1)} custom-call(f32[16,64,128]{2,1,0:T(8,128)S(1)} %all-to-all-done.parts_ref), custom_call_target="tpu_custom_call" | custom-call | tf_op jit(solution)/shard_map/totals/pallas_call | solution.py:247
  41.5 4.6 %all-to-all-start.1 = ((bf16[16,64,128]{2,1,0:T(8,128)(2,1)}), bf16[16,64,128]{2,1,0:T(8,128)(2,1)S(1)}, u32[]{:S(2)}, u32[]{:S(2)}) async-start(bf16[16,64,128]{2,1,0:T(8,128)(2,1)} %totals.1), calls=%async_computation.1 | async-start | bytes 524288 | tf_op jit(solution)/shard_map/all_to_all | solution.py:537
  46.2 8.8 %messages.1 = bf16[8,256,128]{2,1,0:T(8,128)(2,1)} custom-call(s32[1]{0:T(128)} %bitcast.16.count_ref, bf16[1024,1536]{1,0:T(8,128)(2,1)} %get-tuple-element.62.early_hbm, f32[1024,128]{1,0:T(8,128)S(1)} %get-tuple-element.63.partial_ref, f32[256,256]{1,0:T(8,128)S(1)} %get-tuple-element.56.high_key, f32[256,256]{1,0:T(8,128)S(1)} %get-tuple-element.57.low_key, ...), custom_call_target="tpu_custom_call" | custom-call | tf_op jit(solution)/shard_map/messages/pallas_call | solution.py:412
  55.0 0.7 %all-to-all-done.1 = bf16[16,64,128]{2,1,0:T(8,128)(2,1)S(1)} async-done(((bf16[16,64,128]{2,1,0:T(8,128)(2,1)}), bf16[16,64,128]{2,1,0:T(8,128)(2,1)S(1)}, u32[]{:S(2)}, u32[]{:S(2)}) %all-to-all-start.1) | async-done | bytes 262176 | tf_op jit(solution)/shard_map/all_to_all | solution.py:537
  55.7 0.0 collective-permute-start.6
  55.7 1.5 %collective-permute-done.6.refs_0_ = bf16[1024,128]{1,0:T(8,128)(2,1)S(1)} collective-permute-done((bf16[1024,128]{1,0:T(8,128)(2,1)S(1)}, bf16[1024,128]{1,0:T(8,128)(2,1)S(1)}, u32[]{:S(2)}, u32[]{:S(2)}) %collective-permute-start.6) | collective-permute-done | bytes 262176 | tf_op jit(solution)/shard_map/ppermute | solution.py:489
  57.2 5.4 %back.1 = f32[2048,128]{1,0:T(8,128)} custom-call(s32[1]{0:T(128)} %bitcast.17.count_ref, bf16[2048,2048]{1,0:T(8,128)(2,1)} %get-tuple-element.76.table_hbm, bf16[1024,128]{1,0:T(8,128)(2,1)S(1)} %collective-permute-done.6.refs_0_, bf16[1024,128]{1,0:T(8,128)(2,1)S(1)} %bitcast.19), custom_call_target="tpu_custom_call" | custom-call | tf_op jit(solution)/shard_map/back/pallas_call | solution.py:466
Async XLA Ops:
  12.8 2.1 %collective-permute-start = (f32[1024,128]{1,0:T(8,128)S(1)}, f32[1024,128]{1,0:T(8,128)S(1)}, u32[]{:S(2)}, u32[]{:S(2)}) collective-permute-start(f32[1024,128]{1,0:T(8,128)S(1)} %get-tuple-element.41), channel_id=1, source_target_pairs={{0,1},{1,0},{2,3},{3,2},{4,5},{5,4},{6,7},{7,6},{8,9},{9,8},{10,11... | collective-permute-start | bytes 1572872 | tf_op jit(solution)/shard_map/ppermute | solution.py:489
  15.7 25.0 %all-to-all-start = ((f32[16,64,128]{2,1,0:T(8,128)}), f32[16,64,128]{2,1,0:T(8,128)S(1)}, u32[]{:S(2)}, u32[]{:S(2)}) async-start(f32[16,64,128]{2,1,0:T(8,128)} %bitcast.9), calls=%async_computation | async-start | bytes 1048576 | tf_op jit(solution)/shard_map/all_to_all | solution.py:522
  26.7 12.4 %collective-permute-start.5 = (bf16[2,256,128]{2,1,0:T(8,128)(2,1)S(1)}, bf16[2,256,128]{2,1,0:T(8,128)(2,1)S(1)}, u32[]{:S(2)}, u32[]{:S(2)}) collective-permute-start(bf16[2,256,128]{2,1,0:T(8,128)(2,1)S(1)} %get-tuple-element.55), channel_id=1, source_target_pairs={{0,1},{1,0},{2,3},{3,2},{4,5},{5,4},{6,7},{7,6},{8,9},{9,8},{10,11... | collective-permute-start | bytes 393224 | tf_op jit(solution)/shard_map/ppermute | solution.py:489
  26.8 12.3 %collective-permute-start.1 = (bf16[256,128]{1,0:T(8,128)(2,1)S(1)}, bf16[256,128]{1,0:T(8,128)(2,1)S(1)}, u32[]{:S(2)}, u32[]{:S(2)}) collective-permute-start(bf16[256,128]{1,0:T(8,128)(2,1)S(1)} %get-tuple-element.51), channel_id=1, source_target_pairs={{0,8},{8,16},{16,24},{24,0},{1,9},{9,17},{17,25},{25,1},{2,10},{10... | collective-permute-start | bytes 196616 | tf_op jit(solution)/shard_map/ppermute | solution.py:489
  28.7 10.3 %collective-permute-start.2 = (bf16[256,128]{1,0:T(8,128)(2,1)S(1)}, bf16[256,128]{1,0:T(8,128)(2,1)S(1)}, u32[]{:S(2)}, u32[]{:S(2)}) collective-permute-start(bf16[256,128]{1,0:T(8,128)(2,1)S(1)} %get-tuple-element.52), channel_id=1, source_target_pairs={{0,24},{8,0},{16,8},{24,16},{1,25},{9,1},{17,9},{25,17},{2,26},{10... | collective-permute-start | bytes 196616 | tf_op jit(solution)/shard_map/ppermute | solution.py:489
  30.6 8.4 %collective-permute-start.3 = (bf16[256,128]{1,0:T(8,128)(2,1)S(1)}, bf16[256,128]{1,0:T(8,128)(2,1)S(1)}, u32[]{:S(2)}, u32[]{:S(2)}) collective-permute-start(bf16[256,128]{1,0:T(8,128)(2,1)S(1)} %get-tuple-element.53), channel_id=1, source_target_pairs={{0,2},{2,4},{4,6},{6,0},{1,3},{3,5},{5,7},{7,1},{8,10},{10,12},{12... | collective-permute-start | bytes 196616 | tf_op jit(solution)/shard_map/ppermute | solution.py:489
  32.5 6.5 %collective-permute-start.4 = (bf16[256,128]{1,0:T(8,128)(2,1)S(1)}, bf16[256,128]{1,0:T(8,128)(2,1)S(1)}, u32[]{:S(2)}, u32[]{:S(2)}) collective-permute-start(bf16[256,128]{1,0:T(8,128)(2,1)S(1)} %get-tuple-element.54), channel_id=1, source_target_pairs={{0,6},{2,0},{4,2},{6,4},{1,7},{3,1},{5,3},{7,5},{8,14},{10,8},{12,... | collective-permute-start | bytes 196616 | tf_op jit(solution)/shard_map/ppermute | solution.py:489
  41.5 14.2 %all-to-all-start.1 = ((bf16[16,64,128]{2,1,0:T(8,128)(2,1)}), bf16[16,64,128]{2,1,0:T(8,128)(2,1)S(1)}, u32[]{:S(2)}, u32[]{:S(2)}) async-start(bf16[16,64,128]{2,1,0:T(8,128)(2,1)} %totals.1), calls=%async_computation.1 | async-start | bytes 524288 | tf_op jit(solution)/shard_map/all_to_all | solution.py:537
  55.7 1.5 %collective-permute-start.6 = (bf16[1024,128]{1,0:T(8,128)(2,1)S(1)}, bf16[1024,128]{1,0:T(8,128)(2,1)S(1)}, u32[]{:S(2)}, u32[]{:S(2)}) collective-permute-start(bf16[1024,128]{1,0:T(8,128)(2,1)S(1)} %bitcast.18), channel_id=1, source_target_pairs={{0,1},{1,0},{2,3},{3,2},{4,5},{5,4},{6,7},{7,6},{8,9},{9,8},{10,11... | collective-permute-start | bytes 786440 | tf_op jit(solution)/shard_map/ppermute | solution.py:489

commit v6 on v5

--- a/solution.py
+++ b/solution.py
@@ -11,7 +11,7 @@
 
 F32 = jnp.float32
 BF16 = jnp.bfloat16
-VMEM_LIMIT = 18 << 20
+VMEM_LIMIT = 22 << 20
 EARLY = 2
 
 
@@ -404,7 +404,7 @@
     groups = keys[0].shape[0]
     atoms, width = own.shape
     halo_rows = early_adj.shape[1]
-    span = min(64, groups // 4)
+    span = min(128, groups // 2)
     vmem = pl.BlockSpec(memory_space=pltpu.VMEM)
     arrays = [partial, *keys, own, *halos, wmsg]
     steps = groups // span

time: 63.2 us -> 63.2 us (level)
  Pallas kernels: 35.6 us -> 34.8 us
  waiting for transfers between devices: 4.56 us -> 5.32 us
    pallas_call x1, Pallas kernels: 8.79 us -> 8.03 us  [messages(): pl.pallas_call(functools.partial(message_kernel, low, span, slots, early)...]
    all_to_all x1, waiting for transfers between devices: 0.72 us -> 1.49 us  [shards(): lax.all_to_all(shares, ('gx', 'gy'), 0, 0, tiled=True)]
  transfers between devices with their start and end apart: 9 -> 9, of which waited for: 5 -> 5; matrix products, arithmetic and copies ran while one was open for 0% -> 0% of each run, Pallas kernels for 29% -> 27%
where the time goes in v6:
time: 63.2 us; the launch traced here: 62.8 us
  Pallas kernels  34.8 us (55%)
  starting transfers between devices  20.3 us (32%)
  waiting for transfers between devices  5.32 us (8%)
  between operations  1.51 us (2%)
  other arithmetic  0.92 us (1%)
    pallas_call x1, Pallas kernels, phases(): pl.pallas_call(functools.partial(phase_kernel, sizes, scale, paired), gri...  11.5 us
    all_to_all x1, starting transfers between devices, shards(): lax.all_to_all(mine.reshape(plane, part, width), ('gx', 'gy'), 0, 0, tile...  8.24 us
    pallas_call x1, Pallas kernels, messages(): pl.pallas_call(functools.partial(message_kernel, low, span, slots, early)...  8.03 us
    ppermute x7, starting transfers between devices, passed_along(): return lax.ppermute(value, axis, pairs)  7.39 us
    pallas_call x1, Pallas kernels, back(): pl.pallas_call(functools.partial(back_kernel, scale), in_specs=[pl.BlockS...  5.43 us
    pallas_call x1, Pallas kernels, built(): pl.pallas_call(functools.partial(build_kernel, low, span), grid=(here //...  5.23 us
    all_to_all x1, starting transfers between devices, shards(): lax.all_to_all(shares, ('gx', 'gy'), 0, 0, tiled=True)  4.65 us
    pallas_call x1, Pallas kernels, selected(): pl.pallas_call(select_kernel, in_specs=[pl.BlockSpec((faces, 1, picks), l...  2.7 us
  transfers between devices with their start and end apart: 9, of which 5 were waited for; matrix products, arithmetic and copies ran while one was open for 0% of the time, Pallas kernels for 27%

profile of v6, /device:TPU:0, one launch (start us, length us, event | category | flops | bytes accessed | tf_op | source)
XLA Modules:
  0.0 62.8 jit_solution(8143733691928912048)
XLA Ops:
  1.3 0.1 pad_add_fusion.place_ref
  1.4 11.5 %phases.1 = (bf16[2048,2048]{1,0:T(8,128)(2,1)}, bf16[2048,128]{1,0:T(8,128)(2,1)S(1)}, f32[1024,128]{1,0:T(8,128)S(1)}, f32[1024,128]{1,0:T(8,128)S(1)}) custom-call(s32[3]{0:T(128)S(1)} %pad_add_fusion.place_ref, s32[1]{0:T(128)} %bitcast.15.count_ref, f32[3,1,2048]{2,1,0:T(1,128)} %bitcast.25, bf16[2048,128]{1,0:T(8,128)(2,1)} %bitcast.22, ...), custom_call_target="tpu_custom_call" | custom-call | tf_op jit(solution)/shard_map/phases/pallas_call | solution.py:163
  12.8 0.5 collective-permute-start
  13.3 1.2 %prepared.1 = (f32[256,256]{1,0:T(8,128)S(1)}, f32[256,256]{1,0:T(8,128)S(1)}, f32[256,256]{1,0:T(8,128)S(1)}, bf16[128,128]{1,0:T(8,128)(2,1)S(1)}) custom-call(s32[32,2048]{1,0:T(8,128)} %bitcast.23, bf16[32,2048]{1,0:T(8,128)(2,1)} %bitcast.24, bf16[128,128]{1,0:T(8,128)(2,1)} %wmsg_ref.1), custom_call_target="tpu_custom_call" | custom-call | tf_op jit(solution)/shard_map/prepared/pallas_call | solution.py:276
  14.5 0.3 collective-permute-done
  14.9 0.8 %add.3 = f32[1024,128]{1,0:T(8,128)} add(f32[1024,128]{1,0:T(8,128)S(1)} %get-tuple-element.40, f32[1024,128]{1,0:T(8,128)S(1)} %collective-permute-done) | non-fusion elementwise | flops 131072 | bytes 1572864 | tf_op jit(solution)/shard_map/add | solution.py:515
  15.7 8.2 %all-to-all-start = ((f32[16,64,128]{2,1,0:T(8,128)}), f32[16,64,128]{2,1,0:T(8,128)S(1)}, u32[]{:S(2)}, u32[]{:S(2)}) async-start(f32[16,64,128]{2,1,0:T(8,128)} %bitcast.9), calls=%async_computation | async-start | bytes 1048576 | tf_op jit(solution)/shard_map/all_to_all | solution.py:522
  24.0 2.7 %selected.1 = (bf16[256,128]{1,0:T(8,128)(2,1)S(1)}, bf16[256,128]{1,0:T(8,128)(2,1)S(1)}, bf16[256,128]{1,0:T(8,128)(2,1)S(1)}, bf16[256,128]{1,0:T(8,128)(2,1)S(1)}, bf16[2,256,128]{2,1,0:T(8,128)(2,1)S(1)}) custom-call(s32[6,1,256]{2,1,0:T(1,128)} %bitcast.26, bf16[2048,128]{1,0:T(8,128)(2,1)S(1)} %get-tuple-element.50.own_ref), custom_call_target="tpu_custom_call" | custom-call | tf_op jit(solution)/shard_map/selected/pallas_call | solution.py:223
  26.7 0.1 collective-permute-start.5
  26.8 2.0 %collective-permute-start.1 = (bf16[256,128]{1,0:T(8,128)(2,1)S(1)}, bf16[256,128]{1,0:T(8,128)(2,1)S(1)}, u32[]{:S(2)}, u32[]{:S(2)}) collective-permute-start(bf16[256,128]{1,0:T(8,128)(2,1)S(1)} %get-tuple-element.51), channel_id=1, source_target_pairs={{0,8},{8,16},{16,24},{24,0},{1,9},{9,17},{17,25},{25,1},{2,10},{10... | collective-permute-start | bytes 196616 | tf_op jit(solution)/shard_map/ppermute | solution.py:489
  28.7 1.9 %collective-permute-start.2 = (bf16[256,128]{1,0:T(8,128)(2,1)S(1)}, bf16[256,128]{1,0:T(8,128)(2,1)S(1)}, u32[]{:S(2)}, u32[]{:S(2)}) collective-permute-start(bf16[256,128]{1,0:T(8,128)(2,1)S(1)} %get-tuple-element.52), channel_id=1, source_target_pairs={{0,24},{8,0},{16,8},{24,16},{1,25},{9,1},{17,9},{25,17},{2,26},{10... | collective-permute-start | bytes 196616 | tf_op jit(solution)/shard_map/ppermute | solution.py:489
  30.6 1.9 %collective-permute-start.3 = (bf16[256,128]{1,0:T(8,128)(2,1)S(1)}, bf16[256,128]{1,0:T(8,128)(2,1)S(1)}, u32[]{:S(2)}, u32[]{:S(2)}) collective-permute-start(bf16[256,128]{1,0:T(8,128)(2,1)S(1)} %get-tuple-element.53), channel_id=1, source_target_pairs={{0,2},{2,4},{4,6},{6,0},{1,3},{3,5},{5,7},{7,1},{8,10},{10,12},{12... | collective-permute-start | bytes 196616 | tf_op jit(solution)/shard_map/ppermute | solution.py:489
  32.5 1.0 %collective-permute-start.4 = (bf16[256,128]{1,0:T(8,128)(2,1)S(1)}, bf16[256,128]{1,0:T(8,128)(2,1)S(1)}, u32[]{:S(2)}, u32[]{:S(2)}) collective-permute-start(bf16[256,128]{1,0:T(8,128)(2,1)S(1)} %get-tuple-element.54), channel_id=1, source_target_pairs={{0,6},{2,0},{4,2},{6,4},{1,7},{3,1},{5,3},{7,5},{8,14},{10,8},{12,... | collective-permute-start | bytes 196616 | tf_op jit(solution)/shard_map/ppermute | solution.py:489
  33.6 5.2 %built.1 = (bf16[1024,1536]{1,0:T(8,128)(2,1)}, f32[1024,128]{1,0:T(8,128)S(1)}) custom-call(f32[256,256]{1,0:T(8,128)S(1)} %get-tuple-element.56.high_key, f32[256,256]{1,0:T(8,128)S(1)} %get-tuple-element.57.low_key, f32[256,256]{1,0:T(8,128)S(1)} %get-tuple-element.58.edge, bf16[2048,128]{1,0:T(8,128)(2,1)S(1)} %get-tuple-element.50.own_ref), custom_call_target="tpu_custom_call" | custom-call | tf_op jit(solution)/shard_map/built/pallas_call | solution.py:343
  38.8 0.2 collective-permute-done.1.refs_0_
  39.0 0.0 collective-permute-done.2.refs_1_
  39.0 0.0 collective-permute-done.3.refs_2_
  39.0 0.0 collective-permute-done.4.refs_3_
  39.0 0.0 collective-permute-done.5.refs_4_
  39.0 1.7 %all-to-all-done.parts_ref = f32[16,64,128]{2,1,0:T(8,128)S(1)} async-done(((f32[16,64,128]{2,1,0:T(8,128)}), f32[16,64,128]{2,1,0:T(8,128)S(1)}, u32[]{:S(2)}, u32[]{:S(2)}) %all-to-all-start) | async-done | bytes 524320 | tf_op jit(solution)/shard_map/all_to_all | solution.py:522
  40.8 0.7 %totals.1 = bf16[16,64,128]{2,1,0:T(8,128)(2,1)} custom-call(f32[16,64,128]{2,1,0:T(8,128)S(1)} %all-to-all-done.parts_ref), custom_call_target="tpu_custom_call" | custom-call | tf_op jit(solution)/shard_map/totals/pallas_call | solution.py:247
  41.5 4.6 %all-to-all-start.1 = ((bf16[16,64,128]{2,1,0:T(8,128)(2,1)}), bf16[16,64,128]{2,1,0:T(8,128)(2,1)S(1)}, u32[]{:S(2)}, u32[]{:S(2)}) async-start(bf16[16,64,128]{2,1,0:T(8,128)(2,1)} %totals.1), calls=%async_computation.1 | async-start | bytes 524288 | tf_op jit(solution)/shard_map/all_to_all | solution.py:537
  46.2 8.0 %messages.1 = bf16[8,256,128]{2,1,0:T(8,128)(2,1)} custom-call(s32[1]{0:T(128)} %bitcast.16.count_ref, bf16[1024,1536]{1,0:T(8,128)(2,1)} %get-tuple-element.62.early_hbm, f32[1024,128]{1,0:T(8,128)S(1)} %get-tuple-element.63.partial_ref, f32[256,256]{1,0:T(8,128)S(1)} %get-tuple-element.56.high_key, f32[256,256]{1,0:T(8,128)S(1)} %get-tuple-element.57.low_key, ...), custom_call_target="tpu_custom_call" | custom-call | tf_op jit(solution)/shard_map/messages/pallas_call | solution.py:412
  54.2 1.5 %all-to-all-done.1 = bf16[16,64,128]{2,1,0:T(8,128)(2,1)S(1)} async-done(((bf16[16,64,128]{2,1,0:T(8,128)(2,1)}), bf16[16,64,128]{2,1,0:T(8,128)(2,1)S(1)}, u32[]{:S(2)}, u32[]{:S(2)}) %all-to-all-start.1) | async-done | bytes 262176 | tf_op jit(solution)/shard_map/all_to_all | solution.py:537
  55.7 0.0 collective-permute-start.6
  55.7 1.5 %collective-permute-done.6.refs_0_ = bf16[1024,128]{1,0:T(8,128)(2,1)S(1)} collective-permute-done((bf16[1024,128]{1,0:T(8,128)(2,1)S(1)}, bf16[1024,128]{1,0:T(8,128)(2,1)S(1)}, u32[]{:S(2)}, u32[]{:S(2)}) %collective-permute-start.6) | collective-permute-done | bytes 262176 | tf_op jit(solution)/shard_map/ppermute | solution.py:489
  57.2 5.4 %back.1 = f32[2048,128]{1,0:T(8,128)} custom-call(s32[1]{0:T(128)} %bitcast.17.count_ref, bf16[2048,2048]{1,0:T(8,128)(2,1)} %get-tuple-element.76.table_hbm, bf16[1024,128]{1,0:T(8,128)(2,1)S(1)} %collective-permute-done.6.refs_0_, bf16[1024,128]{1,0:T(8,128)(2,1)S(1)} %bitcast.19), custom_call_target="tpu_custom_call" | custom-call | tf_op jit(solution)/shard_map/back/pallas_call | solution.py:466
Async XLA Ops:
  12.8 2.1 %collective-permute-start = (f32[1024,128]{1,0:T(8,128)S(1)}, f32[1024,128]{1,0:T(8,128)S(1)}, u32[]{:S(2)}, u32[]{:S(2)}) collective-permute-start(f32[1024,128]{1,0:T(8,128)S(1)} %get-tuple-element.41), channel_id=1, source_target_pairs={{0,1},{1,0},{2,3},{3,2},{4,5},{5,4},{6,7},{7,6},{8,9},{9,8},{10,11... | collective-permute-start | bytes 1572872 | tf_op jit(solution)/shard_map/ppermute | solution.py:489
  15.7 25.0 %all-to-all-start = ((f32[16,64,128]{2,1,0:T(8,128)}), f32[16,64,128]{2,1,0:T(8,128)S(1)}, u32[]{:S(2)}, u32[]{:S(2)}) async-start(f32[16,64,128]{2,1,0:T(8,128)} %bitcast.9), calls=%async_computation | async-start | bytes 1048576 | tf_op jit(solution)/shard_map/all_to_all | solution.py:522
  26.7 12.4 %collective-permute-start.5 = (bf16[2,256,128]{2,1,0:T(8,128)(2,1)S(1)}, bf16[2,256,128]{2,1,0:T(8,128)(2,1)S(1)}, u32[]{:S(2)}, u32[]{:S(2)}) collective-permute-start(bf16[2,256,128]{2,1,0:T(8,128)(2,1)S(1)} %get-tuple-element.55), channel_id=1, source_target_pairs={{0,1},{1,0},{2,3},{3,2},{4,5},{5,4},{6,7},{7,6},{8,9},{9,8},{10,11... | collective-permute-start | bytes 393224 | tf_op jit(solution)/shard_map/ppermute | solution.py:489
  26.8 12.3 %collective-permute-start.1 = (bf16[256,128]{1,0:T(8,128)(2,1)S(1)}, bf16[256,128]{1,0:T(8,128)(2,1)S(1)}, u32[]{:S(2)}, u32[]{:S(2)}) collective-permute-start(bf16[256,128]{1,0:T(8,128)(2,1)S(1)} %get-tuple-element.51), channel_id=1, source_target_pairs={{0,8},{8,16},{16,24},{24,0},{1,9},{9,17},{17,25},{25,1},{2,10},{10... | collective-permute-start | bytes 196616 | tf_op jit(solution)/shard_map/ppermute | solution.py:489
  28.7 10.3 %collective-permute-start.2 = (bf16[256,128]{1,0:T(8,128)(2,1)S(1)}, bf16[256,128]{1,0:T(8,128)(2,1)S(1)}, u32[]{:S(2)}, u32[]{:S(2)}) collective-permute-start(bf16[256,128]{1,0:T(8,128)(2,1)S(1)} %get-tuple-element.52), channel_id=1, source_target_pairs={{0,24},{8,0},{16,8},{24,16},{1,25},{9,1},{17,9},{25,17},{2,26},{10... | collective-permute-start | bytes 196616 | tf_op jit(solution)/shard_map/ppermute | solution.py:489
  30.6 8.4 %collective-permute-start.3 = (bf16[256,128]{1,0:T(8,128)(2,1)S(1)}, bf16[256,128]{1,0:T(8,128)(2,1)S(1)}, u32[]{:S(2)}, u32[]{:S(2)}) collective-permute-start(bf16[256,128]{1,0:T(8,128)(2,1)S(1)} %get-tuple-element.53), channel_id=1, source_target_pairs={{0,2},{2,4},{4,6},{6,0},{1,3},{3,5},{5,7},{7,1},{8,10},{10,12},{12... | collective-permute-start | bytes 196616 | tf_op jit(solution)/shard_map/ppermute | solution.py:489
  32.5 6.5 %collective-permute-start.4 = (bf16[256,128]{1,0:T(8,128)(2,1)S(1)}, bf16[256,128]{1,0:T(8,128)(2,1)S(1)}, u32[]{:S(2)}, u32[]{:S(2)}) collective-permute-start(bf16[256,128]{1,0:T(8,128)(2,1)S(1)} %get-tuple-element.54), channel_id=1, source_target_pairs={{0,6},{2,0},{4,2},{6,4},{1,7},{3,1},{5,3},{7,5},{8,14},{10,8},{12,... | collective-permute-start | bytes 196616 | tf_op jit(solution)/shard_map/ppermute | solution.py:489
  41.5 14.2 %all-to-all-start.1 = ((bf16[16,64,128]{2,1,0:T(8,128)(2,1)}), bf16[16,64,128]{2,1,0:T(8,128)(2,1)S(1)}, u32[]{:S(2)}, u32[]{:S(2)}) async-start(bf16[16,64,128]{2,1,0:T(8,128)(2,1)} %totals.1), calls=%async_computation.1 | async-start | bytes 524288 | tf_op jit(solution)/shard_map/all_to_all | solution.py:537
  55.7 1.5 %collective-permute-start.6 = (bf16[1024,128]{1,0:T(8,128)(2,1)S(1)}, bf16[1024,128]{1,0:T(8,128)(2,1)S(1)}, u32[]{:S(2)}, u32[]{:S(2)}) collective-permute-start(bf16[1024,128]{1,0:T(8,128)(2,1)S(1)} %bitcast.18), channel_id=1, source_target_pairs={{0,1},{1,0},{2,3},{3,2},{4,5},{5,4},{6,7},{7,6},{8,9},{9,8},{10,11... | collective-permute-start | bytes 786440 | tf_op jit(solution)/shard_map/ppermute | solution.py:489
